TPU v7x, 256 devices: a whole 4x4x8 slice. The times are simulated.
256 devices in a mesh: grp: 4 (over y), tok: 64 (over x, z, core).
Axes of the slice: x: 4, y: 4, z: 8, core: 2. Of those that a mesh axis runs over, the one named last changes fastest.
Arguments:
- hidden_in: bfloat16 [4, 16384, 2048], P('grp', 'tok'), may hold values from -6 to 6
- doc_ids: int32 [4, 16384], P('grp', 'tok'), may hold values from 0 to 63, never falling along the last dimension, each value on 1 to 512 neighbouring positions
- prefix_kv: bfloat16 [4, 2048, 1024], P('grp', 'tok'), may hold values from -1024 to 1024
- prefix_owner: int32 [4], replicated, may hold values from 0 to 3, each once
- norm_gain: bfloat16 [2048], replicated, may hold values from 0.5 to 2
- query_gain: bfloat16 [128], replicated, may hold values from 0.59765625 to 2.390625
- key_norm_gain: bfloat16 [128], replicated, may hold values from 0.59765625 to 2.390625
- w_qkv: bfloat16 [2048, 2048], P('tok'), may hold values from -0.125 to 0.125
- w_out: bfloat16 [1024, 2048], P('tok'), may hold values from -0.1875 to 0.1875
Outputs:
- attn_out: bfloat16 [4, 16384, 2048], P('grp', 'tok')
- key_cache: bfloat16 [4, 16384, 512], P('grp', 'tok')
- value_cache: bfloat16 [4, 16384, 512], P('grp', 'tok')
Inputs may be any that keep to these rules, and one draw needn't show every extreme that they name: `doc_ids`: in each group the ids never fall; every one of the 64 requests has 1 to 512 tokens, and one has exactly 512. `prefix_owner`: A permutation of the groups.
All inputs are finite; a program needn't handle non-finite values.
Results may differ from a plain program's by a relative error of at most 0.013.
The roundings to bfloat16 on the way count: a program that leaves them out, or rounds other values in their place, can miss the bound.
Values may be sent and summed in bfloat16 or wider, within the bound.
No kernel may reach another device: no remote copies, remote signals or barrier semaphores. Data moves between devices by JAX's collectives and lax.ppermute only.
A program may use at most 128 MiB of HBM per device.

v0:
```python
import functools
import math

import jax
import jax.numpy as jnp
from jax import lax
from jax.experimental import pallas as pl
from jax.experimental.pallas import tpu as pltpu
from jax.sharding import PartitionSpec as P

NX, NZ, NC, NY = 4, 8, 2, 4

epsilon = 1e-06
theta_base = 1000000.0
floor_score = -1e30
VMEM_LIMIT = 56 * 1024 * 1024


def place(x, z, c):
    return (x * NZ + z) * NC + c


def from_tok(block, dx=0, dz=0, dc=0):
    route = [
        (place((x + dx) % NX, (z + dz) % NZ, (c + dc) % NC), place(x, z, c))
        for x in range(NX)
        for z in range(NZ)
        for c in range(NC)
    ]
    return lax.ppermute(block, "tok", route)


def from_grp(block, dy):
    return lax.ppermute(block, "grp", [((y + dy) % NY, y) for y in range(NY)])


def from_previous_chip(block):
    chips = NX * NZ
    route = [(p * NC + c, (p + 1) * NC + c) for p in range(chips - 1) for c in range(NC)]
    return lax.ppermute(block, "tok", route)


def in_core_order(core, mine, other, axis):
    first = jnp.where(core == 0, mine, other)
    second = jnp.where(core == 0, other, mine)
    return jnp.concatenate([first, second], axis=axis)


def norm_kernel(x_ref, own_ref, peer_ref, gain_ref, np_ref, nq_ref, scratch):
    half = own_ref.shape[0]
    gain = gain_ref[...].astype(jnp.float32)
    x = x_ref[0]
    for part, ref in enumerate((own_ref, peer_ref)):
        tokens = ref[...].astype(jnp.float32)
        mean = jnp.mean(tokens * tokens, axis=-1, keepdims=True)
        scratch[...] = (tokens * lax.rsqrt(mean + epsilon) * gain).astype(jnp.bfloat16)
        for j in range(NX):
            at = pl.multiple_of(((x + j) % NX) * 512, 512)
            np_ref[pl.ds(part * half, half), j * 256 : (j + 1) * 256] = scratch[:, pl.ds(at, 256)]
            at = pl.multiple_of(((x + j) % NX) * 512 + 256, 256)
            nq_ref[pl.ds(part * half, half), j * 256 : (j + 1) * 256] = scratch[:, pl.ds(at, 256)]


def input_norm(x, own, peer, gain):
    rows, width = own.shape
    out = jax.ShapeDtypeStruct((2 * rows, width // 2), jnp.bfloat16)
    vmem = pl.BlockSpec(memory_space=pltpu.VMEM)
    return pl.pallas_call(
        norm_kernel,
        out_shape=(out, out),
        in_specs=[pl.BlockSpec(memory_space=pltpu.SMEM), vmem, vmem, vmem],
        out_specs=(vmem, vmem),
        scratch_shapes=[pltpu.VMEM((rows, width), jnp.bfloat16)],
        compiler_params=pltpu.CompilerParams(vmem_limit_bytes=VMEM_LIMIT),
        name="input_norm",
    )(x, own, peer, gain)


def qkv_kernel(
    y_ref, np_ref, nq_ref, p0, p1, p2, p3, q0, q1, q2, q3, cos_ref, sin_ref, qg_ref, kg_ref,
    q_out, kv_out, acc
):
    step = pl.program_id(0)
    block = (y_ref[0] + step) % NY

    def dot(a, b):
        return jnp.dot(a, b, preferred_element_type=jnp.float32)

    for k, p in enumerate((p0, p1, p2, p3)):

        @pl.when(step == k)
        def _(p=p, k=k):
            total = dot(np_ref[...], p[...])
            for j, q in enumerate((q0, q1, q2, q3)):
                total = total + dot(
                    nq_ref[:, j * 256 : (j + 1) * 256], q[k * 256 : (k + 1) * 256, :]
                )
            acc[...] = total

    def turned(gain_ref, out):
        gain = gain_ref[...].astype(jnp.float32)
        for h in range(2):
            a = acc[:, h * 128 : (h + 1) * 128]
            mean = jnp.mean(a * a, axis=-1, keepdims=True)
            a = a * lax.rsqrt(mean + epsilon) * gain
            a = a * cos_ref[...] + pltpu.roll(a, 64, 1) * sin_ref[...]
            out[0, :, h * 128 : (h + 1) * 128] = a.astype(jnp.bfloat16)

    @pl.when(block < 2)
    def _():
        turned(qg_ref, q_out)

    @pl.when(block == 2)
    def _():
        turned(kg_ref, kv_out)

    @pl.when(block == 3)
    def _():
        kv_out[0] = acc[...].astype(jnp.bfloat16)


def query_block(i, y_ref):
    block = (y_ref[0] + i) % NY
    return jnp.where(block < 2, block, jnp.where(i >= block - 1, 1, 0)), 0, 0


def key_value_block(i, y_ref):
    block = (y_ref[0] + i) % NY
    return jnp.where(block >= 2, block - 2, jnp.where(i >= block + 1, 1, 0)), 0, 0


def joint_projection(y, normed_p, normed_q, p, q, cosine, sine, query_gain, key_gain):
    rows = normed_p.shape[0]
    whole = lambda a: pl.BlockSpec(a.shape, lambda i, y_ref: (0,) * a.ndim)
    args = [normed_p, normed_q, *p, *q, cosine, sine, query_gain, key_gain]
    out = jax.ShapeDtypeStruct((2, rows, 256), jnp.bfloat16)
    return pl.pallas_call(
        qkv_kernel,
        out_shape=(out, out),
        grid_spec=pltpu.PrefetchScalarGridSpec(
            num_scalar_prefetch=1,
            grid=(NY,),
            in_specs=[whole(a) for a in args],
            out_specs=(
                pl.BlockSpec((1, rows, 256), query_block),
                pl.BlockSpec((1, rows, 256), key_value_block),
            ),
            scratch_shapes=[pltpu.VMEM((rows, 256), jnp.float32)],
        ),
        compiler_params=pltpu.CompilerParams(
            dimension_semantics=("arbitrary",), vmem_limit_bytes=VMEM_LIMIT
        ),
        cost_estimate=pl.CostEstimate(
            flops=2 * rows * 2048 * 1024, transcendentals=0, bytes_accessed=8 << 20
        ),
        name="joint_projection",
    )(y, *args)


LANES = (((1,), (1,)), ((), ()))


def fold(op, blocks):
    return functools.reduce(
        op, [b[:, i : i + 128] for b in blocks for i in range(0, b.shape[1], 128)]
    )


def row_max(blocks):
    return jnp.max(fold(jnp.maximum, blocks), axis=-1, keepdims=True)


def prefix_kernel(scale, core_ref, q_ref, k_ref, v_ref, acc_ref, top_ref, total_ref):
    rows = q_ref.shape[1]
    step = 512
    starts = range(0, k_ref.shape[0], step)
    q = jnp.concatenate([q_ref[0, :, :128], q_ref[0, :, 128:]], axis=0)
    scores = [
        lax.dot_general(q, k_ref[i : i + step, :], LANES, preferred_element_type=jnp.float32)
        for i in starts
    ]
    top = row_max(scores)
    total = jnp.zeros(q.shape, jnp.float32)
    acc = jnp.zeros(q.shape, jnp.float32)
    for s, i in zip(scores, starts):
        w = jnp.exp2((s - top) * scale)
        total = total + fold(jnp.add, [w])
        acc = acc + jnp.dot(
            w.astype(jnp.bfloat16), v_ref[i : i + step, :], preferred_element_type=jnp.float32
        )
    total = jnp.sum(total, axis=-1, keepdims=True)
    for h in range(2):
        at = slice(h * rows, (h + 1) * rows)
        acc_ref[h], top_ref[h], total_ref[h] = acc[at], top[at], total[at]


def prefix_attention(core, qkv, prefix, scale):
    rows = qkv.shape[1]
    keys = prefix.shape[0]
    stat = jax.ShapeDtypeStruct((4, rows, 1), jnp.float32)
    pair = lambda width: pl.BlockSpec((2, rows, width), lambda g, c: (g, 0, 0))
    return pl.pallas_call(
        functools.partial(prefix_kernel, scale),
        out_shape=(jax.ShapeDtypeStruct((4, rows, 128), jnp.float32), stat, stat),
        grid_spec=pltpu.PrefetchScalarGridSpec(
            num_scalar_prefetch=1,
            grid=(2,),
            in_specs=[
                pl.BlockSpec((1, rows, 256), lambda g, c: (g, 0, 0)),
                pl.BlockSpec((keys, 128), lambda g, c: (0, 2 * c[0] + g)),
                pl.BlockSpec((keys, 128), lambda g, c: (0, 4 + 2 * c[0] + g)),
            ],
            out_specs=(pair(128), pair(1), pair(1)),
        ),
        compiler_params=pltpu.CompilerParams(
            dimension_semantics=("arbitrary",), vmem_limit_bytes=VMEM_LIMIT
        ),
        cost_estimate=pl.CostEstimate(
            flops=4 * 4 * rows * keys * 128, transcendentals=4 * rows * keys, bytes_accessed=4 << 20
        ),
        name="prefix_attention",
    )(core, qkv, prefix, prefix)


def suffix_kernel(
    scale, q_ref, ko_ref, vo_ref, kh_ref, vh_ref, acc_ref, top_ref, total_ref,
    bias, own_ref, peer_ref
):
    rows, chip = q_ref.shape[1], ko_ref.shape[1]

    for h in range(2):
        at = slice(h * 128, (h + 1) * 128)
        q = q_ref[0, :, at]
        scores = [
            lax.dot_general(q, k[0], LANES, preferred_element_type=jnp.float32)
            + bias[:, i * chip : (i + 1) * chip]
            for i, k in enumerate((kh_ref, ko_ref))
        ]
        before = top_ref[h]
        top = jnp.maximum(before, row_max(scores))
        shrink = jnp.exp2((before - top) * scale)
        total = jnp.zeros((rows, 128), jnp.float32)
        acc = acc_ref[h] * shrink
        for s, v in zip(scores, (vh_ref, vo_ref)):
            w = jnp.exp2((s - top) * scale)
            total = total + fold(jnp.add, [w])
            acc = acc + jnp.dot(w.astype(jnp.bfloat16), v[0], preferred_element_type=jnp.float32)
        total = total_ref[h] * shrink + jnp.sum(total, axis=-1, keepdims=True)
        out = (acc / total).astype(jnp.bfloat16)
        own_ref[:, at] = out[: rows // 2]
        peer_ref[:, at] = out[rows // 2 :]


def suffix_attention(queries, own, halo, partial, bias, scale):
    rows = queries.shape[1]
    pair = lambda width: pl.BlockSpec((2, rows, width), lambda g: (g, 0, 0))
    head = lambda block: pl.BlockSpec((1, rows, 128), lambda g: (block, 0, g))
    out = jax.ShapeDtypeStruct((rows // 2, 512), jnp.bfloat16)
    out_spec = pl.BlockSpec((rows // 2, 256), lambda g: (0, g))
    return pl.pallas_call(
        functools.partial(suffix_kernel, scale),
        out_shape=(out, out),
        grid=(2,),
        in_specs=[
            pl.BlockSpec((1, rows, 256), lambda g: (g, 0, 0)),
            head(0),
            head(1),
            head(0),
            head(1),
            pair(128),
            pair(1),
            pair(1),
            pl.BlockSpec(bias.shape, lambda g: (0, 0)),
        ],
        out_specs=(out_spec, out_spec),
        compiler_params=pltpu.CompilerParams(
            dimension_semantics=("arbitrary",), vmem_limit_bytes=VMEM_LIMIT
        ),
        cost_estimate=pl.CostEstimate(
            flops=4 * 4 * rows * 1024 * 128, transcendentals=4 * rows * 1024, bytes_accessed=4 << 20
        ),
        name="suffix_attention",
    )(queries, own, own, halo, halo, *partial, bias)


def out_kernel(place_ref, mine_ref, other_ref, *refs):
    *weights, out_ref, heads = refs
    x, core = place_ref[0], place_ref[1]
    heads[:, pl.ds(pl.multiple_of(core * 512, 512), 512)] = mine_ref[...]
    heads[:, pl.ds(pl.multiple_of((1 - core) * 512, 512), 512)] = other_ref[...]
    for c, strips in ((core, weights[:NX]), (1 - core, weights[NX:])):
        total = jnp.zeros((mine_ref.shape[0], 1024), jnp.float32)
        for j, strip in enumerate(strips):
            at = pl.multiple_of(((x + j) % NX) * 256, 256)
            total = total + jnp.dot(
                heads[:, pl.ds(at, 256)], strip[...], preferred_element_type=jnp.float32
            )
        out_ref[:, pl.ds(pl.multiple_of(c * 1024, 1024), 1024)] = total.astype(jnp.bfloat16)


def output_projection(x, core, mine, other, strips, strips_other):
    rows = mine.shape[0]
    vmem = pl.BlockSpec(memory_space=pltpu.VMEM)
    args = [mine, other, *strips, *strips_other]
    return pl.pallas_call(
        out_kernel,
        out_shape=jax.ShapeDtypeStruct((rows, 2048), jnp.bfloat16),
        in_specs=[pl.BlockSpec(memory_space=pltpu.SMEM)] + [vmem] * len(args),
        out_specs=vmem,
        scratch_shapes=[pltpu.VMEM((rows, 1024), jnp.bfloat16)],
        compiler_params=pltpu.CompilerParams(vmem_limit_bytes=VMEM_LIMIT),
        cost_estimate=pl.CostEstimate(
            flops=2 * rows * 1024 * 2048, transcendentals=0, bytes_accessed=6 << 20
        ),
        name="output_projection",
    )(jnp.stack([x, core]), *args)


def pack_kernel(p0, p1, p2, p3, q0, q1, q2, q3, p_ref, q_ref, prefix_ref):
    for k, (p, q) in enumerate(((p0, q0), (p1, q1), (p2, q2), (p3, q3))):
        p_ref[k * 256 : (k + 1) * 256, :] = p[:256, :]
        q_ref[k * 256 : (k + 1) * 256, :] = q[...]
        for i in range(4):
            prefix_ref[k * 32 : (k + 1) * 32, i * 256 : (i + 1) * 256] = p[
                256 + 32 * i : 288 + 32 * i, :
            ]


def pack(p_all, q_all):
    vmem = pl.BlockSpec(memory_space=pltpu.VMEM)
    strip = jax.ShapeDtypeStruct((1024, 256), jnp.bfloat16)
    return pl.pallas_call(
        pack_kernel,
        out_shape=(strip, strip, jax.ShapeDtypeStruct((128, 1024), jnp.bfloat16)),
        in_specs=[vmem] * 8,
        out_specs=(vmem, vmem, vmem),
        compiler_params=pltpu.CompilerParams(vmem_limit_bytes=VMEM_LIMIT),
        name="pack",
    )(*p_all, *q_all)


GROUP_ZC = [[place(x, z, c) for z in range(NZ) for c in range(NC)] for x in range(NX)]


def per_device(
    hidden_in, doc_ids, prefix_kv, prefix_owner, norm_gain, query_gain, key_norm_gain, w_qkv, w_out
):
    rows = hidden_in.shape[1]
    head_dim = query_gain.shape[0]
    prefix_len = prefix_kv.shape[1] * lax.axis_size("tok")
    scale = head_dim ** (-0.5) * math.log2(math.e)
    place_tok = lax.axis_index("tok")
    y = lax.axis_index("grp")
    x, z, core = place_tok // (NZ * NC), (place_tok // NC) % NZ, place_tok % NC

    own = hidden_in[0]
    out_strip = lax.all_gather(w_out, "tok", axis_index_groups=GROUP_ZC, tiled=True)
    owners = [prefix_kv[0]] + [from_grp(prefix_kv[0], d) for d in range(1, NY)]
    owner = (prefix_owner[y] - y) % NY

    def columns(c):
        start = jnp.where(y < 2, 512 * c + 256 * y, 512 * y + 256 * c)
        return lax.dynamic_slice(w_qkv, (jnp.int32(0), start), (w_qkv.shape[0], 256))

    marks = (doc_ids + 1).astype(jnp.bfloat16)
    first = jnp.concatenate(
        [
            jnp.concatenate([columns(0), columns(1)], axis=1),
            jnp.pad(marks, ((0, 7), (0, 256))),
        ],
        axis=0,
    )
    both = lax.all_gather(first, "tok", axis_index_groups=GROUP_ZC)
    peer = from_tok(own, dc=1)
    both, owners, peer, norm_gain, query_gain, key_norm_gain = lax.optimization_barrier(
        (both, owners, peer, norm_gain, query_gain, key_norm_gain)
    )

    marks_x = both[:, 32, :256]
    strip = lax.dynamic_slice_in_dim(both[:, :32], core * 256, 256, 2).reshape(512, 256)
    prefix_rows = lax.dynamic_index_in_dim(jnp.stack(owners), owner, 0, keepdims=False)
    p_own = jnp.concatenate(
        [strip[:256]]
        + [prefix_rows[:, i * 256 : (i + 1) * 256] for i in range(4)]
        + [jnp.pad(marks_x[14:], ((0, 6), (0, 0)))]
    )
    q_own = strip[256:]
    p_all = [p_own] + [from_tok(p_own, dx=d) for d in (2, 1, 3)]
    p_all = [p_all[0], p_all[2], p_all[1], p_all[3]]
    q_all = [q_own] + [from_grp(q_own, d) for d in range(1, NY)]
    p_all, q_all = lax.optimization_barrier((p_all, q_all))

    p0, q0, prefix_part = pack(p_all, q_all)
    p2 = from_grp(p0, 2)
    p1, p3 = from_grp(p0, 1), from_grp(p0, 3)
    q1, q3 = from_tok(q0, dx=1), from_tok(q0, dx=3)
    q2 = from_tok(q0, dx=2)
    prefix = lax.all_gather(prefix_part, "tok", axis_index_groups=GROUP_ZC, tiled=True)

    normed_p, normed_q = input_norm(x[None], own, peer, norm_gain[None, :])
    marks_left = jnp.where(x > 0, p_all[3][384:386], 0)
    near = lax.dynamic_slice_in_dim(
        jnp.concatenate([marks_left, marks_x]).astype(jnp.float32), 2 * z, 4, 0
    )
    near = near.reshape(2, 2, rows)
    near = jnp.where(core == 0, near, near[:, ::-1])
    marks_k = near.reshape(1, 4 * rows)
    marks_q = near[1].reshape(2 * rows, 1)
    index = jnp.arange(rows, dtype=jnp.int32)
    index_chip = jnp.concatenate([index + core * rows, index + (1 - core) * rows])
    index_k = jnp.concatenate([jnp.full((2 * rows,), -1, jnp.int32), index_chip])[None, :]
    index_q = index_chip[:, None]
    earlier = (marks_q == marks_k) & (index_k < index_q)
    allowed = (marks_q == marks_k) & (index_k <= index_q)
    bias = jnp.where(allowed, jnp.float32(0), jnp.float32(floor_score))
    offset = jnp.sum(earlier.astype(jnp.int32), axis=1)
    token_positions = (prefix_len + offset).astype(jnp.float32)
    half_width = head_dim // 2
    freqs = theta_base ** (-jnp.arange(half_width, dtype=jnp.float32) / half_width)
    angles = token_positions[:, None] * freqs[None, :]
    cosine, sine = jnp.cos(angles), jnp.sin(angles)
    cosine = jnp.concatenate([cosine, cosine], axis=1)
    sine = jnp.concatenate([-sine, sine], axis=1)
    gains = (query_gain[None, :], key_norm_gain[None, :])

    under = (normed_p, normed_q, cosine, sine, bias, gains)
    pieces = ([p0, p1, p2, p3], [q0, q1, q2, q3])

    out_mine = lax.dynamic_slice_in_dim(out_strip, core * 1024, 1024, 1)
    out_mine, pieces, under = lax.optimization_barrier((out_mine, pieces, under))
    normed_p, normed_q, cosine, sine, bias, gains = under
    strips = [out_mine] + [from_tok(out_mine, dx=d) for d in range(1, NX)]
    queries, kv = joint_projection(y[None], normed_p, normed_q, *pieces, cosine, sine, *gains)
    halo = from_previous_chip(kv)

    partial = prefix_attention(core[None], queries, prefix, scale)
    strips, partial, kv_sent = lax.optimization_barrier((strips, partial, kv))
    strips_other = [from_tok(s, dc=1) for s in strips]
    kv_got = from_tok(kv_sent, dc=1)[:, rows:]
    mine, others = suffix_attention(queries, kv, halo, partial, bias, scale)
    got = from_tok(others, dc=1)
    projected = output_projection(x, core, mine, got, strips, strips_other)
    cache = in_core_order(core, kv[:, :rows], kv_got, 2)
    return (projected[None], cache[0][None], cache[1][None])


def solution(mesh):
    return jax.shard_map(
        per_device,
        mesh=mesh,
        in_specs=(
            P("grp", "tok", None),
            P("grp", "tok"),
            P("grp", "tok", None),
            P(),
            P(),
            P(),
            P(),
            P("tok", None),
            P("tok", None),
        ),
        out_specs=(P("grp", "tok", None), P("grp", "tok", None), P("grp", "tok", None)),
        check_vma=False,
    )
```

profile of v0, /device:TPU:23, one launch (start us, length us, event | category | flops | bytes accessed | tf_op | source)
XLA Modules:
  0.0 155.2 jit_solution(16902131133400837157)
XLA Ops:
  7.2 0.8 collective-permute-start.3
  8.2 2.6 %collective-permute-start.1 = (bf16[32,1024]{1,0:T(8,128)(2,1)}, bf16[32,1024]{1,0:T(8,128)(2,1)S(1)}, u32[]{:S(2)}, u32[]{:S(2)}) collective-permute-start(bf16[32,1024]{1,0:T(8,128)(2,1)} %bitcast.40), channel_id=1, source_target_pairs={{128,0},{192,64},{0,128},{64,192},{129,1},{193,65},{1,129},{65,193... | collective-permute-start | bytes 196616 | tf_op jit(solution)/shard_map/ppermute | solution.py:34
  10.9 0.7 constant_dynamic-slice_fusion.3
  11.6 0.7 add_convert_fusion.1
  12.3 22.5 %all-gather = bf16[640,512]{1,0:T(8,128)(2,1)S(1)} all-gather(bf16[40,512]{1,0:T(8,128)(2,1)S(1)} %fusion.8), channel_id=2, replica_groups={{0,1,2,3,4,5,6,7,8,9,10,11,12,13,14,15},{16,17,18,19,20,21,22,23,24,25,..., dimensions={0}, use_global_device_ids=true | all-gather | bytes 696320 | tf_op jit(solution)/shard_map/all_gather | solution.py:373
  34.8 1.2 dynamic_slice.26
  37.1 1.9 %collective-permute-start.7 = (bf16[256,256]{1,0:T(8,128)(2,1)S(1)}, bf16[256,256]{1,0:T(8,128)(2,1)S(1)}, u32[]{:S(2)}, u32[]{:S(2)}) collective-permute-start(bf16[256,256]{1,0:T(8,128)(2,1)S(1)} %bitcast.35), channel_id=1, source_target_pairs={{64,0},{128,64},{192,128},{0,192},{65,1},{129,65},{193,129},{1,193... | collective-permute-start | bytes 393224 | tf_op jit(solution)/shard_map/ppermute | solution.py:34
  39.1 0.6 collective-permute-start.4
  39.7 0.8 collective-permute-start.5
  40.6 1.8 %collective-permute-start.6 = (bf16[392,256]{1,0:T(8,128)(2,1)S(1)}, bf16[392,256]{1,0:T(8,128)(2,1)S(1)}, u32[]{:S(2)}, u32[]{:S(2)}) collective-permute-start(bf16[392,256]{1,0:T(8,128)(2,1)S(1)} %constant_dynamic-update-slice_fusion.p0), channel_id=1, source_target_pairs={{48,0},{49,1},{50,2},{51,3},{52,4},{53,5},{54,6},{55,7},{56,8},{57... | collective-permute-start | bytes 602120 | tf_op jit(solution)/shard_map/ppermute | solution.py:30
  42.4 1.4 collective-permute-start.8
  43.8 0.9 collective-permute-start.9
  44.7 3.4 %collective-permute-done.8.q2 = bf16[256,256]{1,0:T(8,128)(2,1)S(1)} collective-permute-done((bf16[256,256]{1,0:T(8,128)(2,1)S(1)}, bf16[256,256]{1,0:T(8,128)(2,1)S(1)}, u32[]{:S(2)}, u32[]{:S(2)}) %collective-permute-start.8) | collective-permute-done | bytes 131104 | tf_op jit(solution)/shard_map/ppermute | solution.py:34
  48.0 3.5 %collective-permute-done.9.q3 = bf16[256,256]{1,0:T(8,128)(2,1)S(1)} collective-permute-done((bf16[256,256]{1,0:T(8,128)(2,1)S(1)}, bf16[256,256]{1,0:T(8,128)(2,1)S(1)}, u32[]{:S(2)}, u32[]{:S(2)}) %collective-permute-start.9) | collective-permute-done | bytes 131104 | tf_op jit(solution)/shard_map/ppermute | solution.py:34
  51.6 0.6 copy-done.18
  52.3 0.7 copy-done.13
  53.0 2.5 %pack.1 = (bf16[1024,256]{1,0:T(8,128)(2,1)}, bf16[1024,256]{1,0:T(8,128)(2,1)}, bf16[128,1024]{1,0:T(8,128)(2,1)}) custom-call(bf16[392,256]{1,0:T(8,128)(2,1)} %copy-done.3, bf16[392,256]{1,0:T(8,128)(2,1)} %copy-done.14, bf16[392,256]{1,0:T(8,128)(2,1)} %copy-done.15, bf16[392,256]{1,0:T(8,128)(2,1)} %copy-done.13, bf16[256,256]{1,0:T(8,128)(2,1)} %bitcast.38, ...), custom_call_target="tpu_custom_call" | custom-call | tf_op jit(solution)/shard_map/pack/pallas_call | solution.py:332
  55.7 0.6 broadcast_in_dim.37.gain_ref
  56.3 4.0 %input_norm.1 = (bf16[512,1024]{1,0:T(8,128)(2,1)}, bf16[512,1024]{1,0:T(8,128)(2,1)}) custom-call(s32[1]{0:T(128)} %bitcast.x_ref, bf16[256,2048]{1,0:T(8,128)(2,1)} %bitcast.32, bf16[256,2048]{1,0:T(8,128)(2,1)} %copy-done.2, bf16[1,2048]{1,0:T(2,128)(2,1)} %broadcast_in_dim.37.gain_ref), custom_call_target="tpu_custom_call" | custom-call | tf_op jit(solution)/shard_map/input_norm/pallas_call | solution.py:68
  60.3 0.8 collective-permute-start.11
  61.1 2.1 %collective-permute-start.12 = (bf16[1024,256]{1,0:T(8,128)(2,1)S(1)}, bf16[1024,256]{1,0:T(8,128)(2,1)S(1)}, u32[]{:S(2)}, u32[]{:S(2)}) collective-permute-start(bf16[1024,256]{1,0:T(8,128)(2,1)S(1)} %copy-done.21), channel_id=1, source_target_pairs={{192,0},{0,64},{64,128},{128,192},{193,1},{1,65},{65,129},{129,193... | collective-permute-start | bytes 1572872 | tf_op jit(solution)/shard_map/ppermute | solution.py:34
  63.2 1.0 collective-permute-start.13
  64.2 3.1 %collective-permute-start.14 = (bf16[1024,256]{1,0:T(8,128)(2,1)S(1)}, bf16[1024,256]{1,0:T(8,128)(2,1)}, u32[]{:S(2)}, u32[]{:S(2)}) collective-permute-start(bf16[1024,256]{1,0:T(8,128)(2,1)S(1)} %copy-done.22), channel_id=1, source_target_pairs={{32,0},{33,1},{34,2},{35,3},{36,4},{37,5},{38,6},{39,7},{40,8},{41... | collective-permute-start | bytes 1572872 | tf_op jit(solution)/shard_map/ppermute | solution.py:30
  67.2 0.7 broadcast_select_fusion.3
  68.1 0.5 convert_reduce_fusion
  68.6 1.0 fusion.2
  69.6 3.2 %collective-permute-done.10.p1 = bf16[1024,256]{1,0:T(8,128)(2,1)S(1)} collective-permute-done((bf16[1024,256]{1,0:T(8,128)(2,1)S(1)}, bf16[1024,256]{1,0:T(8,128)(2,1)S(1)}, u32[]{:S(2)}, u32[]{:S(2)}) %collective-permute-start.10) | collective-permute-done | bytes 524320 | tf_op jit(solution)/shard_map/ppermute | solution.py:34
  72.8 2.8 %collective-permute-start.15 = (bf16[1024,256]{1,0:T(8,128)(2,1)S(1)}, bf16[1024,256]{1,0:T(8,128)(2,1)}, u32[]{:S(2)}, u32[]{:S(2)}) collective-permute-start(bf16[1024,256]{1,0:T(8,128)(2,1)S(1)} %copy-done.22), channel_id=1, source_target_pairs={{48,0},{49,1},{50,2},{51,3},{52,4},{53,5},{54,6},{55,7},{56,8},{57... | collective-permute-start | bytes 1572872 | tf_op jit(solution)/shard_map/ppermute | solution.py:30
  75.7 0.8 pad_maximum_fusion.1.cos_ref
  76.5 0.8 pad_maximum_fusion.2.sin_ref
  77.4 1.7 %fusion.bias = f32[512,1024]{1,0:T(8,128)} fusion(s32[1024]{0:T(1024)S(1)} %pad_add_fusion, f32[1024]{0:T(1024)S(1)} %bitcast.46, f32[512]{0:T(512)S(1)} %bitcast.50, s32[512]{0:T(512)S(1)} %pad_add_fusion.1), kind=kLoop, calls=%fused_computation.3 | loop fusion | flops 2097152 | bytes 2109440 | tf_op jit(solution)/shard_map/jit(_where)/select_n | solution.py:415
  79.1 1.1 constant_dynamic-slice_fusion.4.refs_0_
  80.2 6.1 %collective-permute-done.12.p3 = bf16[1024,256]{1,0:T(8,128)(2,1)S(1)} collective-permute-done((bf16[1024,256]{1,0:T(8,128)(2,1)S(1)}, bf16[1024,256]{1,0:T(8,128)(2,1)S(1)}, u32[]{:S(2)}, u32[]{:S(2)}) %collective-permute-start.12) | collective-permute-done | bytes 524320 | tf_op jit(solution)/shard_map/ppermute | solution.py:34
  86.3 2.9 %collective-permute-done.14.q2 = bf16[1024,256]{1,0:T(8,128)(2,1)} collective-permute-done((bf16[1024,256]{1,0:T(8,128)(2,1)S(1)}, bf16[1024,256]{1,0:T(8,128)(2,1)}, u32[]{:S(2)}, u32[]{:S(2)}) %collective-permute-start.14) | collective-permute-done | bytes 524320 | tf_op jit(solution)/shard_map/ppermute | solution.py:30
  89.2 1.4 collective-permute-start.17
  90.6 2.6 %collective-permute-start.18 = (bf16[256,1024]{1,0:T(8,128)(2,1)S(1)}, bf16[256,1024]{1,0:T(8,128)(2,1)S(1)}, u32[]{:S(2)}, u32[]{:S(2)}) collective-permute-start(bf16[256,1024]{1,0:T(8,128)(2,1)S(1)} %constant_dynamic-slice_fusion.4.refs_0_), channel_id=1, source_target_pairs={{32,0},{33,1},{34,2},{35,3},{36,4},{37,5},{38,6},{39,7},{40,8},{41... | collective-permute-start | bytes 1572872 | tf_op jit(solution)/shard_map/ppermute | solution.py:30
  93.2 8.2 %joint_projection.1 = (bf16[2,512,256]{2,1,0:T(8,128)(2,1)}, bf16[2,512,256]{2,1,0:T(8,128)(2,1)}) custom-call(s32[1]{0:T(128)} %bitcast.2.y_ref, bf16[512,1024]{1,0:T(8,128)(2,1)} %get-tuple-element.77.np_ref, bf16[512,1024]{1,0:T(8,128)(2,1)} %get-tuple-element.78.nq_ref, bf16[1024,256]{1,0:T(8,128)(2,1)} %get-tuple-element.79.p0, ...), custom_call_target="tpu_custom_call" | custom-call | flops 2147483648 | bytes 8388608 | tf_op jit(solution)/shard_map/joint_projection/pallas_call | solution.py:137
  101.4 3.3 %collective-permute-start.16 = (bf16[2,512,256]{2,1,0:T(8,128)(2,1)}, bf16[2,512,256]{2,1,0:T(8,128)(2,1)S(1)}, u32[]{:S(2)}, u32[]{:S(2)}) collective-permute-start(bf16[2,512,256]{2,1,0:T(8,128)(2,1)} %get-tuple-element.108.ko_ref.vo_ref), channel_id=1, source_target_pairs={{0,2},{1,3},{2,4},{3,5},{4,6},{5,7},{6,8},{7,9},{8,10},{9,11},{10,... | collective-permute-start | bytes 1572872 | tf_op jit(solution)/shard_map/ppermute | solution.py:40
  104.7 12.6 %prefix_attention.1 = (f32[4,512,128]{2,1,0:T(8,128)}, f32[4,512,1]{2,1,0:T(8,128)}, f32[4,512,1]{2,1,0:T(8,128)}) custom-call(s32[1]{0:T(128)} %bitcast.1.core_ref, bf16[2,512,256]{2,1,0:T(8,128)(2,1)} %get-tuple-element.91.q_ref, bf16[2048,1024]{1,0:T(8,128)(2,1)} %all-gather.6.cloned.1.call-done.k_ref.v_ref, ...), custom_call_target="tpu_custom_call" | custom-call | flops 2147483648 | bytes 4194304 | tf_op jit(solution)/shard_map/prefix_attention/pallas_call | solution.py:202
  117.4 7.5 %collective-permute-done.19.refs_3_ = bf16[256,1024]{1,0:T(8,128)(2,1)S(1)} collective-permute-done((bf16[256,1024]{1,0:T(8,128)(2,1)S(1)}, bf16[256,1024]{1,0:T(8,128)(2,1)S(1)}, u32[]{:S(2)}, u32[]{:S(2)}) %collective-permute-start.19) | collective-permute-done | bytes 524320 | tf_op jit(solution)/shard_map/ppermute | solution.py:30
  124.9 3.2 %collective-permute-start.25 = (bf16[2,512,256]{2,1,0:T(8,128)(2,1)}, bf16[2,512,256]{2,1,0:T(8,128)(2,1)S(1)}, u32[]{:S(2)}, u32[]{:S(2)}) collective-permute-start(bf16[2,512,256]{2,1,0:T(8,128)(2,1)} %get-tuple-element.108.ko_ref.vo_ref), channel_id=1, source_target_pairs={{1,0},{0,1},{3,2},{2,3},{5,4},{4,5},{7,6},{6,7},{9,8},{8,9},{11,10... | collective-permute-start | bytes 1572872 | tf_op jit(solution)/shard_map/ppermute | solution.py:30
  128.7 0.4 collective-permute-start.24
  129.1 0.6 pad_add_fusion.2.place_ref
  129.7 10.5 %suffix_attention.1 = (bf16[256,512]{1,0:T(8,128)(2,1)}, bf16[256,512]{1,0:T(8,128)(2,1)}) custom-call(bf16[2,512,256]{2,1,0:T(8,128)(2,1)} %get-tuple-element.91.q_ref, bf16[2,512,256]{2,1,0:T(8,128)(2,1)} %get-tuple-element.108.ko_ref.vo_ref, bf16[2,512,256]{2,1,0:T(8,128)(2,1)} %get-tuple-element.108.ko_ref.vo_ref, bf16[2,512,256]{2,1,0:T(8,128)(2,1)} %copy-done.1, ...), custom_call_target="tpu_custom_call" | custom-call | flops 1073741824 | bytes 4194304 | tf_op jit(solution)/shard_map/suffix_attention/pallas_call | solution.py:260
  140.5 1.0 broadcast_select_fusion
  141.5 0.8 pad_maximum_fusion
  142.5 0.6 copy-done.12
  143.8 4.6 %output_projection.1 = bf16[256,2048]{1,0:T(8,128)(2,1)} custom-call(s32[2]{0:T(128)} %pad_add_fusion.2.place_ref, bf16[256,512]{1,0:T(8,128)(2,1)} %get-tuple-element.102.mine_ref, bf16[256,512]{1,0:T(8,128)(2,1)} %copy-done.12, bf16[256,1024]{1,0:T(8,128)(2,1)} %copy-done, bf16[256,1024]{1,0:T(8,128)(2,1)} %copy-done.4, bf16[256,1024]{1,0:T(8,128)(2,1)} %copy-done.5, ...), custom_call_target="tpu_custom_call" | custom-call | flops 1073741824 | bytes 6291456 | tf_op jit(solution)/shard_map/output_projection/pallas_call | solution.py:305
  (110 shorter events, 2.8 us)
Async XLA Ops:
  7.2 31.8 %copy-start.19 = (bf16[1,32,1024]{2,1,0:T(8,128)(2,1)S(1)}, bf16[1,32,1024]{2,1,0:T(8,128)(2,1)}, u32[]{:S(2)}) copy-start(bf16[1,32,1024]{2,1,0:T(8,128)(2,1)} %param.11) | copy-start | bytes 196612
  7.2 71.9 %all-gather.4.cloned.1.call-start = ((), (), s32[]{:S(2)}) async-start(), calls=%async_computation | async-start | bytes 1114112 | tf_op jit(solution)/shard_map/all_gather | solution.py:357
  7.2 29.5 %collective-permute-start.3 = (bf16[256,2048]{1,0:T(8,128)(2,1)}, bf16[256,2048]{1,0:T(8,128)(2,1)S(1)}, u32[]{:S(2)}, u32[]{:S(2)}) collective-permute-start(bf16[256,2048]{1,0:T(8,128)(2,1)} %bitcast.31), channel_id=1, source_target_pairs={{1,0},{0,1},{3,2},{2,3},{5,4},{4,5},{7,6},{6,7},{9,8},{8,9},{11,10... | collective-permute-start | bytes 3145736 | tf_op jit(solution)/shard_map/ppermute | solution.py:30
  8.0 28.7 %collective-permute-start = (bf16[32,1024]{1,0:T(8,128)(2,1)}, bf16[32,1024]{1,0:T(8,128)(2,1)S(1)}, u32[]{:S(2)}, u32[]{:S(2)}) collective-permute-start(bf16[32,1024]{1,0:T(8,128)(2,1)} %bitcast.39), channel_id=1, source_target_pairs={{64,0},{128,64},{192,128},{0,192},{65,1},{129,65},{193,129},{1,193... | collective-permute-start | bytes 196616 | tf_op jit(solution)/shard_map/ppermute | solution.py:34
  8.2 28.6 %collective-permute-start.1 = (bf16[32,1024]{1,0:T(8,128)(2,1)}, bf16[32,1024]{1,0:T(8,128)(2,1)S(1)}, u32[]{:S(2)}, u32[]{:S(2)}) collective-permute-start(bf16[32,1024]{1,0:T(8,128)(2,1)} %bitcast.40), channel_id=1, source_target_pairs={{128,0},{192,64},{0,128},{64,192},{129,1},{193,65},{1,129},{65,193... | collective-permute-start | bytes 196616 | tf_op jit(solution)/shard_map/ppermute | solution.py:34
  10.8 25.9 %collective-permute-start.2 = (bf16[32,1024]{1,0:T(8,128)(2,1)}, bf16[32,1024]{1,0:T(8,128)(2,1)S(1)}, u32[]{:S(2)}, u32[]{:S(2)}) collective-permute-start(bf16[32,1024]{1,0:T(8,128)(2,1)} %bitcast.41), channel_id=1, source_target_pairs={{192,0},{0,64},{64,128},{128,192},{193,1},{1,65},{65,129},{129,193... | collective-permute-start | bytes 196616 | tf_op jit(solution)/shard_map/ppermute | solution.py:34
  10.8 93.9 %all-gather.6.cloned.1.call-start = ((), (), s32[]{:S(2)}) async-start(), calls=%async_computation.1 | async-start | bytes 4456448 | tf_op jit(solution)/shard_map/all_gather | solution.py:398
  36.7 18.7 %copy-start.2 = (bf16[256,2048]{1,0:T(8,128)(2,1)}, bf16[256,2048]{1,0:T(8,128)(2,1)S(1)}, u32[]{:S(2)}) copy-start(bf16[256,2048]{1,0:T(8,128)(2,1)S(1)} %collective-permute-done.3.peer_ref) | copy-start | bytes 3145732
  36.8 18.9 %copy-start.20 = (bf16[2048]{0:T(1024)(128)(2,1)S(1)}, bf16[2048]{0:T(1024)(128)(2,1)}, u32[]{:S(2)}) copy-start(bf16[2048]{0:T(1024)(128)(2,1)} %param.13) | copy-start | bytes 12292
  37.1 14.5 %copy-start.11 = (bf16[8,32,256]{2,1,0:T(8,128)(2,1)}, bf16[8,32,256]{2,1,0:T(8,128)(2,1)S(1)}, u32[]{:S(2)}) copy-start(bf16[8,32,256]{2,1,0:T(8,128)(2,1)S(1)} %get-tuple-element.113) | copy-start | bytes 393220
  37.1 6.7 %collective-permute-start.7 = (bf16[256,256]{1,0:T(8,128)(2,1)S(1)}, bf16[256,256]{1,0:T(8,128)(2,1)S(1)}, u32[]{:S(2)}, u32[]{:S(2)}) collective-permute-start(bf16[256,256]{1,0:T(8,128)(2,1)S(1)} %bitcast.35), channel_id=1, source_target_pairs={{64,0},{128,64},{192,128},{0,192},{65,1},{129,65},{193,129},{1,193... | collective-permute-start | bytes 393224 | tf_op jit(solution)/shard_map/ppermute | solution.py:34
  39.1 12.5 %copy-start.3 = (bf16[392,256]{1,0:T(8,128)(2,1)}, bf16[392,256]{1,0:T(8,128)(2,1)S(1)}, u32[]{:S(2)}) copy-start(bf16[392,256]{1,0:T(8,128)(2,1)S(1)} %constant_dynamic-update-slice_fusion.p0) | copy-start | bytes 602116
  39.1 12.4 %collective-permute-start.4 = (bf16[392,256]{1,0:T(8,128)(2,1)S(1)}, bf16[392,256]{1,0:T(8,128)(2,1)S(1)}, u32[]{:S(2)}, u32[]{:S(2)}) collective-permute-start(bf16[392,256]{1,0:T(8,128)(2,1)S(1)} %constant_dynamic-update-slice_fusion.p0), channel_id=1, source_target_pairs={{16,0},{17,1},{18,2},{19,3},{20,4},{21,5},{22,6},{23,7},{24,8},{25... | collective-permute-start | bytes 602120 | tf_op jit(solution)/shard_map/ppermute | solution.py:30
  39.7 11.8 %collective-permute-start.5 = (bf16[392,256]{1,0:T(8,128)(2,1)S(1)}, bf16[392,256]{1,0:T(8,128)(2,1)S(1)}, u32[]{:S(2)}, u32[]{:S(2)}) collective-permute-start(bf16[392,256]{1,0:T(8,128)(2,1)S(1)} %constant_dynamic-update-slice_fusion.p0), channel_id=1, source_target_pairs={{32,0},{33,1},{34,2},{35,3},{36,4},{37,5},{38,6},{39,7},{40,8},{41... | collective-permute-start | bytes 602120 | tf_op jit(solution)/shard_map/ppermute | solution.py:30
  40.6 11.0 %collective-permute-start.6 = (bf16[392,256]{1,0:T(8,128)(2,1)S(1)}, bf16[392,256]{1,0:T(8,128)(2,1)S(1)}, u32[]{:S(2)}, u32[]{:S(2)}) collective-permute-start(bf16[392,256]{1,0:T(8,128)(2,1)S(1)} %constant_dynamic-update-slice_fusion.p0), channel_id=1, source_target_pairs={{48,0},{49,1},{50,2},{51,3},{52,4},{53,5},{54,6},{55,7},{56,8},{57... | collective-permute-start | bytes 602120 | tf_op jit(solution)/shard_map/ppermute | solution.py:30
  42.4 5.7 %collective-permute-start.8 = (bf16[256,256]{1,0:T(8,128)(2,1)S(1)}, bf16[256,256]{1,0:T(8,128)(2,1)S(1)}, u32[]{:S(2)}, u32[]{:S(2)}) collective-permute-start(bf16[256,256]{1,0:T(8,128)(2,1)S(1)} %bitcast.36), channel_id=1, source_target_pairs={{128,0},{192,64},{0,128},{64,192},{129,1},{193,65},{1,129},{65,193... | collective-permute-start | bytes 393224 | tf_op jit(solution)/shard_map/ppermute | solution.py:34
  43.8 7.8 %copy-start.16 = (bf16[256,256]{1,0:T(8,128)(2,1)}, bf16[256,256]{1,0:T(8,128)(2,1)S(1)}, u32[]{:S(2)}) copy-start(bf16[256,256]{1,0:T(8,128)(2,1)S(1)} %collective-permute-done.7.q1) | copy-start | bytes 393220
  43.8 7.8 %collective-permute-start.9 = (bf16[256,256]{1,0:T(8,128)(2,1)S(1)}, bf16[256,256]{1,0:T(8,128)(2,1)S(1)}, u32[]{:S(2)}, u32[]{:S(2)}) collective-permute-start(bf16[256,256]{1,0:T(8,128)(2,1)S(1)} %bitcast.37), channel_id=1, source_target_pairs={{192,0},{0,64},{64,128},{128,192},{193,1},{1,65},{65,129},{129,193... | collective-permute-start | bytes 393224 | tf_op jit(solution)/shard_map/ppermute | solution.py:34
  48.0 3.5 %copy-start.17 = (bf16[256,256]{1,0:T(8,128)(2,1)}, bf16[256,256]{1,0:T(8,128)(2,1)S(1)}, u32[]{:S(2)}) copy-start(bf16[256,256]{1,0:T(8,128)(2,1)S(1)} %collective-permute-done.8.q2) | copy-start | bytes 393220
  55.5 4.8 %copy-start.21 = (bf16[1024,256]{1,0:T(8,128)(2,1)S(1)}, bf16[1024,256]{1,0:T(8,128)(2,1)}, u32[]{:S(2)}) copy-start(bf16[1024,256]{1,0:T(8,128)(2,1)} %get-tuple-element.79.p0) | copy-start | bytes 1572868
  55.5 7.7 %copy-start.22 = (bf16[1024,256]{1,0:T(8,128)(2,1)S(1)}, bf16[1024,256]{1,0:T(8,128)(2,1)}, u32[]{:S(2)}) copy-start(bf16[1024,256]{1,0:T(8,128)(2,1)} %get-tuple-element.83.q0) | copy-start | bytes 1572868
  60.3 12.6 %collective-permute-start.10 = (bf16[1024,256]{1,0:T(8,128)(2,1)S(1)}, bf16[1024,256]{1,0:T(8,128)(2,1)S(1)}, u32[]{:S(2)}, u32[]{:S(2)}) collective-permute-start(bf16[1024,256]{1,0:T(8,128)(2,1)S(1)} %copy-done.21), channel_id=1, source_target_pairs={{64,0},{128,64},{192,128},{0,192},{65,1},{129,65},{193,129},{1,193... | collective-permute-start | bytes 1572872 | tf_op jit(solution)/shard_map/ppermute | solution.py:34
  60.3 19.9 %collective-permute-start.11 = (bf16[1024,256]{1,0:T(8,128)(2,1)S(1)}, bf16[1024,256]{1,0:T(8,128)(2,1)S(1)}, u32[]{:S(2)}, u32[]{:S(2)}) collective-permute-start(bf16[1024,256]{1,0:T(8,128)(2,1)S(1)} %copy-done.21), channel_id=1, source_target_pairs={{128,0},{192,64},{0,128},{64,192},{129,1},{193,65},{1,129},{65,193... | collective-permute-start | bytes 1572872 | tf_op jit(solution)/shard_map/ppermute | solution.py:34
  61.1 25.1 %collective-permute-start.12 = (bf16[1024,256]{1,0:T(8,128)(2,1)S(1)}, bf16[1024,256]{1,0:T(8,128)(2,1)S(1)}, u32[]{:S(2)}, u32[]{:S(2)}) collective-permute-start(bf16[1024,256]{1,0:T(8,128)(2,1)S(1)} %copy-done.21), channel_id=1, source_target_pairs={{192,0},{0,64},{64,128},{128,192},{193,1},{1,65},{65,129},{129,193... | collective-permute-start | bytes 1572872 | tf_op jit(solution)/shard_map/ppermute | solution.py:34
  63.2 23.1 %collective-permute-start.13 = (bf16[1024,256]{1,0:T(8,128)(2,1)S(1)}, bf16[1024,256]{1,0:T(8,128)(2,1)}, u32[]{:S(2)}, u32[]{:S(2)}) collective-permute-start(bf16[1024,256]{1,0:T(8,128)(2,1)S(1)} %copy-done.22), channel_id=1, source_target_pairs={{16,0},{17,1},{18,2},{19,3},{20,4},{21,5},{22,6},{23,7},{24,8},{25... | collective-permute-start | bytes 1572872 | tf_op jit(solution)/shard_map/ppermute | solution.py:30
  64.2 25.0 %collective-permute-start.14 = (bf16[1024,256]{1,0:T(8,128)(2,1)S(1)}, bf16[1024,256]{1,0:T(8,128)(2,1)}, u32[]{:S(2)}, u32[]{:S(2)}) collective-permute-start(bf16[1024,256]{1,0:T(8,128)(2,1)S(1)} %copy-done.22), channel_id=1, source_target_pairs={{32,0},{33,1},{34,2},{35,3},{36,4},{37,5},{38,6},{39,7},{40,8},{41... | collective-permute-start | bytes 1572872 | tf_op jit(solution)/shard_map/ppermute | solution.py:30
  72.8 6.2 %copy-start.23 = (bf16[1024,256]{1,0:T(8,128)(2,1)}, bf16[1024,256]{1,0:T(8,128)(2,1)S(1)}, u32[]{:S(2)}) copy-start(bf16[1024,256]{1,0:T(8,128)(2,1)S(1)} %collective-permute-done.10.p1) | copy-start | bytes 1572868
  72.8 16.3 %collective-permute-start.15 = (bf16[1024,256]{1,0:T(8,128)(2,1)S(1)}, bf16[1024,256]{1,0:T(8,128)(2,1)}, u32[]{:S(2)}, u32[]{:S(2)}) collective-permute-start(bf16[1024,256]{1,0:T(8,128)(2,1)S(1)} %copy-done.22), channel_id=1, source_target_pairs={{48,0},{49,1},{50,2},{51,3},{52,4},{53,5},{54,6},{55,7},{56,8},{57... | collective-permute-start | bytes 1572872 | tf_op jit(solution)/shard_map/ppermute | solution.py:30
  80.2 47.9 %copy-start = (bf16[256,1024]{1,0:T(8,128)(2,1)}, bf16[256,1024]{1,0:T(8,128)(2,1)S(1)}, u32[]{:S(2)}) copy-start(bf16[256,1024]{1,0:T(8,128)(2,1)S(1)} %constant_dynamic-slice_fusion.4.refs_0_) | copy-start | bytes 1572868
  80.2 9.0 %copy-start.24 = (bf16[1024,256]{1,0:T(8,128)(2,1)}, bf16[1024,256]{1,0:T(8,128)(2,1)S(1)}, u32[]{:S(2)}) copy-start(bf16[1024,256]{1,0:T(8,128)(2,1)S(1)} %collective-permute-done.11.p2) | copy-start | bytes 1572868
  86.3 2.9 %copy-start.25 = (bf16[1024,256]{1,0:T(8,128)(2,1)}, bf16[1024,256]{1,0:T(8,128)(2,1)S(1)}, u32[]{:S(2)}) copy-start(bf16[1024,256]{1,0:T(8,128)(2,1)S(1)} %collective-permute-done.12.p3) | copy-start | bytes 1572868
  89.2 28.2 %collective-permute-start.17 = (bf16[256,1024]{1,0:T(8,128)(2,1)S(1)}, bf16[256,1024]{1,0:T(8,128)(2,1)S(1)}, u32[]{:S(2)}, u32[]{:S(2)}) collective-permute-start(bf16[256,1024]{1,0:T(8,128)(2,1)S(1)} %constant_dynamic-slice_fusion.4.refs_0_), channel_id=1, source_target_pairs={{16,0},{17,1},{18,2},{19,3},{20,4},{21,5},{22,6},{23,7},{24,8},{25... | collective-permute-start | bytes 1572872 | tf_op jit(solution)/shard_map/ppermute | solution.py:30
  90.6 26.8 %collective-permute-start.18 = (bf16[256,1024]{1,0:T(8,128)(2,1)S(1)}, bf16[256,1024]{1,0:T(8,128)(2,1)S(1)}, u32[]{:S(2)}, u32[]{:S(2)}) collective-permute-start(bf16[256,1024]{1,0:T(8,128)(2,1)S(1)} %constant_dynamic-slice_fusion.4.refs_0_), channel_id=1, source_target_pairs={{32,0},{33,1},{34,2},{35,3},{36,4},{37,5},{38,6},{39,7},{40,8},{41... | collective-permute-start | bytes 1572872 | tf_op jit(solution)/shard_map/ppermute | solution.py:30
  93.2 31.7 %collective-permute-start.19 = (bf16[256,1024]{1,0:T(8,128)(2,1)S(1)}, bf16[256,1024]{1,0:T(8,128)(2,1)S(1)}, u32[]{:S(2)}, u32[]{:S(2)}) collective-permute-start(bf16[256,1024]{1,0:T(8,128)(2,1)S(1)} %constant_dynamic-slice_fusion.4.refs_0_), channel_id=1, source_target_pairs={{48,0},{49,1},{50,2},{51,3},{52,4},{53,5},{54,6},{55,7},{56,8},{57... | collective-permute-start | bytes 1572872 | tf_op jit(solution)/shard_map/ppermute | solution.py:30
  101.4 27.3 %collective-permute-start.16 = (bf16[2,512,256]{2,1,0:T(8,128)(2,1)}, bf16[2,512,256]{2,1,0:T(8,128)(2,1)S(1)}, u32[]{:S(2)}, u32[]{:S(2)}) collective-permute-start(bf16[2,512,256]{2,1,0:T(8,128)(2,1)} %get-tuple-element.108.ko_ref.vo_ref), channel_id=1, source_target_pairs={{0,2},{1,3},{2,4},{3,5},{4,6},{5,7},{6,8},{7,9},{8,10},{9,11},{10,... | collective-permute-start | bytes 1572872 | tf_op jit(solution)/shard_map/ppermute | solution.py:40
  117.4 25.1 %copy-start.4 = (bf16[256,1024]{1,0:T(8,128)(2,1)}, bf16[256,1024]{1,0:T(8,128)(2,1)S(1)}, u32[]{:S(2)}) copy-start(bf16[256,1024]{1,0:T(8,128)(2,1)S(1)} %collective-permute-done.17.refs_1_) | copy-start | bytes 1572868
  117.4 25.0 %copy-start.5 = (bf16[256,1024]{1,0:T(8,128)(2,1)}, bf16[256,1024]{1,0:T(8,128)(2,1)S(1)}, u32[]{:S(2)}) copy-start(bf16[256,1024]{1,0:T(8,128)(2,1)S(1)} %collective-permute-done.18.refs_2_) | copy-start | bytes 1572868
  124.9 17.6 %copy-start.6 = (bf16[256,1024]{1,0:T(8,128)(2,1)}, bf16[256,1024]{1,0:T(8,128)(2,1)S(1)}, u32[]{:S(2)}) copy-start(bf16[256,1024]{1,0:T(8,128)(2,1)S(1)} %collective-permute-done.19.refs_3_) | copy-start | bytes 1572868
  124.9 15.3 %collective-permute-start.25 = (bf16[2,512,256]{2,1,0:T(8,128)(2,1)}, bf16[2,512,256]{2,1,0:T(8,128)(2,1)S(1)}, u32[]{:S(2)}, u32[]{:S(2)}) collective-permute-start(bf16[2,512,256]{2,1,0:T(8,128)(2,1)} %get-tuple-element.108.ko_ref.vo_ref), channel_id=1, source_target_pairs={{1,0},{0,1},{3,2},{2,3},{5,4},{4,5},{7,6},{6,7},{9,8},{8,9},{11,10... | collective-permute-start | bytes 1572872 | tf_op jit(solution)/shard_map/ppermute | solution.py:30
  128.1 14.3 %collective-permute-start.21 = (bf16[256,1024]{1,0:T(8,128)(2,1)S(1)}, bf16[256,1024]{1,0:T(8,128)(2,1)S(1)}, u32[]{:S(2)}, u32[]{:S(2)}) collective-permute-start(bf16[256,1024]{1,0:T(8,128)(2,1)S(1)} %constant_dynamic-slice_fusion.4.refs_0_), channel_id=1, source_target_pairs={{1,0},{0,1},{3,2},{2,3},{5,4},{4,5},{7,6},{6,7},{9,8},{8,9},{11,10... | collective-permute-start | bytes 1572872 | tf_op jit(solution)/shard_map/ppermute | solution.py:30
  128.2 14.2 %collective-permute-start.22 = (bf16[256,1024]{1,0:T(8,128)(2,1)S(1)}, bf16[256,1024]{1,0:T(8,128)(2,1)S(1)}, u32[]{:S(2)}, u32[]{:S(2)}) collective-permute-start(bf16[256,1024]{1,0:T(8,128)(2,1)S(1)} %collective-permute-done.17.refs_1_), channel_id=1, source_target_pairs={{1,0},{0,1},{3,2},{2,3},{5,4},{4,5},{7,6},{6,7},{9,8},{8,9},{11,10... | collective-permute-start | bytes 1572872 | tf_op jit(solution)/shard_map/ppermute | solution.py:30
  128.6 13.8 %collective-permute-start.23 = (bf16[256,1024]{1,0:T(8,128)(2,1)S(1)}, bf16[256,1024]{1,0:T(8,128)(2,1)S(1)}, u32[]{:S(2)}, u32[]{:S(2)}) collective-permute-start(bf16[256,1024]{1,0:T(8,128)(2,1)S(1)} %collective-permute-done.18.refs_2_), channel_id=1, source_target_pairs={{1,0},{0,1},{3,2},{2,3},{5,4},{4,5},{7,6},{6,7},{9,8},{8,9},{11,10... | collective-permute-start | bytes 1572872 | tf_op jit(solution)/shard_map/ppermute | solution.py:30
  128.7 1.0 copy-start.1
  128.7 13.7 %collective-permute-start.24 = (bf16[256,1024]{1,0:T(8,128)(2,1)S(1)}, bf16[256,1024]{1,0:T(8,128)(2,1)S(1)}, u32[]{:S(2)}, u32[]{:S(2)}) collective-permute-start(bf16[256,1024]{1,0:T(8,128)(2,1)S(1)} %collective-permute-done.19.refs_3_), channel_id=1, source_target_pairs={{1,0},{0,1},{3,2},{2,3},{5,4},{4,5},{7,6},{6,7},{9,8},{8,9},{11,10... | collective-permute-start | bytes 1572872 | tf_op jit(solution)/shard_map/ppermute | solution.py:30
  140.2 2.1 %collective-permute-start.20 = (bf16[256,512]{1,0:T(8,128)(2,1)}, bf16[256,512]{1,0:T(8,128)(2,1)S(1)}, u32[]{:S(2)}, u32[]{:S(2)}) collective-permute-start(bf16[256,512]{1,0:T(8,128)(2,1)} %get-tuple-element.103), channel_id=1, source_target_pairs={{1,0},{0,1},{3,2},{2,3},{5,4},{4,5},{7,6},{6,7},{9,8},{8,9},{11,10... | collective-permute-start | bytes 786440 | tf_op jit(solution)/shard_map/ppermute | solution.py:30
  142.4 1.0 copy-start.8
  142.4 1.2 copy-start.9
  142.4 1.3 copy-start.10
  (6 other events, 4.5 us)
Sparse Core Ops, SparseCore 0:
  10.9 42.0 all-gather.3
  55.6 41.0 all-gather.5
where the time goes:
time: 157 us; the launch traced here: 155 us
  Pallas kernels  42.4 us (27%)
  starting transfers between devices  32.7 us (21%)
  waiting for transfers between devices  26.6 us (17%)
  blocking collectives  22.5 us (14%)
  between operations  15.3 us (10%)
  other arithmetic  8.8 us (6%)
  local copies, waits for them, and re-layouts  6.9 us (4%)
    all_gather x1, blocking collectives, per_device(): both = lax.all_gather(first, 'tok', axis_index_groups=GROUP_ZC)  22.5 us
    ppermute x16, starting transfers between devices, from_tok(): return lax.ppermute(block, 'tok', route)  19.5 us
    ppermute x9, waiting for transfers between devices, from_grp(): return lax.ppermute(block, 'grp', [((y + dy) % NY, y) for y in range(NY)])  16.1 us
    pallas_call x1, Pallas kernels, prefix_attention(): pl.pallas_call(functools.partial(prefix_kernel, scale), out_shape=(jax.Sh...  12.6 us
    pallas_call x1, Pallas kernels, suffix_attention(): pl.pallas_call(functools.partial(suffix_kernel, scale), out_shape=(out, o...  10.5 us
    ppermute x16, waiting for transfers between devices, from_tok(): return lax.ppermute(block, 'tok', route)  10.4 us
    ppermute x9, starting transfers between devices, from_grp(): return lax.ppermute(block, 'grp', [((y + dy) % NY, y) for y in range(NY)])  9.89 us
    pallas_call x1, Pallas kernels, joint_projection(): pl.pallas_call(qkv_kernel, out_shape=(out, out), grid_spec=pltpu.Prefetch...  8.2 us
  transfers between devices with their start and end apart: 28, of which 6 were waited for; matrix products, arithmetic and copies ran while one was open for 8% of the time, Pallas kernels for 24%

commit v1 on v0

--- a/solution.py
+++ b/solution.py
@@ -170,38 +170,42 @@
     return jnp.max(fold(jnp.maximum, blocks), axis=-1, keepdims=True)
 
 
-def prefix_kernel(scale, core_ref, q_ref, k_ref, v_ref, acc_ref, top_ref, total_ref):
-    rows = q_ref.shape[1]
-    step = 512
+def prefix_kernel(scale, core_ref, q_ref, k_ref, v_ref, acc_ref, stat_ref):
+    rows, step = 256, 512
     starts = range(0, k_ref.shape[0], step)
-    q = jnp.concatenate([q_ref[0, :, :128], q_ref[0, :, 128:]], axis=0)
-    scores = [
-        lax.dot_general(q, k_ref[i : i + step, :], LANES, preferred_element_type=jnp.float32)
-        for i in starts
-    ]
-    top = row_max(scores)
-    total = jnp.zeros(q.shape, jnp.float32)
-    acc = jnp.zeros(q.shape, jnp.float32)
-    for s, i in zip(scores, starts):
-        w = jnp.exp2((s - top) * scale)
-        total = total + fold(jnp.add, [w])
-        acc = acc + jnp.dot(
-            w.astype(jnp.bfloat16), v_ref[i : i + step, :], preferred_element_type=jnp.float32
-        )
-    total = jnp.sum(total, axis=-1, keepdims=True)
-    for h in range(2):
-        at = slice(h * rows, (h + 1) * rows)
-        acc_ref[h], top_ref[h], total_ref[h] = acc[at], top[at], total[at]
+    for r in range(0, q_ref.shape[1], rows):
+        for h in range(2):
+            q = q_ref[0, r : r + rows, h * 128 : (h + 1) * 128]
+            scores = [
+                lax.dot_general(
+                    q, k_ref[i : i + step, :], LANES, preferred_element_type=jnp.float32
+                )
+                for i in starts
+            ]
+            top = row_max(scores)
+            total = jnp.zeros(q.shape, jnp.float32)
+            acc = jnp.zeros(q.shape, jnp.float32)
+            for s, i in zip(scores, starts):
+                w = jnp.exp2((s - top) * scale)
+                total = total + fold(jnp.add, [w])
+                acc = acc + jnp.dot(
+                    w.astype(jnp.bfloat16),
+                    v_ref[i : i + step, :],
+                    preferred_element_type=jnp.float32,
+                )
+            acc_ref[h, r : r + rows, :] = acc
+            stat_ref[h, r : r + rows, 0:1] = top
+            stat_ref[h, r : r + rows, 1:2] = jnp.sum(total, axis=-1, keepdims=True)
 
 
 def prefix_attention(core, qkv, prefix, scale):
     rows = qkv.shape[1]
     keys = prefix.shape[0]
-    stat = jax.ShapeDtypeStruct((4, rows, 1), jnp.float32)
-    pair = lambda width: pl.BlockSpec((2, rows, width), lambda g, c: (g, 0, 0))
+    out = jax.ShapeDtypeStruct((4, rows, 128), jnp.float32)
+    pair = pl.BlockSpec((2, rows, 128), lambda g, c: (g, 0, 0))
     return pl.pallas_call(
         functools.partial(prefix_kernel, scale),
-        out_shape=(jax.ShapeDtypeStruct((4, rows, 128), jnp.float32), stat, stat),
+        out_shape=(out, out),
         grid_spec=pltpu.PrefetchScalarGridSpec(
             num_scalar_prefetch=1,
             grid=(2,),
@@ -210,7 +214,7 @@
                 pl.BlockSpec((keys, 128), lambda g, c: (0, 2 * c[0] + g)),
                 pl.BlockSpec((keys, 128), lambda g, c: (0, 4 + 2 * c[0] + g)),
             ],
-            out_specs=(pair(128), pair(1), pair(1)),
+            out_specs=(pair, pair),
         ),
         compiler_params=pltpu.CompilerParams(
             dimension_semantics=("arbitrary",), vmem_limit_bytes=VMEM_LIMIT
@@ -223,64 +227,70 @@
 
 
 def suffix_kernel(
-    scale, q_ref, ko_ref, vo_ref, kh_ref, vh_ref, acc_ref, top_ref, total_ref,
-    bias, own_ref, peer_ref
+    scale, core_ref, q_ref, ko_ref, vo_ref, kh_ref, vh_ref, acc_ref, stat_ref, bias_ref,
+    own_ref, peer_ref
 ):
-    rows, chip = q_ref.shape[1], ko_ref.shape[1]
-
-    for h in range(2):
-        at = slice(h * 128, (h + 1) * 128)
-        q = q_ref[0, :, at]
-        scores = [
-            lax.dot_general(q, k[0], LANES, preferred_element_type=jnp.float32)
-            + bias[:, i * chip : (i + 1) * chip]
-            for i, k in enumerate((kh_ref, ko_ref))
-        ]
-        before = top_ref[h]
-        top = jnp.maximum(before, row_max(scores))
-        shrink = jnp.exp2((before - top) * scale)
-        total = jnp.zeros((rows, 128), jnp.float32)
-        acc = acc_ref[h] * shrink
-        for s, v in zip(scores, (vh_ref, vo_ref)):
-            w = jnp.exp2((s - top) * scale)
-            total = total + fold(jnp.add, [w])
-            acc = acc + jnp.dot(w.astype(jnp.bfloat16), v[0], preferred_element_type=jnp.float32)
-        total = total_ref[h] * shrink + jnp.sum(total, axis=-1, keepdims=True)
-        out = (acc / total).astype(jnp.bfloat16)
-        own_ref[:, at] = out[: rows // 2]
-        peer_ref[:, at] = out[rows // 2 :]
-
-
-def suffix_attention(queries, own, halo, partial, bias, scale):
+    core = core_ref[0]
+    rows = own_ref.shape[0]
+    zero = pl.ds(pl.multiple_of(core * rows, rows), rows)
+    one = pl.ds(pl.multiple_of((1 - core) * rows, rows), rows)
+    for r, out_ref in enumerate((own_ref, peer_ref)):
+        block = slice(r * rows, (r + 1) * rows)
+        third = [jnp.where(core == r, h[0, block, :], o[0, block, :])
+                 for h, o in ((kh_ref, ko_ref), (vh_ref, vo_ref))]
+        keys = [kh_ref[0, one, :], ko_ref[0, zero, :], third[0]]
+        values = [vh_ref[0, one, :], vo_ref[0, zero, :], third[1]]
+        for h in range(2):
+            q = q_ref[0, block, h * 128 : (h + 1) * 128]
+            scores = [
+                lax.dot_general(q, k, LANES, preferred_element_type=jnp.float32)
+                + bias_ref[r, :, i * rows : (i + 1) * rows].astype(jnp.float32)
+                for i, k in enumerate(keys)
+            ]
+            before = stat_ref[h, block, 0:1]
+            top = jnp.maximum(before, row_max(scores))
+            shrink = jnp.exp2((before - top) * scale)
+            weights = [jnp.exp2((s - top) * scale) for s in scores]
+            total = jnp.sum(fold(jnp.add, weights), axis=-1, keepdims=True)
+            total = stat_ref[h, block, 1:2] * shrink + total
+            acc = acc_ref[h, block, :] * shrink
+            for w, v in zip(weights, values):
+                acc = acc + jnp.dot(w.astype(jnp.bfloat16), v, preferred_element_type=jnp.float32)
+            out_ref[:, h * 128 : (h + 1) * 128] = (acc / total).astype(jnp.bfloat16)
+
+
+def suffix_attention(core, queries, own, halo, partial, bias, scale):
     rows = queries.shape[1]
-    pair = lambda width: pl.BlockSpec((2, rows, width), lambda g: (g, 0, 0))
-    head = lambda block: pl.BlockSpec((1, rows, 128), lambda g: (block, 0, g))
+    pair = pl.BlockSpec((2, rows, 128), lambda g, c: (g, 0, 0))
+    head = lambda block: pl.BlockSpec((1, rows, 128), lambda g, c: (block, 0, g))
     out = jax.ShapeDtypeStruct((rows // 2, 512), jnp.bfloat16)
-    out_spec = pl.BlockSpec((rows // 2, 256), lambda g: (0, g))
+    out_spec = pl.BlockSpec((rows // 2, 256), lambda g, c: (0, g))
     return pl.pallas_call(
         functools.partial(suffix_kernel, scale),
         out_shape=(out, out),
-        grid=(2,),
-        in_specs=[
-            pl.BlockSpec((1, rows, 256), lambda g: (g, 0, 0)),
-            head(0),
-            head(1),
-            head(0),
-            head(1),
-            pair(128),
-            pair(1),
-            pair(1),
-            pl.BlockSpec(bias.shape, lambda g: (0, 0)),
-        ],
-        out_specs=(out_spec, out_spec),
+        grid_spec=pltpu.PrefetchScalarGridSpec(
+            num_scalar_prefetch=1,
+            grid=(2,),
+            in_specs=[
+                pl.BlockSpec((1, rows, 256), lambda g, c: (g, 0, 0)),
+                head(0),
+                head(1),
+                head(0),
+                head(1),
+                pair,
+                pair,
+                pl.BlockSpec(bias.shape, lambda g, c: (0, 0, 0)),
+            ],
+            out_specs=(out_spec, out_spec),
+        ),
         compiler_params=pltpu.CompilerParams(
             dimension_semantics=("arbitrary",), vmem_limit_bytes=VMEM_LIMIT
         ),
         cost_estimate=pl.CostEstimate(
-            flops=4 * 4 * rows * 1024 * 128, transcendentals=4 * rows * 1024, bytes_accessed=4 << 20
+            flops=4 * 4 * rows * 768 * 128, transcendentals=4 * rows * 768, bytes_accessed=4 << 20
         ),
         name="suffix_attention",
-    )(queries, own, own, halo, halo, *partial, bias)
+    )(core, queries, own, own, halo, halo, *partial, bias)
 
 
 def out_kernel(place_ref, mine_ref, other_ref, *refs):
@@ -372,8 +382,8 @@
     )
     both = lax.all_gather(first, "tok", axis_index_groups=GROUP_ZC)
     peer = from_tok(own, dc=1)
-    both, owners, peer, norm_gain, query_gain, key_norm_gain = lax.optimization_barrier(
-        (both, owners, peer, norm_gain, query_gain, key_norm_gain)
+    both, owners, peer, query_gain, key_norm_gain = lax.optimization_barrier(
+        (both, owners, peer, query_gain, key_norm_gain)
     )
 
     marks_x = both[:, 32, :256]
@@ -397,23 +407,30 @@
     q2 = from_tok(q0, dx=2)
     prefix = lax.all_gather(prefix_part, "tok", axis_index_groups=GROUP_ZC, tiled=True)
 
+    own, peer, norm_gain, p1 = lax.optimization_barrier((own, peer, norm_gain, p1))
     normed_p, normed_q = input_norm(x[None], own, peer, norm_gain[None, :])
     marks_left = jnp.where(x > 0, p_all[3][384:386], 0)
     near = lax.dynamic_slice_in_dim(
         jnp.concatenate([marks_left, marks_x]).astype(jnp.float32), 2 * z, 4, 0
     )
-    near = near.reshape(2, 2, rows)
-    near = jnp.where(core == 0, near, near[:, ::-1])
-    marks_k = near.reshape(1, 4 * rows)
-    marks_q = near[1].reshape(2 * rows, 1)
-    index = jnp.arange(rows, dtype=jnp.int32)
-    index_chip = jnp.concatenate([index + core * rows, index + (1 - core) * rows])
-    index_k = jnp.concatenate([jnp.full((2 * rows,), -1, jnp.int32), index_chip])[None, :]
-    index_q = index_chip[:, None]
-    earlier = (marks_q == marks_k) & (index_k < index_q)
-    allowed = (marks_q == marks_k) & (index_k <= index_q)
-    bias = jnp.where(allowed, jnp.float32(0), jnp.float32(floor_score))
-    offset = jnp.sum(earlier.astype(jnp.int32), axis=1)
+    row = lax.broadcasted_iota(jnp.int32, (rows, rows), 0)
+    column = lax.broadcasted_iota(jnp.int32, (rows, rows), 1)
+    bias, offset = [], []
+    for part in range(2):
+        upper = (core + part) % 2
+        marks_q = lax.dynamic_index_in_dim(near, 2 + upper, 0, keepdims=False)[:, None]
+        third = jnp.where(upper == 0, near[0], near[3])
+        counted = 0
+        for keys, whole in ((near[1], True), (near[2], upper == 1), (third, upper == 0)):
+            same = marks_q == keys[None, :]
+            seen = same & ((column <= row) | whole)
+            bias.append(jnp.where(seen, 0.0, floor_score).astype(jnp.bfloat16))
+            counted += jnp.sum((same & ((column < row) | whole)).astype(jnp.int32), axis=1)
+        offset.append(counted)
+    bias = jnp.stack(
+        [jnp.concatenate(bias[:3], axis=1), jnp.concatenate(bias[3:], axis=1)]
+    )
+    offset = jnp.concatenate(offset)
     token_positions = (prefix_len + offset).astype(jnp.float32)
     half_width = head_dim // 2
     freqs = theta_base ** (-jnp.arange(half_width, dtype=jnp.float32) / half_width)
@@ -429,7 +446,8 @@
     out_mine = lax.dynamic_slice_in_dim(out_strip, core * 1024, 1024, 1)
     out_mine, pieces, under = lax.optimization_barrier((out_mine, pieces, under))
     normed_p, normed_q, cosine, sine, bias, gains = under
-    strips = [out_mine] + [from_tok(out_mine, dx=d) for d in range(1, NX)]
+    strip_3 = from_tok(out_mine, dx=3)
+    strips = [out_mine] + [from_tok(out_mine, dx=d) for d in (1, 2)]
     queries, kv = joint_projection(y[None], normed_p, normed_q, *pieces, cosine, sine, *gains)
     halo = from_previous_chip(kv)
 
@@ -437,8 +455,11 @@
     strips, partial, kv_sent = lax.optimization_barrier((strips, partial, kv))
     strips_other = [from_tok(s, dc=1) for s in strips]
     kv_got = from_tok(kv_sent, dc=1)[:, rows:]
-    mine, others = suffix_attention(queries, kv, halo, partial, bias, scale)
+    mine, others = suffix_attention(core[None], queries, kv, halo, partial, bias, scale)
     got = from_tok(others, dc=1)
+    strip_3, mine = lax.optimization_barrier((strip_3, mine))
+    strips.append(strip_3)
+    strips_other.append(from_tok(strip_3, dc=1))
     projected = output_projection(x, core, mine, got, strips, strips_other)
     cache = in_core_order(core, kv[:, :rows], kv_got, 2)
     return (projected[None], cache[0][None], cache[1][None])

time: 157 us -> 143 us (0.911)
  waiting for transfers between devices: 26.6 us -> 18.9 us
  Pallas kernels: 42.4 us -> 35.4 us
  starting transfers between devices: 32.7 us -> 34.3 us
    ppermute x9, waiting for transfers between devices: 16.1 us -> 12.3 us  [from_grp(): return lax.ppermute(block, 'grp', [((y + dy) % NY, y) for y in range(NY)])]
    ppermute x16, waiting for transfers between devices: 10.4 us -> 6.56 us  [from_tok(): return lax.ppermute(block, 'tok', route)]
    pallas_call x1, Pallas kernels: 12.6 us -> 8.82 us  [prefix_attention(): pl.pallas_call(functools.partial(prefix_kernel, scale), out_shape=(out, o...]
    pallas_call x1, Pallas kernels: 10.5 us -> 7.38 us  [suffix_attention(): pl.pallas_call(functools.partial(suffix_kernel, scale), out_shape=(out, o...]
    ppermute x16, starting transfers between devices: 19.5 us -> 22.2 us  [from_tok(): return lax.ppermute(block, 'tok', route)]
    select_n x2 -> x1, other arithmetic: 1.72 us -> 0.03 us  [per_device(): third = jnp.where(upper == 0, near[0], near[3])]
  transfers between devices with their start and end apart: 28 -> 28, of which waited for: 6 -> 9; matrix products, arithmetic and copies ran while one was open for 8% -> 9% of each run, Pallas kernels for 24% -> 22%
where the time goes in v1:
time: 143 us; the launch traced here: 142 us
  Pallas kernels  35.4 us (25%)
  starting transfers between devices  34.3 us (24%)
  blocking collectives  22.5 us (16%)
  waiting for transfers between devices  18.9 us (13%)
  between operations  15.2 us (11%)
  other arithmetic  8.4 us (6%)
  local copies, waits for them, and re-layouts  6.89 us (5%)
    all_gather x1, blocking collectives, per_device(): both = lax.all_gather(first, 'tok', axis_index_groups=GROUP_ZC)  22.5 us
    ppermute x16, starting transfers between devices, from_tok(): return lax.ppermute(block, 'tok', route)  22.2 us
    ppermute x9, waiting for transfers between devices, from_grp(): return lax.ppermute(block, 'grp', [((y + dy) % NY, y) for y in range(NY)])  12.3 us
    ppermute x9, starting transfers between devices, from_grp(): return lax.ppermute(block, 'grp', [((y + dy) % NY, y) for y in range(NY)])  9.95 us
    pallas_call x1, Pallas kernels, prefix_attention(): pl.pallas_call(functools.partial(prefix_kernel, scale), out_shape=(out, o...  8.82 us
    pallas_call x1, Pallas kernels, joint_projection(): pl.pallas_call(qkv_kernel, out_shape=(out, out), grid_spec=pltpu.Prefetch...  8.25 us
    pallas_call x1, Pallas kernels, suffix_attention(): pl.pallas_call(functools.partial(suffix_kernel, scale), out_shape=(out, o...  7.38 us
    ppermute x16, waiting for transfers between devices, from_tok(): return lax.ppermute(block, 'tok', route)  6.56 us
  transfers between devices with their start and end apart: 28, of which 9 were waited for; matrix products, arithmetic and copies ran while one was open for 9% of the time, Pallas kernels for 22%

profile of v1, /device:TPU:23, one launch (start us, length us, event | category | flops | bytes accessed | tf_op | source)
XLA Modules:
  0.0 141.5 jit_solution(14619498095376073487)
XLA Ops:
  7.2 0.8 collective-permute-start.3
  8.2 2.6 %collective-permute-start.1 = (bf16[32,1024]{1,0:T(8,128)(2,1)}, bf16[32,1024]{1,0:T(8,128)(2,1)S(1)}, u32[]{:S(2)}, u32[]{:S(2)}) collective-permute-start(bf16[32,1024]{1,0:T(8,128)(2,1)} %bitcast.45), channel_id=1, source_target_pairs={{128,0},{192,64},{0,128},{64,192},{129,1},{193,65},{1,129},{65,193... | collective-permute-start | bytes 196616 | tf_op jit(solution)/shard_map/ppermute | solution.py:34
  10.9 0.7 constant_dynamic-slice_fusion.9
  11.6 0.7 add_convert_fusion
  12.3 22.5 %all-gather = bf16[640,512]{1,0:T(8,128)(2,1)S(1)} all-gather(bf16[40,512]{1,0:T(8,128)(2,1)S(1)} %fusion.19), channel_id=2, replica_groups={{0,1,2,3,4,5,6,7,8,9,10,11,12,13,14,15},{16,17,18,19,20,21,22,23,24,25,..., dimensions={0}, use_global_device_ids=true | all-gather | bytes 696320 | tf_op jit(solution)/shard_map/all_gather | solution.py:383
  34.8 1.2 dynamic_slice.39
  37.0 1.9 %collective-permute-start.7 = (bf16[256,256]{1,0:T(8,128)(2,1)S(1)}, bf16[256,256]{1,0:T(8,128)(2,1)S(1)}, u32[]{:S(2)}, u32[]{:S(2)}) collective-permute-start(bf16[256,256]{1,0:T(8,128)(2,1)S(1)} %bitcast.40), channel_id=1, source_target_pairs={{64,0},{128,64},{192,128},{0,192},{65,1},{129,65},{193,129},{1,193... | collective-permute-start | bytes 393224 | tf_op jit(solution)/shard_map/ppermute | solution.py:34
  39.1 0.6 collective-permute-start.4
  39.7 0.8 collective-permute-start.5
  40.5 1.8 %collective-permute-start.6 = (bf16[392,256]{1,0:T(8,128)(2,1)S(1)}, bf16[392,256]{1,0:T(8,128)(2,1)S(1)}, u32[]{:S(2)}, u32[]{:S(2)}) collective-permute-start(bf16[392,256]{1,0:T(8,128)(2,1)S(1)} %constant_dynamic-update-slice_fusion.p0), channel_id=1, source_target_pairs={{48,0},{49,1},{50,2},{51,3},{52,4},{53,5},{54,6},{55,7},{56,8},{57... | collective-permute-start | bytes 602120 | tf_op jit(solution)/shard_map/ppermute | solution.py:30
  42.4 1.4 collective-permute-start.8
  43.8 0.9 collective-permute-start.9
  44.7 3.4 %collective-permute-done.8.q2 = bf16[256,256]{1,0:T(8,128)(2,1)S(1)} collective-permute-done((bf16[256,256]{1,0:T(8,128)(2,1)S(1)}, bf16[256,256]{1,0:T(8,128)(2,1)S(1)}, u32[]{:S(2)}, u32[]{:S(2)}) %collective-permute-start.8) | collective-permute-done | bytes 131104 | tf_op jit(solution)/shard_map/ppermute | solution.py:34
  48.0 3.5 %collective-permute-done.9.q3 = bf16[256,256]{1,0:T(8,128)(2,1)S(1)} collective-permute-done((bf16[256,256]{1,0:T(8,128)(2,1)S(1)}, bf16[256,256]{1,0:T(8,128)(2,1)S(1)}, u32[]{:S(2)}, u32[]{:S(2)}) %collective-permute-start.9) | collective-permute-done | bytes 131104 | tf_op jit(solution)/shard_map/ppermute | solution.py:34
  52.3 0.7 copy-done.11
  53.0 2.5 %pack.1 = (bf16[1024,256]{1,0:T(8,128)(2,1)}, bf16[1024,256]{1,0:T(8,128)(2,1)}, bf16[128,1024]{1,0:T(8,128)(2,1)}) custom-call(bf16[392,256]{1,0:T(8,128)(2,1)} %copy-done.5, bf16[392,256]{1,0:T(8,128)(2,1)} %copy-done.12, bf16[392,256]{1,0:T(8,128)(2,1)} %copy-done.13, bf16[392,256]{1,0:T(8,128)(2,1)} %copy-done.11, bf16[256,256]{1,0:T(8,128)(2,1)} %bitcast.43, ...), custom_call_target="tpu_custom_call" | custom-call | tf_op jit(solution)/shard_map/pack/pallas_call | solution.py:342
  55.7 0.9 collective-permute-start.11
  56.7 2.0 %collective-permute-start.12 = (bf16[1024,256]{1,0:T(8,128)(2,1)}, bf16[1024,256]{1,0:T(8,128)(2,1)S(1)}, u32[]{:S(2)}, u32[]{:S(2)}) collective-permute-start(bf16[1024,256]{1,0:T(8,128)(2,1)} %get-tuple-element.85.p0), channel_id=1, source_target_pairs={{192,0},{0,64},{64,128},{128,192},{193,1},{1,65},{65,129},{129,193... | collective-permute-start | bytes 1572872 | tf_op jit(solution)/shard_map/ppermute | solution.py:34
  58.6 1.0 collective-permute-start.13
  59.6 3.1 %collective-permute-start.14 = (bf16[1024,256]{1,0:T(8,128)(2,1)}, bf16[1024,256]{1,0:T(8,128)(2,1)}, u32[]{:S(2)}, u32[]{:S(2)}) collective-permute-start(bf16[1024,256]{1,0:T(8,128)(2,1)} %get-tuple-element.89.q0), channel_id=1, source_target_pairs={{32,0},{33,1},{34,2},{35,3},{36,4},{37,5},{38,6},{39,7},{40,8},{41... | collective-permute-start | bytes 1572872 | tf_op jit(solution)/shard_map/ppermute | solution.py:30
  62.6 0.7 broadcast_select_fusion.4
  63.8 1.0 fusion.13
  65.1 3.4 %collective-permute-done.10.p1 = bf16[1024,256]{1,0:T(8,128)(2,1)S(1)} collective-permute-done((bf16[1024,256]{1,0:T(8,128)(2,1)}, bf16[1024,256]{1,0:T(8,128)(2,1)S(1)}, u32[]{:S(2)}, u32[]{:S(2)}) %collective-permute-start.10) | collective-permute-done | bytes 524320 | tf_op jit(solution)/shard_map/ppermute | solution.py:34
  68.5 2.8 %collective-permute-start.15 = (bf16[1024,256]{1,0:T(8,128)(2,1)}, bf16[1024,256]{1,0:T(8,128)(2,1)}, u32[]{:S(2)}, u32[]{:S(2)}) collective-permute-start(bf16[1024,256]{1,0:T(8,128)(2,1)} %get-tuple-element.89.q0), channel_id=1, source_target_pairs={{48,0},{49,1},{50,2},{51,3},{52,4},{53,5},{54,6},{55,7},{56,8},{57... | collective-permute-start | bytes 1572872 | tf_op jit(solution)/shard_map/ppermute | solution.py:30
  71.3 0.8 pad_maximum_fusion.2.cos_ref
  72.2 0.9 pad_maximum_fusion.3.sin_ref
  73.1 1.0 pad_maximum_fusion.bias_ref
  74.1 0.6 broadcast_in_dim.46.gain_ref
  74.7 4.0 %input_norm.1 = (bf16[512,1024]{1,0:T(8,128)(2,1)}, bf16[512,1024]{1,0:T(8,128)(2,1)}) custom-call(s32[1]{0:T(128)} %bitcast.x_ref, bf16[256,2048]{1,0:T(8,128)(2,1)} %bitcast.37, bf16[256,2048]{1,0:T(8,128)(2,1)} %copy-done.4, bf16[1,2048]{1,0:T(2,128)(2,1)} %broadcast_in_dim.46.gain_ref), custom_call_target="tpu_custom_call" | custom-call | tf_op jit(solution)/shard_map/input_norm/pallas_call | solution.py:68
  78.7 1.1 constant_dynamic-slice_fusion.10.refs_0_
  79.8 2.0 %collective-permute-done.12.p3 = bf16[1024,256]{1,0:T(8,128)(2,1)S(1)} collective-permute-done((bf16[1024,256]{1,0:T(8,128)(2,1)}, bf16[1024,256]{1,0:T(8,128)(2,1)S(1)}, u32[]{:S(2)}, u32[]{:S(2)}) %collective-permute-start.12) | collective-permute-done | bytes 524320 | tf_op jit(solution)/shard_map/ppermute | solution.py:34
  81.9 2.9 %collective-permute-done.14.q2 = bf16[1024,256]{1,0:T(8,128)(2,1)} collective-permute-done((bf16[1024,256]{1,0:T(8,128)(2,1)}, bf16[1024,256]{1,0:T(8,128)(2,1)}, u32[]{:S(2)}, u32[]{:S(2)}) %collective-permute-start.14) | collective-permute-done | bytes 524320 | tf_op jit(solution)/shard_map/ppermute | solution.py:30
  84.8 1.4 %collective-permute-start.18 = (bf16[256,1024]{1,0:T(8,128)(2,1)S(1)}, bf16[256,1024]{1,0:T(8,128)(2,1)S(1)}, u32[]{:S(2)}, u32[]{:S(2)}) collective-permute-start(bf16[256,1024]{1,0:T(8,128)(2,1)S(1)} %constant_dynamic-slice_fusion.10.refs_0_), channel_id=1, source_target_pairs={{16,0},{17,1},{18,2},{19,3},{20,4},{21,5},{22,6},{23,7},{24,8},{25... | collective-permute-start | bytes 1572872 | tf_op jit(solution)/shard_map/ppermute | solution.py:30
  86.2 2.8 %collective-permute-start.19 = (bf16[256,1024]{1,0:T(8,128)(2,1)S(1)}, bf16[256,1024]{1,0:T(8,128)(2,1)S(1)}, u32[]{:S(2)}, u32[]{:S(2)}) collective-permute-start(bf16[256,1024]{1,0:T(8,128)(2,1)S(1)} %constant_dynamic-slice_fusion.10.refs_0_), channel_id=1, source_target_pairs={{32,0},{33,1},{34,2},{35,3},{36,4},{37,5},{38,6},{39,7},{40,8},{41... | collective-permute-start | bytes 1572872 | tf_op jit(solution)/shard_map/ppermute | solution.py:30
  89.0 8.3 %joint_projection.1 = (bf16[2,512,256]{2,1,0:T(8,128)(2,1)}, bf16[2,512,256]{2,1,0:T(8,128)(2,1)}) custom-call(s32[1]{0:T(128)} %bitcast.24.y_ref, bf16[512,1024]{1,0:T(8,128)(2,1)} %get-tuple-element.83.np_ref, bf16[512,1024]{1,0:T(8,128)(2,1)} %get-tuple-element.84.nq_ref, bf16[1024,256]{1,0:T(8,128)(2,1)} %get-tuple-element.85.p0, ...), custom_call_target="tpu_custom_call" | custom-call | flops 2147483648 | bytes 8388608 | tf_op jit(solution)/shard_map/joint_projection/pallas_call | solution.py:137
  97.2 2.0 %collective-permute-start.17 = (bf16[2,512,256]{2,1,0:T(8,128)(2,1)}, bf16[2,512,256]{2,1,0:T(8,128)(2,1)S(1)}, u32[]{:S(2)}, u32[]{:S(2)}) collective-permute-start(bf16[2,512,256]{2,1,0:T(8,128)(2,1)} %get-tuple-element.112.ko_ref.vo_ref), channel_id=1, source_target_pairs={{0,2},{1,3},{2,4},{3,5},{4,6},{5,7},{6,8},{7,9},{8,10},{9,11},{10,... | collective-permute-start | bytes 1572872 | tf_op jit(solution)/shard_map/ppermute | solution.py:40
  99.3 1.0 collective-permute-start.16
  100.3 8.8 %prefix_attention.1 = (f32[4,512,128]{2,1,0:T(8,128)}, f32[4,512,128]{2,1,0:T(8,128)}) custom-call(s32[1]{0:T(128)} %bitcast.1.core_ref, bf16[2,512,256]{2,1,0:T(8,128)(2,1)} %get-tuple-element.97.q_ref, bf16[2048,1024]{1,0:T(8,128)(2,1)} %all-gather.6.cloned.1.call-done.k_ref.v_ref, bf16[2048,1024]{1,0:T(8,128)(2,1)} %all-gather.6.cloned.1.call-done.k_ref.v_ref), custom_call_target="tpu_custom_call" | custom-call | flops 2147483648 | bytes 4194304 | tf_op jit(solution)/shard_map/prefix_attention/pallas_call | solution.py:206
  109.2 1.2 collective-permute-done.19.refs_2_
  110.4 2.7 %collective-permute-start.25 = (bf16[2,512,256]{2,1,0:T(8,128)(2,1)S(1)}, bf16[2,512,256]{2,1,0:T(8,128)(2,1)}, u32[]{:S(2)}, u32[]{:S(2)}) collective-permute-start(bf16[2,512,256]{2,1,0:T(8,128)(2,1)S(1)} %copy-done), channel_id=1, source_target_pairs={{1,0},{0,1},{3,2},{2,3},{5,4},{4,5},{7,6},{6,7},{9,8},{8,9},{11,10... | collective-permute-start | bytes 1572872 | tf_op jit(solution)/shard_map/ppermute | solution.py:30
  113.1 0.8 copy-done.3
  113.9 7.4 %suffix_attention.1 = (bf16[256,512]{1,0:T(8,128)(2,1)}, bf16[256,512]{1,0:T(8,128)(2,1)}) custom-call(s32[1]{0:T(128)} %bitcast.1.core_ref, bf16[2,512,256]{2,1,0:T(8,128)(2,1)} %get-tuple-element.97.q_ref, bf16[2,512,256]{2,1,0:T(8,128)(2,1)} %get-tuple-element.112.ko_ref.vo_ref, bf16[2,512,256]{2,1,0:T(8,128)(2,1)} %get-tuple-element.112.ko_ref.vo_ref, ...), custom_call_target="tpu_custom_call" | custom-call | flops 805306368 | bytes 4194304 | tf_op jit(solution)/shard_map/suffix_attention/pallas_call | solution.py:268
  121.3 1.6 %collective-permute-done.16.refs_3_ = bf16[256,1024]{1,0:T(8,128)(2,1)} collective-permute-done((bf16[256,1024]{1,0:T(8,128)(2,1)S(1)}, bf16[256,1024]{1,0:T(8,128)(2,1)}, u32[]{:S(2)}, u32[]{:S(2)}) %collective-permute-start.16) | collective-permute-done | bytes 524320 | tf_op jit(solution)/shard_map/ppermute | solution.py:30
  122.8 2.4 %collective-permute-start.24 = (bf16[256,1024]{1,0:T(8,128)(2,1)}, bf16[256,1024]{1,0:T(8,128)(2,1)S(1)}, u32[]{:S(2)}, u32[]{:S(2)}) collective-permute-start(bf16[256,1024]{1,0:T(8,128)(2,1)} %collective-permute-done.16.refs_3_), channel_id=1, source_target_pairs={{1,0},{0,1},{3,2},{2,3},{5,4},{4,5},{7,6},{6,7},{9,8},{8,9},{11,10... | collective-permute-start | bytes 1572872 | tf_op jit(solution)/shard_map/ppermute | solution.py:30
  125.8 0.6 pad_add_fusion.place_ref
  126.9 1.0 broadcast_select_fusion
  127.9 0.8 pad_maximum_fusion.1
  130.1 4.6 %output_projection.1 = bf16[256,2048]{1,0:T(8,128)(2,1)} custom-call(s32[2]{0:T(128)} %pad_add_fusion.place_ref, bf16[256,512]{1,0:T(8,128)(2,1)} %get-tuple-element.106.mine_ref, bf16[256,512]{1,0:T(8,128)(2,1)} %copy-done.10, bf16[256,1024]{1,0:T(8,128)(2,1)} %copy-done.2, bf16[256,1024]{1,0:T(8,128)(2,1)} %copy-done.6, bf16[256,1024]{1,0:T(8,128)(2,1)} %copy-done.7, ...), custom_call_target="tpu_custom_call" | custom-call | flops 1073741824 | bytes 6291456 | tf_op jit(solution)/shard_map/output_projection/pallas_call | solution.py:315
  (96 shorter events, 4.9 us)
Async XLA Ops:
  7.2 71.5 %all-gather.4.cloned.1.call-start = ((), (), s32[]{:S(2)}) async-start(), calls=%async_computation | async-start | bytes 1114112 | tf_op jit(solution)/shard_map/all_gather | solution.py:367
  7.2 29.5 %collective-permute-start.3 = (bf16[256,2048]{1,0:T(8,128)(2,1)}, bf16[256,2048]{1,0:T(8,128)(2,1)S(1)}, u32[]{:S(2)}, u32[]{:S(2)}) collective-permute-start(bf16[256,2048]{1,0:T(8,128)(2,1)} %bitcast.36), channel_id=1, source_target_pairs={{1,0},{0,1},{3,2},{2,3},{5,4},{4,5},{7,6},{6,7},{9,8},{8,9},{11,10... | collective-permute-start | bytes 3145736 | tf_op jit(solution)/shard_map/ppermute | solution.py:30
  8.0 28.7 %collective-permute-start = (bf16[32,1024]{1,0:T(8,128)(2,1)}, bf16[32,1024]{1,0:T(8,128)(2,1)S(1)}, u32[]{:S(2)}, u32[]{:S(2)}) collective-permute-start(bf16[32,1024]{1,0:T(8,128)(2,1)} %bitcast.44), channel_id=1, source_target_pairs={{64,0},{128,64},{192,128},{0,192},{65,1},{129,65},{193,129},{1,193... | collective-permute-start | bytes 196616 | tf_op jit(solution)/shard_map/ppermute | solution.py:34
  8.2 28.5 %collective-permute-start.1 = (bf16[32,1024]{1,0:T(8,128)(2,1)}, bf16[32,1024]{1,0:T(8,128)(2,1)S(1)}, u32[]{:S(2)}, u32[]{:S(2)}) collective-permute-start(bf16[32,1024]{1,0:T(8,128)(2,1)} %bitcast.45), channel_id=1, source_target_pairs={{128,0},{192,64},{0,128},{64,192},{129,1},{193,65},{1,129},{65,193... | collective-permute-start | bytes 196616 | tf_op jit(solution)/shard_map/ppermute | solution.py:34
  10.8 25.9 %collective-permute-start.2 = (bf16[32,1024]{1,0:T(8,128)(2,1)}, bf16[32,1024]{1,0:T(8,128)(2,1)S(1)}, u32[]{:S(2)}, u32[]{:S(2)}) collective-permute-start(bf16[32,1024]{1,0:T(8,128)(2,1)} %bitcast.46), channel_id=1, source_target_pairs={{192,0},{0,64},{64,128},{128,192},{193,1},{1,65},{65,129},{129,193... | collective-permute-start | bytes 196616 | tf_op jit(solution)/shard_map/ppermute | solution.py:34
  10.8 89.5 %all-gather.6.cloned.1.call-start = ((), (), s32[]{:S(2)}) async-start(), calls=%async_computation.1 | async-start | bytes 4456448 | tf_op jit(solution)/shard_map/all_gather | solution.py:408
  36.7 36.3 %copy-start.4 = (bf16[256,2048]{1,0:T(8,128)(2,1)}, bf16[256,2048]{1,0:T(8,128)(2,1)S(1)}, u32[]{:S(2)}) copy-start(bf16[256,2048]{1,0:T(8,128)(2,1)S(1)} %collective-permute-done.3.peer_ref) | copy-start | bytes 3145732
  37.0 14.5 %copy-start.9 = (bf16[8,32,256]{2,1,0:T(8,128)(2,1)}, bf16[8,32,256]{2,1,0:T(8,128)(2,1)S(1)}, u32[]{:S(2)}) copy-start(bf16[8,32,256]{2,1,0:T(8,128)(2,1)S(1)} %get-tuple-element.123) | copy-start | bytes 393220
  37.0 6.7 %collective-permute-start.7 = (bf16[256,256]{1,0:T(8,128)(2,1)S(1)}, bf16[256,256]{1,0:T(8,128)(2,1)S(1)}, u32[]{:S(2)}, u32[]{:S(2)}) collective-permute-start(bf16[256,256]{1,0:T(8,128)(2,1)S(1)} %bitcast.40), channel_id=1, source_target_pairs={{64,0},{128,64},{192,128},{0,192},{65,1},{129,65},{193,129},{1,193... | collective-permute-start | bytes 393224 | tf_op jit(solution)/shard_map/ppermute | solution.py:34
  39.0 35.1 %copy-start.17 = (bf16[2048]{0:T(1024)(128)(2,1)S(1)}, bf16[2048]{0:T(1024)(128)(2,1)}, u32[]{:S(2)}) copy-start(bf16[2048]{0:T(1024)(128)(2,1)} %param.13) | copy-start | bytes 12292
  39.1 12.5 %copy-start.5 = (bf16[392,256]{1,0:T(8,128)(2,1)}, bf16[392,256]{1,0:T(8,128)(2,1)S(1)}, u32[]{:S(2)}) copy-start(bf16[392,256]{1,0:T(8,128)(2,1)S(1)} %constant_dynamic-update-slice_fusion.p0) | copy-start | bytes 602116
  39.1 12.4 %collective-permute-start.4 = (bf16[392,256]{1,0:T(8,128)(2,1)S(1)}, bf16[392,256]{1,0:T(8,128)(2,1)S(1)}, u32[]{:S(2)}, u32[]{:S(2)}) collective-permute-start(bf16[392,256]{1,0:T(8,128)(2,1)S(1)} %constant_dynamic-update-slice_fusion.p0), channel_id=1, source_target_pairs={{16,0},{17,1},{18,2},{19,3},{20,4},{21,5},{22,6},{23,7},{24,8},{25... | collective-permute-start | bytes 602120 | tf_op jit(solution)/shard_map/ppermute | solution.py:30
  39.7 11.8 %collective-permute-start.5 = (bf16[392,256]{1,0:T(8,128)(2,1)S(1)}, bf16[392,256]{1,0:T(8,128)(2,1)S(1)}, u32[]{:S(2)}, u32[]{:S(2)}) collective-permute-start(bf16[392,256]{1,0:T(8,128)(2,1)S(1)} %constant_dynamic-update-slice_fusion.p0), channel_id=1, source_target_pairs={{32,0},{33,1},{34,2},{35,3},{36,4},{37,5},{38,6},{39,7},{40,8},{41... | collective-permute-start | bytes 602120 | tf_op jit(solution)/shard_map/ppermute | solution.py:30
  40.5 11.0 %collective-permute-start.6 = (bf16[392,256]{1,0:T(8,128)(2,1)S(1)}, bf16[392,256]{1,0:T(8,128)(2,1)S(1)}, u32[]{:S(2)}, u32[]{:S(2)}) collective-permute-start(bf16[392,256]{1,0:T(8,128)(2,1)S(1)} %constant_dynamic-update-slice_fusion.p0), channel_id=1, source_target_pairs={{48,0},{49,1},{50,2},{51,3},{52,4},{53,5},{54,6},{55,7},{56,8},{57... | collective-permute-start | bytes 602120 | tf_op jit(solution)/shard_map/ppermute | solution.py:30
  42.4 5.7 %collective-permute-start.8 = (bf16[256,256]{1,0:T(8,128)(2,1)S(1)}, bf16[256,256]{1,0:T(8,128)(2,1)S(1)}, u32[]{:S(2)}, u32[]{:S(2)}) collective-permute-start(bf16[256,256]{1,0:T(8,128)(2,1)S(1)} %bitcast.41), channel_id=1, source_target_pairs={{128,0},{192,64},{0,128},{64,192},{129,1},{193,65},{1,129},{65,193... | collective-permute-start | bytes 393224 | tf_op jit(solution)/shard_map/ppermute | solution.py:34
  43.8 7.8 %copy-start.14 = (bf16[256,256]{1,0:T(8,128)(2,1)}, bf16[256,256]{1,0:T(8,128)(2,1)S(1)}, u32[]{:S(2)}) copy-start(bf16[256,256]{1,0:T(8,128)(2,1)S(1)} %collective-permute-done.7.q1) | copy-start | bytes 393220
  43.8 7.8 %collective-permute-start.9 = (bf16[256,256]{1,0:T(8,128)(2,1)S(1)}, bf16[256,256]{1,0:T(8,128)(2,1)S(1)}, u32[]{:S(2)}, u32[]{:S(2)}) collective-permute-start(bf16[256,256]{1,0:T(8,128)(2,1)S(1)} %bitcast.42), channel_id=1, source_target_pairs={{192,0},{0,64},{64,128},{128,192},{193,1},{1,65},{65,129},{129,193... | collective-permute-start | bytes 393224 | tf_op jit(solution)/shard_map/ppermute | solution.py:34
  48.0 3.5 %copy-start.15 = (bf16[256,256]{1,0:T(8,128)(2,1)}, bf16[256,256]{1,0:T(8,128)(2,1)S(1)}, u32[]{:S(2)}) copy-start(bf16[256,256]{1,0:T(8,128)(2,1)S(1)} %collective-permute-done.8.q2) | copy-start | bytes 393220
  51.5 0.7 copy-start.12
  51.5 0.8 copy-start.13
  52.3 0.7 copy-start.11
  55.6 12.9 %collective-permute-start.10 = (bf16[1024,256]{1,0:T(8,128)(2,1)}, bf16[1024,256]{1,0:T(8,128)(2,1)S(1)}, u32[]{:S(2)}, u32[]{:S(2)}) collective-permute-start(bf16[1024,256]{1,0:T(8,128)(2,1)} %get-tuple-element.85.p0), channel_id=1, source_target_pairs={{64,0},{128,64},{192,128},{0,192},{65,1},{129,65},{193,129},{1,193... | collective-permute-start | bytes 1572872 | tf_op jit(solution)/shard_map/ppermute | solution.py:34
  55.7 24.1 %collective-permute-start.11 = (bf16[1024,256]{1,0:T(8,128)(2,1)}, bf16[1024,256]{1,0:T(8,128)(2,1)S(1)}, u32[]{:S(2)}, u32[]{:S(2)}) collective-permute-start(bf16[1024,256]{1,0:T(8,128)(2,1)} %get-tuple-element.85.p0), channel_id=1, source_target_pairs={{128,0},{192,64},{0,128},{64,192},{129,1},{193,65},{1,129},{65,193... | collective-permute-start | bytes 1572872 | tf_op jit(solution)/shard_map/ppermute | solution.py:34
  56.7 25.2 %collective-permute-start.12 = (bf16[1024,256]{1,0:T(8,128)(2,1)}, bf16[1024,256]{1,0:T(8,128)(2,1)S(1)}, u32[]{:S(2)}, u32[]{:S(2)}) collective-permute-start(bf16[1024,256]{1,0:T(8,128)(2,1)} %get-tuple-element.85.p0), channel_id=1, source_target_pairs={{192,0},{0,64},{64,128},{128,192},{193,1},{1,65},{65,129},{129,193... | collective-permute-start | bytes 1572872 | tf_op jit(solution)/shard_map/ppermute | solution.py:34
  58.6 23.3 %collective-permute-start.13 = (bf16[1024,256]{1,0:T(8,128)(2,1)}, bf16[1024,256]{1,0:T(8,128)(2,1)S(1)}, u32[]{:S(2)}, u32[]{:S(2)}) collective-permute-start(bf16[1024,256]{1,0:T(8,128)(2,1)} %get-tuple-element.89.q0), channel_id=1, source_target_pairs={{16,0},{17,1},{18,2},{19,3},{20,4},{21,5},{22,6},{23,7},{24,8},{25... | collective-permute-start | bytes 1572872 | tf_op jit(solution)/shard_map/ppermute | solution.py:30
  59.6 25.2 %collective-permute-start.14 = (bf16[1024,256]{1,0:T(8,128)(2,1)}, bf16[1024,256]{1,0:T(8,128)(2,1)}, u32[]{:S(2)}, u32[]{:S(2)}) collective-permute-start(bf16[1024,256]{1,0:T(8,128)(2,1)} %get-tuple-element.89.q0), channel_id=1, source_target_pairs={{32,0},{33,1},{34,2},{35,3},{36,4},{37,5},{38,6},{39,7},{40,8},{41... | collective-permute-start | bytes 1572872 | tf_op jit(solution)/shard_map/ppermute | solution.py:30
  68.5 20.5 %copy-start.18 = (bf16[1024,256]{1,0:T(8,128)(2,1)}, bf16[1024,256]{1,0:T(8,128)(2,1)S(1)}, u32[]{:S(2)}) copy-start(bf16[1024,256]{1,0:T(8,128)(2,1)S(1)} %collective-permute-done.10.p1) | copy-start | bytes 1572868
  68.5 16.3 %collective-permute-start.15 = (bf16[1024,256]{1,0:T(8,128)(2,1)}, bf16[1024,256]{1,0:T(8,128)(2,1)}, u32[]{:S(2)}, u32[]{:S(2)}) collective-permute-start(bf16[1024,256]{1,0:T(8,128)(2,1)} %get-tuple-element.89.q0), channel_id=1, source_target_pairs={{48,0},{49,1},{50,2},{51,3},{52,4},{53,5},{54,6},{55,7},{56,8},{57... | collective-permute-start | bytes 1572872 | tf_op jit(solution)/shard_map/ppermute | solution.py:30
  79.8 45.5 %copy-start.2 = (bf16[256,1024]{1,0:T(8,128)(2,1)}, bf16[256,1024]{1,0:T(8,128)(2,1)S(1)}, u32[]{:S(2)}) copy-start(bf16[256,1024]{1,0:T(8,128)(2,1)S(1)} %constant_dynamic-slice_fusion.10.refs_0_) | copy-start | bytes 1572868
  79.8 9.2 %copy-start.19 = (bf16[1024,256]{1,0:T(8,128)(2,1)}, bf16[1024,256]{1,0:T(8,128)(2,1)S(1)}, u32[]{:S(2)}) copy-start(bf16[1024,256]{1,0:T(8,128)(2,1)S(1)} %collective-permute-done.11.p2) | copy-start | bytes 1572868
  81.9 7.1 %copy-start.20 = (bf16[1024,256]{1,0:T(8,128)(2,1)}, bf16[1024,256]{1,0:T(8,128)(2,1)S(1)}, u32[]{:S(2)}) copy-start(bf16[1024,256]{1,0:T(8,128)(2,1)S(1)} %collective-permute-done.12.p3) | copy-start | bytes 1572868
  81.9 2.9 %copy-start.21 = (bf16[1024,256]{1,0:T(8,128)(2,1)}, bf16[1024,256]{1,0:T(8,128)(2,1)S(1)}, u32[]{:S(2)}) copy-start(bf16[1024,256]{1,0:T(8,128)(2,1)S(1)} %collective-permute-done.13.q1) | copy-start | bytes 1572868
  84.8 24.3 %collective-permute-start.18 = (bf16[256,1024]{1,0:T(8,128)(2,1)S(1)}, bf16[256,1024]{1,0:T(8,128)(2,1)S(1)}, u32[]{:S(2)}, u32[]{:S(2)}) collective-permute-start(bf16[256,1024]{1,0:T(8,128)(2,1)S(1)} %constant_dynamic-slice_fusion.10.refs_0_), channel_id=1, source_target_pairs={{16,0},{17,1},{18,2},{19,3},{20,4},{21,5},{22,6},{23,7},{24,8},{25... | collective-permute-start | bytes 1572872 | tf_op jit(solution)/shard_map/ppermute | solution.py:30
  86.2 24.2 %collective-permute-start.19 = (bf16[256,1024]{1,0:T(8,128)(2,1)S(1)}, bf16[256,1024]{1,0:T(8,128)(2,1)S(1)}, u32[]{:S(2)}, u32[]{:S(2)}) collective-permute-start(bf16[256,1024]{1,0:T(8,128)(2,1)S(1)} %constant_dynamic-slice_fusion.10.refs_0_), channel_id=1, source_target_pairs={{32,0},{33,1},{34,2},{35,3},{36,4},{37,5},{38,6},{39,7},{40,8},{41... | collective-permute-start | bytes 1572872 | tf_op jit(solution)/shard_map/ppermute | solution.py:30
  97.2 15.9 %collective-permute-start.17 = (bf16[2,512,256]{2,1,0:T(8,128)(2,1)}, bf16[2,512,256]{2,1,0:T(8,128)(2,1)S(1)}, u32[]{:S(2)}, u32[]{:S(2)}) collective-permute-start(bf16[2,512,256]{2,1,0:T(8,128)(2,1)} %get-tuple-element.112.ko_ref.vo_ref), channel_id=1, source_target_pairs={{0,2},{1,3},{2,4},{3,5},{4,6},{5,7},{6,8},{7,9},{8,10},{9,11},{10,... | collective-permute-start | bytes 1572872 | tf_op jit(solution)/shard_map/ppermute | solution.py:40
  99.3 23.6 %collective-permute-start.16 = (bf16[256,1024]{1,0:T(8,128)(2,1)S(1)}, bf16[256,1024]{1,0:T(8,128)(2,1)}, u32[]{:S(2)}, u32[]{:S(2)}) collective-permute-start(bf16[256,1024]{1,0:T(8,128)(2,1)S(1)} %constant_dynamic-slice_fusion.10.refs_0_), channel_id=1, source_target_pairs={{48,0},{49,1},{50,2},{51,3},{52,4},{53,5},{54,6},{55,7},{56,8},{57... | collective-permute-start | bytes 1572872 | tf_op jit(solution)/shard_map/ppermute | solution.py:30
  100.3 10.1 %copy-start = (bf16[2,512,256]{2,1,0:T(8,128)(2,1)S(1)}, bf16[2,512,256]{2,1,0:T(8,128)(2,1)}, u32[]{:S(2)}) copy-start(bf16[2,512,256]{2,1,0:T(8,128)(2,1)} %get-tuple-element.112.ko_ref.vo_ref) | copy-start | bytes 1572868
  109.2 17.7 %copy-start.1 = (bf16[2,512,256]{2,1,0:T(8,128)(2,1)S(1)}, bf16[2,512,256]{2,1,0:T(8,128)(2,1)}, u32[]{:S(2)}) copy-start(bf16[2,512,256]{2,1,0:T(8,128)(2,1)} %get-tuple-element.112.ko_ref.vo_ref) | copy-start | bytes 1572868
  109.2 20.4 %copy-start.6 = (bf16[256,1024]{1,0:T(8,128)(2,1)}, bf16[256,1024]{1,0:T(8,128)(2,1)S(1)}, u32[]{:S(2)}) copy-start(bf16[256,1024]{1,0:T(8,128)(2,1)S(1)} %collective-permute-done.18.refs_1_) | copy-start | bytes 1572868
  110.4 19.2 %copy-start.7 = (bf16[256,1024]{1,0:T(8,128)(2,1)}, bf16[256,1024]{1,0:T(8,128)(2,1)S(1)}, u32[]{:S(2)}) copy-start(bf16[256,1024]{1,0:T(8,128)(2,1)S(1)} %collective-permute-done.19.refs_2_) | copy-start | bytes 1572868
  110.4 16.0 %collective-permute-start.25 = (bf16[2,512,256]{2,1,0:T(8,128)(2,1)S(1)}, bf16[2,512,256]{2,1,0:T(8,128)(2,1)}, u32[]{:S(2)}, u32[]{:S(2)}) collective-permute-start(bf16[2,512,256]{2,1,0:T(8,128)(2,1)S(1)} %copy-done), channel_id=1, source_target_pairs={{1,0},{0,1},{3,2},{2,3},{5,4},{4,5},{7,6},{6,7},{9,8},{8,9},{11,10... | collective-permute-start | bytes 1572872 | tf_op jit(solution)/shard_map/ppermute | solution.py:30
  113.1 0.8 copy-start.3
  122.8 6.4 %collective-permute-start.24 = (bf16[256,1024]{1,0:T(8,128)(2,1)}, bf16[256,1024]{1,0:T(8,128)(2,1)S(1)}, u32[]{:S(2)}, u32[]{:S(2)}) collective-permute-start(bf16[256,1024]{1,0:T(8,128)(2,1)} %collective-permute-done.16.refs_3_), channel_id=1, source_target_pairs={{1,0},{0,1},{3,2},{2,3},{5,4},{4,5},{7,6},{6,7},{9,8},{8,9},{11,10... | collective-permute-start | bytes 1572872 | tf_op jit(solution)/shard_map/ppermute | solution.py:30
  125.3 4.0 %collective-permute-start.21 = (bf16[256,1024]{1,0:T(8,128)(2,1)S(1)}, bf16[256,1024]{1,0:T(8,128)(2,1)}, u32[]{:S(2)}, u32[]{:S(2)}) collective-permute-start(bf16[256,1024]{1,0:T(8,128)(2,1)S(1)} %constant_dynamic-slice_fusion.10.refs_0_), channel_id=1, source_target_pairs={{1,0},{0,1},{3,2},{2,3},{5,4},{4,5},{7,6},{6,7},{9,8},{8,9},{11,10... | collective-permute-start | bytes 1572872 | tf_op jit(solution)/shard_map/ppermute | solution.py:30
  125.3 4.0 %collective-permute-start.22 = (bf16[256,1024]{1,0:T(8,128)(2,1)S(1)}, bf16[256,1024]{1,0:T(8,128)(2,1)}, u32[]{:S(2)}, u32[]{:S(2)}) collective-permute-start(bf16[256,1024]{1,0:T(8,128)(2,1)S(1)} %collective-permute-done.18.refs_1_), channel_id=1, source_target_pairs={{1,0},{0,1},{3,2},{2,3},{5,4},{4,5},{7,6},{6,7},{9,8},{8,9},{11,10... | collective-permute-start | bytes 1572872 | tf_op jit(solution)/shard_map/ppermute | solution.py:30
  125.8 3.8 %collective-permute-start.23 = (bf16[256,1024]{1,0:T(8,128)(2,1)S(1)}, bf16[256,1024]{1,0:T(8,128)(2,1)}, u32[]{:S(2)}, u32[]{:S(2)}) collective-permute-start(bf16[256,1024]{1,0:T(8,128)(2,1)S(1)} %collective-permute-done.19.refs_2_), channel_id=1, source_target_pairs={{1,0},{0,1},{3,2},{2,3},{5,4},{4,5},{7,6},{6,7},{9,8},{8,9},{11,10... | collective-permute-start | bytes 1572872 | tf_op jit(solution)/shard_map/ppermute | solution.py:30
  126.4 2.9 %collective-permute-start.20 = (bf16[256,512]{1,0:T(8,128)(2,1)}, bf16[256,512]{1,0:T(8,128)(2,1)S(1)}, u32[]{:S(2)}, u32[]{:S(2)}) collective-permute-start(bf16[256,512]{1,0:T(8,128)(2,1)} %get-tuple-element.107), channel_id=1, source_target_pairs={{1,0},{0,1},{3,2},{2,3},{5,4},{4,5},{7,6},{6,7},{9,8},{8,9},{11,10... | collective-permute-start | bytes 786440 | tf_op jit(solution)/shard_map/ppermute | solution.py:30
  129.3 0.9 copy-start.8
  (2 other events, 1.4 us)
Sparse Core Ops, SparseCore 0:
  10.9 42.0 all-gather.3
  55.6 40.9 all-gather.5

commit v2 on v1

--- a/solution.py
+++ b/solution.py
@@ -326,29 +326,6 @@
     )(jnp.stack([x, core]), *args)
 
 
-def pack_kernel(p0, p1, p2, p3, q0, q1, q2, q3, p_ref, q_ref, prefix_ref):
-    for k, (p, q) in enumerate(((p0, q0), (p1, q1), (p2, q2), (p3, q3))):
-        p_ref[k * 256 : (k + 1) * 256, :] = p[:256, :]
-        q_ref[k * 256 : (k + 1) * 256, :] = q[...]
-        for i in range(4):
-            prefix_ref[k * 32 : (k + 1) * 32, i * 256 : (i + 1) * 256] = p[
-                256 + 32 * i : 288 + 32 * i, :
-            ]
-
-
-def pack(p_all, q_all):
-    vmem = pl.BlockSpec(memory_space=pltpu.VMEM)
-    strip = jax.ShapeDtypeStruct((1024, 256), jnp.bfloat16)
-    return pl.pallas_call(
-        pack_kernel,
-        out_shape=(strip, strip, jax.ShapeDtypeStruct((128, 1024), jnp.bfloat16)),
-        in_specs=[vmem] * 8,
-        out_specs=(vmem, vmem, vmem),
-        compiler_params=pltpu.CompilerParams(vmem_limit_bytes=VMEM_LIMIT),
-        name="pack",
-    )(*p_all, *q_all)
-
-
 GROUP_ZC = [[place(x, z, c) for z in range(NZ) for c in range(NC)] for x in range(NX)]
 
 
@@ -394,13 +371,20 @@
         + [prefix_rows[:, i * 256 : (i + 1) * 256] for i in range(4)]
         + [jnp.pad(marks_x[14:], ((0, 6), (0, 0)))]
     )
-    q_own = strip[256:]
+    q_own = jnp.concatenate([strip[256:], jnp.zeros((8, 256), jnp.bfloat16)])
     p_all = [p_own] + [from_tok(p_own, dx=d) for d in (2, 1, 3)]
     p_all = [p_all[0], p_all[2], p_all[1], p_all[3]]
     q_all = [q_own] + [from_grp(q_own, d) for d in range(1, NY)]
     p_all, q_all = lax.optimization_barrier((p_all, q_all))
 
-    p0, q0, prefix_part = pack(p_all, q_all)
+    p0 = jnp.concatenate([p[:256] for p in p_all])
+    q0 = jnp.concatenate([q[:256] for q in q_all])
+    prefix_part = jnp.concatenate(
+        [
+            jnp.concatenate([p[256 + 32 * i : 288 + 32 * i] for i in range(4)], axis=1)
+            for p in p_all
+        ]
+    )
     p2 = from_grp(p0, 2)
     p1, p3 = from_grp(p0, 1), from_grp(p0, 3)
     q1, q3 = from_tok(q0, dx=1), from_tok(q0, dx=3)

time: 143 us -> 140 us (0.979)
  Pallas kernels: 35.4 us -> 33 us
    pallas_call x1 -> x0, Pallas kernels: 2.45 us -> none  [pack(): pl.pallas_call(pack_kernel, out_shape=(strip, strip, jax.ShapeDtypeStruct...]
    ppermute x16, waiting for transfers between devices: 6.56 us -> 8.57 us  [from_tok(): return lax.ppermute(block, 'tok', route)]
    unnamed x50 -> x38, local copies, waits for them, and re-layouts: 2.91 us -> 1.77 us
  transfers between devices with their start and end apart: 28 -> 28, of which waited for: 9 -> 8; matrix products, arithmetic and copies ran while one was open for 9% -> 9% of each run, Pallas kernels for 22% -> 20%
where the time goes in v2:
time: 140 us
  starting transfers between devices  34.9 us (25%)
  Pallas kernels  33 us (24%)
  blocking collectives  22.5 us (16%)
  waiting for transfers between devices  19.9 us (14%)
  between operations  15.3 us (11%)
  other arithmetic  8.55 us (6%)
  local copies, waits for them, and re-layouts  5.88 us (4%)
    all_gather x1, blocking collectives, per_device(): both = lax.all_gather(first, 'tok', axis_index_groups=GROUP_ZC)  22.5 us
    ppermute x16, starting transfers between devices, from_tok(): return lax.ppermute(block, 'tok', route)  22 us
    ppermute x9, waiting for transfers between devices, from_grp(): return lax.ppermute(block, 'grp', [((y + dy) % NY, y) for y in range(NY)])  11.3 us
    ppermute x9, starting transfers between devices, from_grp(): return lax.ppermute(block, 'grp', [((y + dy) % NY, y) for y in range(NY)])  10.2 us
    pallas_call x1, Pallas kernels, prefix_attention(): pl.pallas_call(functools.partial(prefix_kernel, scale), out_shape=(out, o...  8.81 us
    ppermute x16, waiting for transfers between devices, from_tok(): return lax.ppermute(block, 'tok', route)  8.57 us
    pallas_call x1, Pallas kernels, joint_projection(): pl.pallas_call(qkv_kernel, out_shape=(out, out), grid_spec=pltpu.Prefetch...  8.35 us
    pallas_call x1, Pallas kernels, suffix_attention(): pl.pallas_call(functools.partial(suffix_kernel, scale), out_shape=(out, o...  7.38 us
  transfers between devices with their start and end apart: 28, of which 8 were waited for; matrix products, arithmetic and copies ran while one was open for 9% of the time, Pallas kernels for 20%

profile of v2, /device:TPU:23, one launch (start us, length us, event | category | flops | bytes accessed | tf_op | source)
XLA Modules:
  0.0 139.9 jit_solution(14463973470050255146)
XLA Ops:
  7.2 0.8 collective-permute-start.3
  8.2 2.6 %collective-permute-start.1 = (bf16[32,1024]{1,0:T(8,128)(2,1)}, bf16[32,1024]{1,0:T(8,128)(2,1)S(1)}, u32[]{:S(2)}, u32[]{:S(2)}) collective-permute-start(bf16[32,1024]{1,0:T(8,128)(2,1)} %bitcast.42), channel_id=1, source_target_pairs={{128,0},{192,64},{0,128},{64,192},{129,1},{193,65},{1,129},{65,193... | collective-permute-start | bytes 196616 | tf_op jit(solution)/shard_map/ppermute | solution.py:34
  10.9 0.7 constant_dynamic-slice_fusion.9
  11.6 0.7 add_convert_fusion
  12.3 22.5 %all-gather = bf16[640,512]{1,0:T(8,128)(2,1)S(1)} all-gather(bf16[40,512]{1,0:T(8,128)(2,1)S(1)} %fusion.19), channel_id=2, replica_groups={{0,1,2,3,4,5,6,7,8,9,10,11,12,13,14,15},{16,17,18,19,20,21,22,23,24,25,..., dimensions={0}, use_global_device_ids=true | all-gather | bytes 696320 | tf_op jit(solution)/shard_map/all_gather | solution.py:360
  34.8 1.2 dynamic_slice.39
  37.1 1.9 %collective-permute-start.7 = (bf16[264,256]{1,0:T(8,128)(2,1)S(1)}, bf16[264,256]{1,0:T(8,128)(2,1)S(1)}, u32[]{:S(2)}, u32[]{:S(2)}) collective-permute-start(bf16[264,256]{1,0:T(8,128)(2,1)S(1)} %concatenate.61), channel_id=1, source_target_pairs={{64,0},{128,64},{192,128},{0,192},{65,1},{129,65},{193,129},{1,193... | collective-permute-start | bytes 405512 | tf_op jit(solution)/shard_map/ppermute | solution.py:34
  39.1 0.6 collective-permute-start.4
  39.7 0.8 collective-permute-start.5
  40.5 1.8 %collective-permute-start.6 = (bf16[392,256]{1,0:T(8,128)(2,1)S(1)}, bf16[392,256]{1,0:T(8,128)(2,1)S(1)}, u32[]{:S(2)}, u32[]{:S(2)}) collective-permute-start(bf16[392,256]{1,0:T(8,128)(2,1)S(1)} %constant_dynamic-update-slice_fusion), channel_id=1, source_target_pairs={{48,0},{49,1},{50,2},{51,3},{52,4},{53,5},{54,6},{55,7},{56,8},{57... | collective-permute-start | bytes 602120 | tf_op jit(solution)/shard_map/ppermute | solution.py:30
  42.4 1.4 collective-permute-start.8
  43.7 1.0 collective-permute-start.9
  44.8 3.3 %collective-permute-done.8 = bf16[264,256]{1,0:T(8,128)(2,1)S(1)} collective-permute-done((bf16[264,256]{1,0:T(8,128)(2,1)S(1)}, bf16[264,256]{1,0:T(8,128)(2,1)S(1)}, u32[]{:S(2)}, u32[]{:S(2)}) %collective-permute-start.8) | collective-permute-done | bytes 135200 | tf_op jit(solution)/shard_map/ppermute | solution.py:34
  48.1 3.6 %collective-permute-done.9 = bf16[264,256]{1,0:T(8,128)(2,1)S(1)} collective-permute-done((bf16[264,256]{1,0:T(8,128)(2,1)S(1)}, bf16[264,256]{1,0:T(8,128)(2,1)S(1)}, u32[]{:S(2)}, u32[]{:S(2)}) %collective-permute-start.9) | collective-permute-done | bytes 135200 | tf_op jit(solution)/shard_map/ppermute | solution.py:34
  51.7 0.7 maximum_maximum_fusion
  52.8 1.0 collective-permute-start.11
  53.8 2.0 %collective-permute-start.12 = (bf16[1024,256]{1,0:T(8,128)(2,1)S(1)}, bf16[1024,256]{1,0:T(8,128)(2,1)}, u32[]{:S(2)}, u32[]{:S(2)}) collective-permute-start(bf16[1024,256]{1,0:T(8,128)(2,1)S(1)} %pad_maximum_fusion.1.p0), channel_id=1, source_target_pairs={{192,0},{0,64},{64,128},{128,192},{193,1},{1,65},{65,129},{129,193... | collective-permute-start | bytes 1572872 | tf_op jit(solution)/shard_map/ppermute | solution.py:34
  55.9 1.6 %collective-permute-start.13 = (bf16[1024,256]{1,0:T(8,128)(2,1)S(1)}, bf16[1024,256]{1,0:T(8,128)(2,1)S(1)}, u32[]{:S(2)}, u32[]{:S(2)}) collective-permute-start(bf16[1024,256]{1,0:T(8,128)(2,1)S(1)} %pad_maximum_fusion.2.q0), channel_id=1, source_target_pairs={{16,0},{17,1},{18,2},{19,3},{20,4},{21,5},{22,6},{23,7},{24,8},{25... | collective-permute-start | bytes 1572872 | tf_op jit(solution)/shard_map/ppermute | solution.py:30
  57.5 3.1 %collective-permute-start.14 = (bf16[1024,256]{1,0:T(8,128)(2,1)S(1)}, bf16[1024,256]{1,0:T(8,128)(2,1)S(1)}, u32[]{:S(2)}, u32[]{:S(2)}) collective-permute-start(bf16[1024,256]{1,0:T(8,128)(2,1)S(1)} %pad_maximum_fusion.2.q0), channel_id=1, source_target_pairs={{32,0},{33,1},{34,2},{35,3},{36,4},{37,5},{38,6},{39,7},{40,8},{41... | collective-permute-start | bytes 1572872 | tf_op jit(solution)/shard_map/ppermute | solution.py:30
  61.0 1.0 fusion.13
  62.4 3.0 %collective-permute-done.10.p1 = bf16[1024,256]{1,0:T(8,128)(2,1)S(1)} collective-permute-done((bf16[1024,256]{1,0:T(8,128)(2,1)S(1)}, bf16[1024,256]{1,0:T(8,128)(2,1)S(1)}, u32[]{:S(2)}, u32[]{:S(2)}) %collective-permute-start.10) | collective-permute-done | bytes 524320 | tf_op jit(solution)/shard_map/ppermute | solution.py:34
  65.3 3.5 %collective-permute-start.15 = (bf16[1024,256]{1,0:T(8,128)(2,1)S(1)}, bf16[1024,256]{1,0:T(8,128)(2,1)}, u32[]{:S(2)}, u32[]{:S(2)}) collective-permute-start(bf16[1024,256]{1,0:T(8,128)(2,1)S(1)} %pad_maximum_fusion.2.q0), channel_id=1, source_target_pairs={{48,0},{49,1},{50,2},{51,3},{52,4},{53,5},{54,6},{55,7},{56,8},{57... | collective-permute-start | bytes 1572872 | tf_op jit(solution)/shard_map/ppermute | solution.py:30
  68.8 0.8 pad_maximum_fusion.4.cos_ref
  69.7 0.8 pad_maximum_fusion.5.sin_ref
  70.6 1.0 pad_maximum_fusion.bias_ref
  71.6 0.6 broadcast_in_dim.47.gain_ref
  72.2 3.9 %input_norm.1 = (bf16[512,1024]{1,0:T(8,128)(2,1)}, bf16[512,1024]{1,0:T(8,128)(2,1)}) custom-call(s32[1]{0:T(128)} %bitcast.x_ref, bf16[256,2048]{1,0:T(8,128)(2,1)} %bitcast.37, bf16[256,2048]{1,0:T(8,128)(2,1)} %copy-done.4, bf16[1,2048]{1,0:T(2,128)(2,1)} %broadcast_in_dim.47.gain_ref), custom_call_target="tpu_custom_call" | custom-call | tf_op jit(solution)/shard_map/input_norm/pallas_call | solution.py:68
  76.1 1.1 constant_dynamic-slice_fusion.10.refs_0_
  77.3 1.4 %collective-permute-done.12.p3 = bf16[1024,256]{1,0:T(8,128)(2,1)} collective-permute-done((bf16[1024,256]{1,0:T(8,128)(2,1)S(1)}, bf16[1024,256]{1,0:T(8,128)(2,1)}, u32[]{:S(2)}, u32[]{:S(2)}) %collective-permute-start.12) | collective-permute-done | bytes 524320 | tf_op jit(solution)/shard_map/ppermute | solution.py:34
  78.7 3.7 %collective-permute-done.14.q2 = bf16[1024,256]{1,0:T(8,128)(2,1)S(1)} collective-permute-done((bf16[1024,256]{1,0:T(8,128)(2,1)S(1)}, bf16[1024,256]{1,0:T(8,128)(2,1)S(1)}, u32[]{:S(2)}, u32[]{:S(2)}) %collective-permute-start.14) | collective-permute-done | bytes 524320 | tf_op jit(solution)/shard_map/ppermute | solution.py:30
  82.4 1.3 collective-permute-start.18
  83.7 2.6 %collective-permute-start.19 = (bf16[256,1024]{1,0:T(8,128)(2,1)S(1)}, bf16[256,1024]{1,0:T(8,128)(2,1)S(1)}, u32[]{:S(2)}, u32[]{:S(2)}) collective-permute-start(bf16[256,1024]{1,0:T(8,128)(2,1)S(1)} %constant_dynamic-slice_fusion.10.refs_0_), channel_id=1, source_target_pairs={{32,0},{33,1},{34,2},{35,3},{36,4},{37,5},{38,6},{39,7},{40,8},{41... | collective-permute-start | bytes 1572872 | tf_op jit(solution)/shard_map/ppermute | solution.py:30
  86.3 8.4 %joint_projection.1 = (bf16[2,512,256]{2,1,0:T(8,128)(2,1)}, bf16[2,512,256]{2,1,0:T(8,128)(2,1)}) custom-call(s32[1]{0:T(128)} %bitcast.24.y_ref, bf16[512,1024]{1,0:T(8,128)(2,1)} %get-tuple-element.78.np_ref, bf16[512,1024]{1,0:T(8,128)(2,1)} %get-tuple-element.79.nq_ref, bf16[1024,256]{1,0:T(8,128)(2,1)} %copy-done.8, bf16[1024,256]{1,0:T(8,128)(2,1)} %copy-done.13, ...), custom_call_target="tpu_custom_call" | custom-call | flops 2147483648 | bytes 8388608 | tf_op jit(solution)/shard_map/joint_projection/pallas_call | solution.py:137
  94.6 2.6 %collective-permute-start.17 = (bf16[2,512,256]{2,1,0:T(8,128)(2,1)}, bf16[2,512,256]{2,1,0:T(8,128)(2,1)S(1)}, u32[]{:S(2)}, u32[]{:S(2)}) collective-permute-start(bf16[2,512,256]{2,1,0:T(8,128)(2,1)} %get-tuple-element.106.ko_ref.vo_ref), channel_id=1, source_target_pairs={{0,2},{1,3},{2,4},{3,5},{4,6},{5,7},{6,8},{7,9},{8,10},{9,11},{10,... | collective-permute-start | bytes 1572872 | tf_op jit(solution)/shard_map/ppermute | solution.py:40
  97.8 8.8 %prefix_attention.1 = (f32[4,512,128]{2,1,0:T(8,128)}, f32[4,512,128]{2,1,0:T(8,128)}) custom-call(s32[1]{0:T(128)} %bitcast.1.core_ref, bf16[2,512,256]{2,1,0:T(8,128)(2,1)} %get-tuple-element.92.q_ref, bf16[2048,1024]{1,0:T(8,128)(2,1)} %all-gather.6.cloned.1.call-done.k_ref.v_ref, bf16[2048,1024]{1,0:T(8,128)(2,1)} %all-gather.6.cloned.1.call-done.k_ref.v_ref), custom_call_target="tpu_custom_call" | custom-call | flops 2147483648 | bytes 4194304 | tf_op jit(solution)/shard_map/prefix_attention/pallas_call | solution.py:206
  106.6 1.1 collective-permute-done.19.refs_2_
  107.7 2.6 %collective-permute-start.25 = (bf16[2,512,256]{2,1,0:T(8,128)(2,1)S(1)}, bf16[2,512,256]{2,1,0:T(8,128)(2,1)}, u32[]{:S(2)}, u32[]{:S(2)}) collective-permute-start(bf16[2,512,256]{2,1,0:T(8,128)(2,1)S(1)} %copy-done), channel_id=1, source_target_pairs={{1,0},{0,1},{3,2},{2,3},{5,4},{4,5},{7,6},{6,7},{9,8},{8,9},{11,10... | collective-permute-start | bytes 1572872 | tf_op jit(solution)/shard_map/ppermute | solution.py:30
  110.4 0.8 copy-done.3
  111.2 7.4 %suffix_attention.1 = (bf16[256,512]{1,0:T(8,128)(2,1)}, bf16[256,512]{1,0:T(8,128)(2,1)}) custom-call(s32[1]{0:T(128)} %bitcast.1.core_ref, bf16[2,512,256]{2,1,0:T(8,128)(2,1)} %get-tuple-element.92.q_ref, bf16[2,512,256]{2,1,0:T(8,128)(2,1)} %get-tuple-element.106.ko_ref.vo_ref, bf16[2,512,256]{2,1,0:T(8,128)(2,1)} %get-tuple-element.106.ko_ref.vo_ref, ...), custom_call_target="tpu_custom_call" | custom-call | flops 805306368 | bytes 4194304 | tf_op jit(solution)/shard_map/suffix_attention/pallas_call | solution.py:268
  118.6 2.8 %collective-permute-done.16.refs_3_ = bf16[256,1024]{1,0:T(8,128)(2,1)} collective-permute-done((bf16[256,1024]{1,0:T(8,128)(2,1)S(1)}, bf16[256,1024]{1,0:T(8,128)(2,1)}, u32[]{:S(2)}, u32[]{:S(2)}) %collective-permute-start.16) | collective-permute-done | bytes 524320 | tf_op jit(solution)/shard_map/ppermute | solution.py:30
  121.4 1.9 %collective-permute-start.21 = (bf16[256,1024]{1,0:T(8,128)(2,1)S(1)}, bf16[256,1024]{1,0:T(8,128)(2,1)S(1)}, u32[]{:S(2)}, u32[]{:S(2)}) collective-permute-start(bf16[256,1024]{1,0:T(8,128)(2,1)S(1)} %constant_dynamic-slice_fusion.10.refs_0_), channel_id=1, source_target_pairs={{1,0},{0,1},{3,2},{2,3},{5,4},{4,5},{7,6},{6,7},{9,8},{8,9},{11,10... | collective-permute-start | bytes 1572872 | tf_op jit(solution)/shard_map/ppermute | solution.py:30
  123.8 0.6 pad_add_fusion.place_ref
  124.4 0.5 collective-permute-start.20
  124.9 1.0 broadcast_select_fusion
  125.9 0.8 pad_maximum_fusion.3
  126.7 0.9 collective-permute-done.20.other_ref
  127.7 0.7 copy-done.10
  128.5 4.6 %output_projection.1 = bf16[256,2048]{1,0:T(8,128)(2,1)} custom-call(s32[2]{0:T(128)} %pad_add_fusion.place_ref, bf16[256,512]{1,0:T(8,128)(2,1)} %get-tuple-element.100.mine_ref, bf16[256,512]{1,0:T(8,128)(2,1)} %copy-done.10, bf16[256,1024]{1,0:T(8,128)(2,1)} %copy-done.2, bf16[256,1024]{1,0:T(8,128)(2,1)} %copy-done.5, bf16[256,1024]{1,0:T(8,128)(2,1)} %copy-done.6, ...), custom_call_target="tpu_custom_call" | custom-call | flops 1073741824 | bytes 6291456 | tf_op jit(solution)/shard_map/output_projection/pallas_call | solution.py:315
  (97 shorter events, 3.2 us)
Async XLA Ops:
  7.2 31.8 %copy-start.11 = (bf16[1,32,1024]{2,1,0:T(8,128)(2,1)S(1)}, bf16[1,32,1024]{2,1,0:T(8,128)(2,1)}, u32[]{:S(2)}) copy-start(bf16[1,32,1024]{2,1,0:T(8,128)(2,1)} %param.11) | copy-start | bytes 196612
  7.2 69.0 %all-gather.4.cloned.1.call-start = ((), (), s32[]{:S(2)}) async-start(), calls=%async_computation | async-start | bytes 1114112 | tf_op jit(solution)/shard_map/all_gather | solution.py:344
  7.2 29.5 %collective-permute-start.3 = (bf16[256,2048]{1,0:T(8,128)(2,1)}, bf16[256,2048]{1,0:T(8,128)(2,1)S(1)}, u32[]{:S(2)}, u32[]{:S(2)}) collective-permute-start(bf16[256,2048]{1,0:T(8,128)(2,1)} %bitcast.36), channel_id=1, source_target_pairs={{1,0},{0,1},{3,2},{2,3},{5,4},{4,5},{7,6},{6,7},{9,8},{8,9},{11,10... | collective-permute-start | bytes 3145736 | tf_op jit(solution)/shard_map/ppermute | solution.py:30
  8.0 28.7 %collective-permute-start = (bf16[32,1024]{1,0:T(8,128)(2,1)}, bf16[32,1024]{1,0:T(8,128)(2,1)S(1)}, u32[]{:S(2)}, u32[]{:S(2)}) collective-permute-start(bf16[32,1024]{1,0:T(8,128)(2,1)} %bitcast.41), channel_id=1, source_target_pairs={{64,0},{128,64},{192,128},{0,192},{65,1},{129,65},{193,129},{1,193... | collective-permute-start | bytes 196616 | tf_op jit(solution)/shard_map/ppermute | solution.py:34
  8.2 28.5 %collective-permute-start.1 = (bf16[32,1024]{1,0:T(8,128)(2,1)}, bf16[32,1024]{1,0:T(8,128)(2,1)S(1)}, u32[]{:S(2)}, u32[]{:S(2)}) collective-permute-start(bf16[32,1024]{1,0:T(8,128)(2,1)} %bitcast.42), channel_id=1, source_target_pairs={{128,0},{192,64},{0,128},{64,192},{129,1},{193,65},{1,129},{65,193... | collective-permute-start | bytes 196616 | tf_op jit(solution)/shard_map/ppermute | solution.py:34
  10.8 25.9 %collective-permute-start.2 = (bf16[32,1024]{1,0:T(8,128)(2,1)}, bf16[32,1024]{1,0:T(8,128)(2,1)S(1)}, u32[]{:S(2)}, u32[]{:S(2)}) collective-permute-start(bf16[32,1024]{1,0:T(8,128)(2,1)} %bitcast.43), channel_id=1, source_target_pairs={{192,0},{0,64},{64,128},{128,192},{193,1},{1,65},{65,129},{129,193... | collective-permute-start | bytes 196616 | tf_op jit(solution)/shard_map/ppermute | solution.py:34
  10.8 86.9 %all-gather.6.cloned.1.call-start = ((), (), s32[]{:S(2)}) async-start(), calls=%async_computation.1 | async-start | bytes 4456448 | tf_op jit(solution)/shard_map/all_gather | solution.py:392
  36.7 19.1 %copy-start.4 = (bf16[256,2048]{1,0:T(8,128)(2,1)}, bf16[256,2048]{1,0:T(8,128)(2,1)S(1)}, u32[]{:S(2)}) copy-start(bf16[256,2048]{1,0:T(8,128)(2,1)S(1)} %collective-permute-done.3.peer_ref) | copy-start | bytes 3145732
  37.1 6.7 %collective-permute-start.7 = (bf16[264,256]{1,0:T(8,128)(2,1)S(1)}, bf16[264,256]{1,0:T(8,128)(2,1)S(1)}, u32[]{:S(2)}, u32[]{:S(2)}) collective-permute-start(bf16[264,256]{1,0:T(8,128)(2,1)S(1)} %concatenate.61), channel_id=1, source_target_pairs={{64,0},{128,64},{192,128},{0,192},{65,1},{129,65},{193,129},{1,193... | collective-permute-start | bytes 405512 | tf_op jit(solution)/shard_map/ppermute | solution.py:34
  39.1 12.6 %collective-permute-start.4 = (bf16[392,256]{1,0:T(8,128)(2,1)S(1)}, bf16[392,256]{1,0:T(8,128)(2,1)S(1)}, u32[]{:S(2)}, u32[]{:S(2)}) collective-permute-start(bf16[392,256]{1,0:T(8,128)(2,1)S(1)} %constant_dynamic-update-slice_fusion), channel_id=1, source_target_pairs={{16,0},{17,1},{18,2},{19,3},{20,4},{21,5},{22,6},{23,7},{24,8},{25... | collective-permute-start | bytes 602120 | tf_op jit(solution)/shard_map/ppermute | solution.py:30
  39.7 12.0 %collective-permute-start.5 = (bf16[392,256]{1,0:T(8,128)(2,1)S(1)}, bf16[392,256]{1,0:T(8,128)(2,1)S(1)}, u32[]{:S(2)}, u32[]{:S(2)}) collective-permute-start(bf16[392,256]{1,0:T(8,128)(2,1)S(1)} %constant_dynamic-update-slice_fusion), channel_id=1, source_target_pairs={{32,0},{33,1},{34,2},{35,3},{36,4},{37,5},{38,6},{39,7},{40,8},{41... | collective-permute-start | bytes 602120 | tf_op jit(solution)/shard_map/ppermute | solution.py:30
  40.5 11.1 %collective-permute-start.6 = (bf16[392,256]{1,0:T(8,128)(2,1)S(1)}, bf16[392,256]{1,0:T(8,128)(2,1)S(1)}, u32[]{:S(2)}, u32[]{:S(2)}) collective-permute-start(bf16[392,256]{1,0:T(8,128)(2,1)S(1)} %constant_dynamic-update-slice_fusion), channel_id=1, source_target_pairs={{48,0},{49,1},{50,2},{51,3},{52,4},{53,5},{54,6},{55,7},{56,8},{57... | collective-permute-start | bytes 602120 | tf_op jit(solution)/shard_map/ppermute | solution.py:30
  42.4 5.7 %collective-permute-start.8 = (bf16[264,256]{1,0:T(8,128)(2,1)S(1)}, bf16[264,256]{1,0:T(8,128)(2,1)S(1)}, u32[]{:S(2)}, u32[]{:S(2)}) collective-permute-start(bf16[264,256]{1,0:T(8,128)(2,1)S(1)} %concatenate.61), channel_id=1, source_target_pairs={{128,0},{192,64},{0,128},{64,192},{129,1},{193,65},{1,129},{65,193... | collective-permute-start | bytes 405512 | tf_op jit(solution)/shard_map/ppermute | solution.py:34
  43.7 7.9 %collective-permute-start.9 = (bf16[264,256]{1,0:T(8,128)(2,1)S(1)}, bf16[264,256]{1,0:T(8,128)(2,1)S(1)}, u32[]{:S(2)}, u32[]{:S(2)}) collective-permute-start(bf16[264,256]{1,0:T(8,128)(2,1)S(1)} %concatenate.61), channel_id=1, source_target_pairs={{192,0},{0,64},{64,128},{128,192},{193,1},{1,65},{65,129},{129,193... | collective-permute-start | bytes 405512 | tf_op jit(solution)/shard_map/ppermute | solution.py:34
  52.7 23.4 %copy-start.8 = (bf16[1024,256]{1,0:T(8,128)(2,1)}, bf16[1024,256]{1,0:T(8,128)(2,1)S(1)}, u32[]{:S(2)}) copy-start(bf16[1024,256]{1,0:T(8,128)(2,1)S(1)} %pad_maximum_fusion.1.p0) | copy-start | bytes 1572868
  52.7 18.9 %copy-start.12 = (bf16[2048]{0:T(1024)(128)(2,1)S(1)}, bf16[2048]{0:T(1024)(128)(2,1)}, u32[]{:S(2)}) copy-start(bf16[2048]{0:T(1024)(128)(2,1)} %param.13) | copy-start | bytes 12292
  52.7 12.6 %collective-permute-start.10 = (bf16[1024,256]{1,0:T(8,128)(2,1)S(1)}, bf16[1024,256]{1,0:T(8,128)(2,1)S(1)}, u32[]{:S(2)}, u32[]{:S(2)}) collective-permute-start(bf16[1024,256]{1,0:T(8,128)(2,1)S(1)} %pad_maximum_fusion.1.p0), channel_id=1, source_target_pairs={{64,0},{128,64},{192,128},{0,192},{65,1},{129,65},{193,129},{1,193... | collective-permute-start | bytes 1572872 | tf_op jit(solution)/shard_map/ppermute | solution.py:34
  52.8 24.4 %collective-permute-start.11 = (bf16[1024,256]{1,0:T(8,128)(2,1)S(1)}, bf16[1024,256]{1,0:T(8,128)(2,1)}, u32[]{:S(2)}, u32[]{:S(2)}) collective-permute-start(bf16[1024,256]{1,0:T(8,128)(2,1)S(1)} %pad_maximum_fusion.1.p0), channel_id=1, source_target_pairs={{128,0},{192,64},{0,128},{64,192},{129,1},{193,65},{1,129},{65,193... | collective-permute-start | bytes 1572872 | tf_op jit(solution)/shard_map/ppermute | solution.py:34
  53.8 24.9 %collective-permute-start.12 = (bf16[1024,256]{1,0:T(8,128)(2,1)S(1)}, bf16[1024,256]{1,0:T(8,128)(2,1)}, u32[]{:S(2)}, u32[]{:S(2)}) collective-permute-start(bf16[1024,256]{1,0:T(8,128)(2,1)S(1)} %pad_maximum_fusion.1.p0), channel_id=1, source_target_pairs={{192,0},{0,64},{64,128},{128,192},{193,1},{1,65},{65,129},{129,193... | collective-permute-start | bytes 1572872 | tf_op jit(solution)/shard_map/ppermute | solution.py:34
  55.9 21.3 %copy-start.9 = (bf16[1024,256]{1,0:T(8,128)(2,1)}, bf16[1024,256]{1,0:T(8,128)(2,1)S(1)}, u32[]{:S(2)}) copy-start(bf16[1024,256]{1,0:T(8,128)(2,1)S(1)} %pad_maximum_fusion.2.q0) | copy-start | bytes 1572868
  55.9 22.8 %collective-permute-start.13 = (bf16[1024,256]{1,0:T(8,128)(2,1)S(1)}, bf16[1024,256]{1,0:T(8,128)(2,1)S(1)}, u32[]{:S(2)}, u32[]{:S(2)}) collective-permute-start(bf16[1024,256]{1,0:T(8,128)(2,1)S(1)} %pad_maximum_fusion.2.q0), channel_id=1, source_target_pairs={{16,0},{17,1},{18,2},{19,3},{20,4},{21,5},{22,6},{23,7},{24,8},{25... | collective-permute-start | bytes 1572872 | tf_op jit(solution)/shard_map/ppermute | solution.py:30
  57.5 24.9 %collective-permute-start.14 = (bf16[1024,256]{1,0:T(8,128)(2,1)S(1)}, bf16[1024,256]{1,0:T(8,128)(2,1)S(1)}, u32[]{:S(2)}, u32[]{:S(2)}) collective-permute-start(bf16[1024,256]{1,0:T(8,128)(2,1)S(1)} %pad_maximum_fusion.2.q0), channel_id=1, source_target_pairs={{32,0},{33,1},{34,2},{35,3},{36,4},{37,5},{38,6},{39,7},{40,8},{41... | collective-permute-start | bytes 1572872 | tf_op jit(solution)/shard_map/ppermute | solution.py:30
  65.3 5.2 %copy-start.13 = (bf16[1024,256]{1,0:T(8,128)(2,1)}, bf16[1024,256]{1,0:T(8,128)(2,1)S(1)}, u32[]{:S(2)}) copy-start(bf16[1024,256]{1,0:T(8,128)(2,1)S(1)} %collective-permute-done.10.p1) | copy-start | bytes 1572868
  65.3 17.1 %collective-permute-start.15 = (bf16[1024,256]{1,0:T(8,128)(2,1)S(1)}, bf16[1024,256]{1,0:T(8,128)(2,1)}, u32[]{:S(2)}, u32[]{:S(2)}) collective-permute-start(bf16[1024,256]{1,0:T(8,128)(2,1)S(1)} %pad_maximum_fusion.2.q0), channel_id=1, source_target_pairs={{48,0},{49,1},{50,2},{51,3},{52,4},{53,5},{54,6},{55,7},{56,8},{57... | collective-permute-start | bytes 1572872 | tf_op jit(solution)/shard_map/ppermute | solution.py:30
  77.2 44.1 %copy-start.2 = (bf16[256,1024]{1,0:T(8,128)(2,1)}, bf16[256,1024]{1,0:T(8,128)(2,1)S(1)}, u32[]{:S(2)}) copy-start(bf16[256,1024]{1,0:T(8,128)(2,1)S(1)} %constant_dynamic-slice_fusion.10.refs_0_) | copy-start | bytes 1572868
  78.7 7.6 %copy-start.14 = (bf16[1024,256]{1,0:T(8,128)(2,1)}, bf16[1024,256]{1,0:T(8,128)(2,1)S(1)}, u32[]{:S(2)}) copy-start(bf16[1024,256]{1,0:T(8,128)(2,1)S(1)} %collective-permute-done.13.q1) | copy-start | bytes 1572868
  82.4 3.9 %copy-start.15 = (bf16[1024,256]{1,0:T(8,128)(2,1)}, bf16[1024,256]{1,0:T(8,128)(2,1)S(1)}, u32[]{:S(2)}) copy-start(bf16[1024,256]{1,0:T(8,128)(2,1)S(1)} %collective-permute-done.14.q2) | copy-start | bytes 1572868
  82.4 24.2 %collective-permute-start.18 = (bf16[256,1024]{1,0:T(8,128)(2,1)S(1)}, bf16[256,1024]{1,0:T(8,128)(2,1)S(1)}, u32[]{:S(2)}, u32[]{:S(2)}) collective-permute-start(bf16[256,1024]{1,0:T(8,128)(2,1)S(1)} %constant_dynamic-slice_fusion.10.refs_0_), channel_id=1, source_target_pairs={{16,0},{17,1},{18,2},{19,3},{20,4},{21,5},{22,6},{23,7},{24,8},{25... | collective-permute-start | bytes 1572872 | tf_op jit(solution)/shard_map/ppermute | solution.py:30
  83.7 24.0 %collective-permute-start.19 = (bf16[256,1024]{1,0:T(8,128)(2,1)S(1)}, bf16[256,1024]{1,0:T(8,128)(2,1)S(1)}, u32[]{:S(2)}, u32[]{:S(2)}) collective-permute-start(bf16[256,1024]{1,0:T(8,128)(2,1)S(1)} %constant_dynamic-slice_fusion.10.refs_0_), channel_id=1, source_target_pairs={{32,0},{33,1},{34,2},{35,3},{36,4},{37,5},{38,6},{39,7},{40,8},{41... | collective-permute-start | bytes 1572872 | tf_op jit(solution)/shard_map/ppermute | solution.py:30
  94.6 15.8 %collective-permute-start.17 = (bf16[2,512,256]{2,1,0:T(8,128)(2,1)}, bf16[2,512,256]{2,1,0:T(8,128)(2,1)S(1)}, u32[]{:S(2)}, u32[]{:S(2)}) collective-permute-start(bf16[2,512,256]{2,1,0:T(8,128)(2,1)} %get-tuple-element.106.ko_ref.vo_ref), channel_id=1, source_target_pairs={{0,2},{1,3},{2,4},{3,5},{4,6},{5,7},{6,8},{7,9},{8,10},{9,11},{10,... | collective-permute-start | bytes 1572872 | tf_op jit(solution)/shard_map/ppermute | solution.py:40
  97.3 24.1 %collective-permute-start.16 = (bf16[256,1024]{1,0:T(8,128)(2,1)S(1)}, bf16[256,1024]{1,0:T(8,128)(2,1)}, u32[]{:S(2)}, u32[]{:S(2)}) collective-permute-start(bf16[256,1024]{1,0:T(8,128)(2,1)S(1)} %constant_dynamic-slice_fusion.10.refs_0_), channel_id=1, source_target_pairs={{48,0},{49,1},{50,2},{51,3},{52,4},{53,5},{54,6},{55,7},{56,8},{57... | collective-permute-start | bytes 1572872 | tf_op jit(solution)/shard_map/ppermute | solution.py:30
  97.8 10.0 %copy-start = (bf16[2,512,256]{2,1,0:T(8,128)(2,1)S(1)}, bf16[2,512,256]{2,1,0:T(8,128)(2,1)}, u32[]{:S(2)}) copy-start(bf16[2,512,256]{2,1,0:T(8,128)(2,1)} %get-tuple-element.106.ko_ref.vo_ref) | copy-start | bytes 1572868
  106.6 18.3 %copy-start.1 = (bf16[2,512,256]{2,1,0:T(8,128)(2,1)S(1)}, bf16[2,512,256]{2,1,0:T(8,128)(2,1)}, u32[]{:S(2)}) copy-start(bf16[2,512,256]{2,1,0:T(8,128)(2,1)} %get-tuple-element.106.ko_ref.vo_ref) | copy-start | bytes 1572868
  106.6 21.1 %copy-start.5 = (bf16[256,1024]{1,0:T(8,128)(2,1)}, bf16[256,1024]{1,0:T(8,128)(2,1)S(1)}, u32[]{:S(2)}) copy-start(bf16[256,1024]{1,0:T(8,128)(2,1)S(1)} %collective-permute-done.18.refs_1_) | copy-start | bytes 1572868
  107.7 19.9 %copy-start.6 = (bf16[256,1024]{1,0:T(8,128)(2,1)}, bf16[256,1024]{1,0:T(8,128)(2,1)S(1)}, u32[]{:S(2)}) copy-start(bf16[256,1024]{1,0:T(8,128)(2,1)S(1)} %collective-permute-done.19.refs_2_) | copy-start | bytes 1572868
  107.7 16.6 %collective-permute-start.25 = (bf16[2,512,256]{2,1,0:T(8,128)(2,1)S(1)}, bf16[2,512,256]{2,1,0:T(8,128)(2,1)}, u32[]{:S(2)}, u32[]{:S(2)}) collective-permute-start(bf16[2,512,256]{2,1,0:T(8,128)(2,1)S(1)} %copy-done), channel_id=1, source_target_pairs={{1,0},{0,1},{3,2},{2,3},{5,4},{4,5},{7,6},{6,7},{9,8},{8,9},{11,10... | collective-permute-start | bytes 1572872 | tf_op jit(solution)/shard_map/ppermute | solution.py:30
  110.4 0.8 copy-start.3
  121.4 6.2 %collective-permute-start.21 = (bf16[256,1024]{1,0:T(8,128)(2,1)S(1)}, bf16[256,1024]{1,0:T(8,128)(2,1)S(1)}, u32[]{:S(2)}, u32[]{:S(2)}) collective-permute-start(bf16[256,1024]{1,0:T(8,128)(2,1)S(1)} %constant_dynamic-slice_fusion.10.refs_0_), channel_id=1, source_target_pairs={{1,0},{0,1},{3,2},{2,3},{5,4},{4,5},{7,6},{6,7},{9,8},{8,9},{11,10... | collective-permute-start | bytes 1572872 | tf_op jit(solution)/shard_map/ppermute | solution.py:30
  123.2 4.4 %collective-permute-start.22 = (bf16[256,1024]{1,0:T(8,128)(2,1)S(1)}, bf16[256,1024]{1,0:T(8,128)(2,1)}, u32[]{:S(2)}, u32[]{:S(2)}) collective-permute-start(bf16[256,1024]{1,0:T(8,128)(2,1)S(1)} %collective-permute-done.18.refs_1_), channel_id=1, source_target_pairs={{1,0},{0,1},{3,2},{2,3},{5,4},{4,5},{7,6},{6,7},{9,8},{8,9},{11,10... | collective-permute-start | bytes 1572872 | tf_op jit(solution)/shard_map/ppermute | solution.py:30
  123.2 4.4 %collective-permute-start.23 = (bf16[256,1024]{1,0:T(8,128)(2,1)S(1)}, bf16[256,1024]{1,0:T(8,128)(2,1)}, u32[]{:S(2)}, u32[]{:S(2)}) collective-permute-start(bf16[256,1024]{1,0:T(8,128)(2,1)S(1)} %collective-permute-done.19.refs_2_), channel_id=1, source_target_pairs={{1,0},{0,1},{3,2},{2,3},{5,4},{4,5},{7,6},{6,7},{9,8},{8,9},{11,10... | collective-permute-start | bytes 1572872 | tf_op jit(solution)/shard_map/ppermute | solution.py:30
  123.7 3.9 %collective-permute-start.24 = (bf16[256,1024]{1,0:T(8,128)(2,1)}, bf16[256,1024]{1,0:T(8,128)(2,1)}, u32[]{:S(2)}, u32[]{:S(2)}) collective-permute-start(bf16[256,1024]{1,0:T(8,128)(2,1)} %collective-permute-done.16.refs_3_), channel_id=1, source_target_pairs={{1,0},{0,1},{3,2},{2,3},{5,4},{4,5},{7,6},{6,7},{9,8},{8,9},{11,10... | collective-permute-start | bytes 1572872 | tf_op jit(solution)/shard_map/ppermute | solution.py:30
  124.4 3.2 %collective-permute-start.20 = (bf16[256,512]{1,0:T(8,128)(2,1)}, bf16[256,512]{1,0:T(8,128)(2,1)S(1)}, u32[]{:S(2)}, u32[]{:S(2)}) collective-permute-start(bf16[256,512]{1,0:T(8,128)(2,1)} %get-tuple-element.101), channel_id=1, source_target_pairs={{1,0},{0,1},{3,2},{2,3},{5,4},{4,5},{7,6},{6,7},{9,8},{8,9},{11,10... | collective-permute-start | bytes 786440 | tf_op jit(solution)/shard_map/ppermute | solution.py:30
  127.6 0.7 copy-start.10
  127.6 0.9 copy-start.7
Sparse Core Ops, SparseCore 0:
  10.9 42.0 all-gather.3
  54.9 40.5 all-gather.5

commit v3 on v2

--- a/solution.py
+++ b/solution.py
@@ -78,23 +78,32 @@
 
 def qkv_kernel(
     y_ref, np_ref, nq_ref, p0, p1, p2, p3, q0, q1, q2, q3, cos_ref, sin_ref, qg_ref, kg_ref,
-    q_out, kv_out, acc
+    q_out, kv_out, acc, b1, b2, b3, sems
 ):
     step = pl.program_id(0)
     block = (y_ref[0] + step) % NY
+    copies = [
+        pltpu.make_async_copy(p, b, sems.at[i])
+        for i, (p, b) in enumerate(((p1, b1), (p2, b2), (p3, b3)))
+    ]
+
+    @pl.when(step == 0)
+    def _():
+        for copy in copies:
+            copy.start()
 
     def dot(a, b):
         return jnp.dot(a, b, preferred_element_type=jnp.float32)
 
-    for k, p in enumerate((p0, p1, p2, p3)):
+    for k, p in enumerate((p0, b1, b2, b3)):
 
         @pl.when(step == k)
         def _(p=p, k=k):
+            if k > 0:
+                copies[k - 1].wait()
             total = dot(np_ref[...], p[...])
             for j, q in enumerate((q0, q1, q2, q3)):
-                total = total + dot(
-                    nq_ref[:, j * 256 : (j + 1) * 256], q[k * 256 : (k + 1) * 256, :]
-                )
+                total = total + dot(nq_ref[:, j * 256 : (j + 1) * 256], q[...])
             acc[...] = total
 
     def turned(gain_ref, out):
@@ -140,12 +149,17 @@
         grid_spec=pltpu.PrefetchScalarGridSpec(
             num_scalar_prefetch=1,
             grid=(NY,),
-            in_specs=[whole(a) for a in args],
+            in_specs=[whole(normed_p), whole(normed_q), whole(p[0])]
+            + [pl.BlockSpec(memory_space=pl.ANY)] * 3
+            + [pl.BlockSpec((256, 256), lambda i, y_ref: (i, 0))] * 4
+            + [whole(a) for a in args[-4:]],
             out_specs=(
                 pl.BlockSpec((1, rows, 256), query_block),
                 pl.BlockSpec((1, rows, 256), key_value_block),
             ),
-            scratch_shapes=[pltpu.VMEM((rows, 256), jnp.float32)],
+            scratch_shapes=[pltpu.VMEM((rows, 256), jnp.float32)]
+            + [pltpu.VMEM((1024, 256), jnp.bfloat16)] * 3
+            + [pltpu.SemaphoreType.DMA((3,))],
         ),
         compiler_params=pltpu.CompilerParams(
             dimension_semantics=("arbitrary",), vmem_limit_bytes=VMEM_LIMIT
@@ -308,7 +322,7 @@
         out_ref[:, pl.ds(pl.multiple_of(c * 1024, 1024), 1024)] = total.astype(jnp.bfloat16)
 
 
-def output_projection(x, core, mine, other, strips, strips_other):
+def output_projection(place_xc, mine, other, strips, strips_other):
     rows = mine.shape[0]
     vmem = pl.BlockSpec(memory_space=pltpu.VMEM)
     args = [mine, other, *strips, *strips_other]
@@ -323,7 +337,7 @@
             flops=2 * rows * 1024 * 2048, transcendentals=0, bytes_accessed=6 << 20
         ),
         name="output_projection",
-    )(jnp.stack([x, core]), *args)
+    )(place_xc, *args)
 
 
 GROUP_ZC = [[place(x, z, c) for z in range(NZ) for c in range(NC)] for x in range(NX)]
@@ -426,9 +440,12 @@
 
     under = (normed_p, normed_q, cosine, sine, bias, gains)
     pieces = ([p0, p1, p2, p3], [q0, q1, q2, q3])
+    place_xc = jnp.stack([x, core])
 
     out_mine = lax.dynamic_slice_in_dim(out_strip, core * 1024, 1024, 1)
-    out_mine, pieces, under = lax.optimization_barrier((out_mine, pieces, under))
+    out_mine, pieces, under, place_xc = lax.optimization_barrier(
+        (out_mine, pieces, under, place_xc)
+    )
     normed_p, normed_q, cosine, sine, bias, gains = under
     strip_3 = from_tok(out_mine, dx=3)
     strips = [out_mine] + [from_tok(out_mine, dx=d) for d in (1, 2)]
@@ -444,7 +461,7 @@
     strip_3, mine = lax.optimization_barrier((strip_3, mine))
     strips.append(strip_3)
     strips_other.append(from_tok(strip_3, dc=1))
-    projected = output_projection(x, core, mine, got, strips, strips_other)
+    projected = output_projection(place_xc, mine, got, strips, strips_other)
     cache = in_core_order(core, kv[:, :rows], kv_got, 2)
     return (projected[None], cache[0][None], cache[1][None])
 

time: 140 us -> 140 us (level)
  transfers between devices with their start and end apart: 28 -> 28, of which waited for: 8 -> 10; matrix products, arithmetic and copies ran while one was open for 9% -> 9% of each run, Pallas kernels for 20% -> 20%
where the time goes in v3:
time: 140 us; the launch traced here: 139 us
  starting transfers between devices  34.9 us (25%)
  Pallas kernels  32.5 us (23%)
  blocking collectives  22.5 us (16%)
  waiting for transfers between devices  20.5 us (15%)
  between operations  15.2 us (11%)
  other arithmetic  8.6 us (6%)
  local copies, waits for them, and re-layouts  5.01 us (4%)
    all_gather x1, blocking collectives, per_device(): both = lax.all_gather(first, 'tok', axis_index_groups=GROUP_ZC)  22.5 us
    ppermute x16, starting transfers between devices, from_tok(): return lax.ppermute(block, 'tok', route)  22.1 us
    ppermute x9, waiting for transfers between devices, from_grp(): return lax.ppermute(block, 'grp', [((y + dy) % NY, y) for y in range(NY)])  11.3 us
    ppermute x9, starting transfers between devices, from_grp(): return lax.ppermute(block, 'grp', [((y + dy) % NY, y) for y in range(NY)])  10.2 us
    ppermute x16, waiting for transfers between devices, from_tok(): return lax.ppermute(block, 'tok', route)  9.23 us
    pallas_call x1, Pallas kernels, prefix_attention(): pl.pallas_call(functools.partial(prefix_kernel, scale), out_shape=(out, o...  8.81 us
    pallas_call x1, Pallas kernels, joint_projection(): pl.pallas_call(qkv_kernel, out_shape=(out, out), grid_spec=pltpu.Prefetch...  7.8 us
    pallas_call x1, Pallas kernels, suffix_attention(): pl.pallas_call(functools.partial(suffix_kernel, scale), out_shape=(out, o...  7.37 us
  transfers between devices with their start and end apart: 28, of which 10 were waited for; matrix products, arithmetic and copies ran while one was open for 9% of the time, Pallas kernels for 20%

profile of v3, /device:TPU:23, one launch (start us, length us, event | category | flops | bytes accessed | tf_op | source)
XLA Modules:
  0.0 139.3 jit_solution(1841695380972081120)
XLA Ops:
  7.2 0.8 collective-permute-start.3
  8.2 2.6 %collective-permute-start.1 = (bf16[32,1024]{1,0:T(8,128)(2,1)}, bf16[32,1024]{1,0:T(8,128)(2,1)S(1)}, u32[]{:S(2)}, u32[]{:S(2)}) collective-permute-start(bf16[32,1024]{1,0:T(8,128)(2,1)} %bitcast.42), channel_id=1, source_target_pairs={{128,0},{192,64},{0,128},{64,192},{129,1},{193,65},{1,129},{65,193... | collective-permute-start | bytes 196616 | tf_op jit(solution)/shard_map/ppermute | solution.py:34
  10.9 0.7 constant_dynamic-slice_fusion.9
  11.6 0.7 add_convert_fusion
  12.3 22.5 %all-gather = bf16[640,512]{1,0:T(8,128)(2,1)S(1)} all-gather(bf16[40,512]{1,0:T(8,128)(2,1)S(1)} %fusion.19), channel_id=2, replica_groups={{0,1,2,3,4,5,6,7,8,9,10,11,12,13,14,15},{16,17,18,19,20,21,22,23,24,25,..., dimensions={0}, use_global_device_ids=true | all-gather | bytes 696320 | tf_op jit(solution)/shard_map/all_gather | solution.py:374
  34.8 1.2 dynamic_slice.39
  37.1 1.9 %collective-permute-start.7 = (bf16[264,256]{1,0:T(8,128)(2,1)S(1)}, bf16[264,256]{1,0:T(8,128)(2,1)S(1)}, u32[]{:S(2)}, u32[]{:S(2)}) collective-permute-start(bf16[264,256]{1,0:T(8,128)(2,1)S(1)} %concatenate.61), channel_id=1, source_target_pairs={{64,0},{128,64},{192,128},{0,192},{65,1},{129,65},{193,129},{1,193... | collective-permute-start | bytes 405512 | tf_op jit(solution)/shard_map/ppermute | solution.py:34
  39.1 0.6 collective-permute-start.4
  39.7 0.8 collective-permute-start.5
  40.5 1.8 %collective-permute-start.6 = (bf16[392,256]{1,0:T(8,128)(2,1)S(1)}, bf16[392,256]{1,0:T(8,128)(2,1)S(1)}, u32[]{:S(2)}, u32[]{:S(2)}) collective-permute-start(bf16[392,256]{1,0:T(8,128)(2,1)S(1)} %constant_dynamic-update-slice_fusion), channel_id=1, source_target_pairs={{48,0},{49,1},{50,2},{51,3},{52,4},{53,5},{54,6},{55,7},{56,8},{57... | collective-permute-start | bytes 602120 | tf_op jit(solution)/shard_map/ppermute | solution.py:30
  42.4 1.4 collective-permute-start.8
  43.7 1.0 collective-permute-start.9
  44.8 3.3 %collective-permute-done.8 = bf16[264,256]{1,0:T(8,128)(2,1)S(1)} collective-permute-done((bf16[264,256]{1,0:T(8,128)(2,1)S(1)}, bf16[264,256]{1,0:T(8,128)(2,1)S(1)}, u32[]{:S(2)}, u32[]{:S(2)}) %collective-permute-start.8) | collective-permute-done | bytes 135200 | tf_op jit(solution)/shard_map/ppermute | solution.py:34
  48.1 3.6 %collective-permute-done.9 = bf16[264,256]{1,0:T(8,128)(2,1)S(1)} collective-permute-done((bf16[264,256]{1,0:T(8,128)(2,1)S(1)}, bf16[264,256]{1,0:T(8,128)(2,1)S(1)}, u32[]{:S(2)}, u32[]{:S(2)}) %collective-permute-start.9) | collective-permute-done | bytes 135200 | tf_op jit(solution)/shard_map/ppermute | solution.py:34
  51.7 0.7 maximum_maximum_fusion
  52.6 0.7 pad_add_fusion.place_ref
  53.5 1.0 collective-permute-start.11
  54.5 2.0 %collective-permute-start.12 = (bf16[1024,256]{1,0:T(8,128)(2,1)S(1)}, bf16[1024,256]{1,0:T(8,128)(2,1)}, u32[]{:S(2)}, u32[]{:S(2)}) collective-permute-start(bf16[1024,256]{1,0:T(8,128)(2,1)S(1)} %pad_maximum_fusion.1.p0), channel_id=1, source_target_pairs={{192,0},{0,64},{64,128},{128,192},{193,1},{1,65},{65,129},{129,193... | collective-permute-start | bytes 1572872 | tf_op jit(solution)/shard_map/ppermute | solution.py:34
  56.6 1.6 %collective-permute-start.13 = (bf16[1024,256]{1,0:T(8,128)(2,1)S(1)}, bf16[1024,256]{1,0:T(8,128)(2,1)S(1)}, u32[]{:S(2)}, u32[]{:S(2)}) collective-permute-start(bf16[1024,256]{1,0:T(8,128)(2,1)S(1)} %pad_maximum_fusion.2.q0), channel_id=1, source_target_pairs={{16,0},{17,1},{18,2},{19,3},{20,4},{21,5},{22,6},{23,7},{24,8},{25... | collective-permute-start | bytes 1572872 | tf_op jit(solution)/shard_map/ppermute | solution.py:30
  58.2 3.1 %collective-permute-start.14 = (bf16[1024,256]{1,0:T(8,128)(2,1)S(1)}, bf16[1024,256]{1,0:T(8,128)(2,1)S(1)}, u32[]{:S(2)}, u32[]{:S(2)}) collective-permute-start(bf16[1024,256]{1,0:T(8,128)(2,1)S(1)} %pad_maximum_fusion.2.q0), channel_id=1, source_target_pairs={{32,0},{33,1},{34,2},{35,3},{36,4},{37,5},{38,6},{39,7},{40,8},{41... | collective-permute-start | bytes 1572872 | tf_op jit(solution)/shard_map/ppermute | solution.py:30
  61.7 1.0 fusion.13
  63.0 3.0 %collective-permute-done.10.p1 = bf16[1024,256]{1,0:T(8,128)(2,1)S(1)} collective-permute-done((bf16[1024,256]{1,0:T(8,128)(2,1)S(1)}, bf16[1024,256]{1,0:T(8,128)(2,1)S(1)}, u32[]{:S(2)}, u32[]{:S(2)}) %collective-permute-start.10) | collective-permute-done | bytes 524320 | tf_op jit(solution)/shard_map/ppermute | solution.py:34
  66.0 3.5 %collective-permute-start.15 = (bf16[1024,256]{1,0:T(8,128)(2,1)S(1)}, bf16[1024,256]{1,0:T(8,128)(2,1)}, u32[]{:S(2)}, u32[]{:S(2)}) collective-permute-start(bf16[1024,256]{1,0:T(8,128)(2,1)S(1)} %pad_maximum_fusion.2.q0), channel_id=1, source_target_pairs={{48,0},{49,1},{50,2},{51,3},{52,4},{53,5},{54,6},{55,7},{56,8},{57... | collective-permute-start | bytes 1572872 | tf_op jit(solution)/shard_map/ppermute | solution.py:30
  69.5 0.8 pad_maximum_fusion.4.cos_ref
  70.3 0.8 pad_maximum_fusion.5.sin_ref
  71.2 1.0 pad_maximum_fusion.bias_ref
  72.2 0.6 broadcast_in_dim.50.gain_ref
  72.8 4.0 %input_norm.1 = (bf16[512,1024]{1,0:T(8,128)(2,1)}, bf16[512,1024]{1,0:T(8,128)(2,1)}) custom-call(s32[1]{0:T(128)} %bitcast.12.x_ref, bf16[256,2048]{1,0:T(8,128)(2,1)} %bitcast.37, bf16[256,2048]{1,0:T(8,128)(2,1)} %copy-done.4, bf16[1,2048]{1,0:T(2,128)(2,1)} %broadcast_in_dim.50.gain_ref), custom_call_target="tpu_custom_call" | custom-call | tf_op jit(solution)/shard_map/input_norm/pallas_call | solution.py:68
  76.8 1.1 constant_dynamic-slice_fusion.10.refs_0_
  77.9 1.4 %collective-permute-done.12.p3 = bf16[1024,256]{1,0:T(8,128)(2,1)} collective-permute-done((bf16[1024,256]{1,0:T(8,128)(2,1)S(1)}, bf16[1024,256]{1,0:T(8,128)(2,1)}, u32[]{:S(2)}, u32[]{:S(2)}) %collective-permute-start.12) | collective-permute-done | bytes 524320 | tf_op jit(solution)/shard_map/ppermute | solution.py:34
  79.4 3.7 %collective-permute-done.14.q2 = bf16[1024,256]{1,0:T(8,128)(2,1)S(1)} collective-permute-done((bf16[1024,256]{1,0:T(8,128)(2,1)S(1)}, bf16[1024,256]{1,0:T(8,128)(2,1)S(1)}, u32[]{:S(2)}, u32[]{:S(2)}) %collective-permute-start.14) | collective-permute-done | bytes 524320 | tf_op jit(solution)/shard_map/ppermute | solution.py:30
  83.1 1.3 collective-permute-start.18
  84.4 2.6 %collective-permute-start.19 = (bf16[256,1024]{1,0:T(8,128)(2,1)S(1)}, bf16[256,1024]{1,0:T(8,128)(2,1)S(1)}, u32[]{:S(2)}, u32[]{:S(2)}) collective-permute-start(bf16[256,1024]{1,0:T(8,128)(2,1)S(1)} %constant_dynamic-slice_fusion.10.refs_0_), channel_id=1, source_target_pairs={{32,0},{33,1},{34,2},{35,3},{36,4},{37,5},{38,6},{39,7},{40,8},{41... | collective-permute-start | bytes 1572872 | tf_op jit(solution)/shard_map/ppermute | solution.py:30
  87.0 7.8 %joint_projection.1 = (bf16[2,512,256]{2,1,0:T(8,128)(2,1)}, bf16[2,512,256]{2,1,0:T(8,128)(2,1)}) custom-call(s32[1]{0:T(128)} %bitcast.24.y_ref, bf16[512,1024]{1,0:T(8,128)(2,1)} %get-tuple-element.80.np_ref, bf16[512,1024]{1,0:T(8,128)(2,1)} %get-tuple-element.81.nq_ref, bf16[1024,256]{1,0:T(8,128)(2,1)} %copy-done.8, bf16[1024,256]{1,0:T(8,128)(2,1)} %copy-done.13, ...), custom_call_target="tpu_custom_call" | custom-call | flops 2147483648 | bytes 8388608 | tf_op jit(solution)/shard_map/joint_projection/pallas_call | solution.py:146
  94.8 2.6 %collective-permute-start.17 = (bf16[2,512,256]{2,1,0:T(8,128)(2,1)}, bf16[2,512,256]{2,1,0:T(8,128)(2,1)S(1)}, u32[]{:S(2)}, u32[]{:S(2)}) collective-permute-start(bf16[2,512,256]{2,1,0:T(8,128)(2,1)} %get-tuple-element.108.ko_ref.vo_ref), channel_id=1, source_target_pairs={{0,2},{1,3},{2,4},{3,5},{4,6},{5,7},{6,8},{7,9},{8,10},{9,11},{10,... | collective-permute-start | bytes 1572872 | tf_op jit(solution)/shard_map/ppermute | solution.py:40
  97.4 0.5 collective-permute-start.16
  97.9 8.8 %prefix_attention.1 = (f32[4,512,128]{2,1,0:T(8,128)}, f32[4,512,128]{2,1,0:T(8,128)}) custom-call(s32[1]{0:T(128)} %bitcast.23.core_ref, bf16[2,512,256]{2,1,0:T(8,128)(2,1)} %get-tuple-element.94.q_ref, bf16[2048,1024]{1,0:T(8,128)(2,1)} %all-gather.6.cloned.1.call-done.k_ref.v_ref, bf16[2048,1024]{1,0:T(8,128)(2,1)} %all-gather.6.cloned.1.call-done.k_ref.v_ref), custom_call_target="tpu_custom_call" | custom-call | flops 2147483648 | bytes 4194304 | tf_op jit(solution)/shard_map/prefix_attention/pallas_call | solution.py:220
  106.8 1.6 %collective-permute-done.19.refs_2_ = bf16[256,1024]{1,0:T(8,128)(2,1)S(1)} collective-permute-done((bf16[256,1024]{1,0:T(8,128)(2,1)S(1)}, bf16[256,1024]{1,0:T(8,128)(2,1)S(1)}, u32[]{:S(2)}, u32[]{:S(2)}) %collective-permute-start.19) | collective-permute-done | bytes 524320 | tf_op jit(solution)/shard_map/ppermute | solution.py:30
  108.4 2.6 %collective-permute-start.25 = (bf16[2,512,256]{2,1,0:T(8,128)(2,1)S(1)}, bf16[2,512,256]{2,1,0:T(8,128)(2,1)}, u32[]{:S(2)}, u32[]{:S(2)}) collective-permute-start(bf16[2,512,256]{2,1,0:T(8,128)(2,1)S(1)} %copy-done), channel_id=1, source_target_pairs={{1,0},{0,1},{3,2},{2,3},{5,4},{4,5},{7,6},{6,7},{9,8},{8,9},{11,10... | collective-permute-start | bytes 1572872 | tf_op jit(solution)/shard_map/ppermute | solution.py:30
  111.1 0.8 copy-done.3
  111.9 7.4 %suffix_attention.1 = (bf16[256,512]{1,0:T(8,128)(2,1)}, bf16[256,512]{1,0:T(8,128)(2,1)}) custom-call(s32[1]{0:T(128)} %bitcast.23.core_ref, bf16[2,512,256]{2,1,0:T(8,128)(2,1)} %get-tuple-element.94.q_ref, bf16[2,512,256]{2,1,0:T(8,128)(2,1)} %get-tuple-element.108.ko_ref.vo_ref, bf16[2,512,256]{2,1,0:T(8,128)(2,1)} %get-tuple-element.108.ko_ref.vo_ref, ...), custom_call_target="tpu_custom_call" | custom-call | flops 805306368 | bytes 4194304 | tf_op jit(solution)/shard_map/suffix_attention/pallas_call | solution.py:282
  119.2 2.3 %collective-permute-done.16.refs_3_ = bf16[256,1024]{1,0:T(8,128)(2,1)} collective-permute-done((bf16[256,1024]{1,0:T(8,128)(2,1)S(1)}, bf16[256,1024]{1,0:T(8,128)(2,1)}, u32[]{:S(2)}, u32[]{:S(2)}) %collective-permute-start.16) | collective-permute-done | bytes 524320 | tf_op jit(solution)/shard_map/ppermute | solution.py:30
  121.5 1.9 %collective-permute-start.21 = (bf16[256,1024]{1,0:T(8,128)(2,1)S(1)}, bf16[256,1024]{1,0:T(8,128)(2,1)S(1)}, u32[]{:S(2)}, u32[]{:S(2)}) collective-permute-start(bf16[256,1024]{1,0:T(8,128)(2,1)S(1)} %constant_dynamic-slice_fusion.10.refs_0_), channel_id=1, source_target_pairs={{1,0},{0,1},{3,2},{2,3},{5,4},{4,5},{7,6},{6,7},{9,8},{8,9},{11,10... | collective-permute-start | bytes 1572872 | tf_op jit(solution)/shard_map/ppermute | solution.py:30
  124.4 1.0 broadcast_select_fusion
  125.4 0.8 pad_maximum_fusion.3
  126.2 0.7 collective-permute-done.20.other_ref
  127.0 0.7 collective-permute-done.23.refs_6_
  127.9 4.6 %output_projection.1 = bf16[256,2048]{1,0:T(8,128)(2,1)} custom-call(s32[2]{0:T(128)} %pad_add_fusion.place_ref, bf16[256,512]{1,0:T(8,128)(2,1)} %get-tuple-element.102.mine_ref, bf16[256,512]{1,0:T(8,128)(2,1)} %copy-done.10, bf16[256,1024]{1,0:T(8,128)(2,1)} %copy-done.2, bf16[256,1024]{1,0:T(8,128)(2,1)} %copy-done.5, bf16[256,1024]{1,0:T(8,128)(2,1)} %copy-done.6, ...), custom_call_target="tpu_custom_call" | custom-call | flops 1073741824 | bytes 6291456 | tf_op jit(solution)/shard_map/output_projection/pallas_call | solution.py:329
  (97 shorter events, 3.2 us)
Async XLA Ops:
  7.2 31.8 %copy-start.11 = (bf16[1,32,1024]{2,1,0:T(8,128)(2,1)S(1)}, bf16[1,32,1024]{2,1,0:T(8,128)(2,1)}, u32[]{:S(2)}) copy-start(bf16[1,32,1024]{2,1,0:T(8,128)(2,1)} %param.11) | copy-start | bytes 196612
  7.2 69.7 %all-gather.4.cloned.1.call-start = ((), (), s32[]{:S(2)}) async-start(), calls=%async_computation | async-start | bytes 1114112 | tf_op jit(solution)/shard_map/all_gather | solution.py:358
  7.2 29.5 %collective-permute-start.3 = (bf16[256,2048]{1,0:T(8,128)(2,1)}, bf16[256,2048]{1,0:T(8,128)(2,1)S(1)}, u32[]{:S(2)}, u32[]{:S(2)}) collective-permute-start(bf16[256,2048]{1,0:T(8,128)(2,1)} %bitcast.36), channel_id=1, source_target_pairs={{1,0},{0,1},{3,2},{2,3},{5,4},{4,5},{7,6},{6,7},{9,8},{8,9},{11,10... | collective-permute-start | bytes 3145736 | tf_op jit(solution)/shard_map/ppermute | solution.py:30
  8.0 28.7 %collective-permute-start = (bf16[32,1024]{1,0:T(8,128)(2,1)}, bf16[32,1024]{1,0:T(8,128)(2,1)S(1)}, u32[]{:S(2)}, u32[]{:S(2)}) collective-permute-start(bf16[32,1024]{1,0:T(8,128)(2,1)} %bitcast.41), channel_id=1, source_target_pairs={{64,0},{128,64},{192,128},{0,192},{65,1},{129,65},{193,129},{1,193... | collective-permute-start | bytes 196616 | tf_op jit(solution)/shard_map/ppermute | solution.py:34
  8.2 28.5 %collective-permute-start.1 = (bf16[32,1024]{1,0:T(8,128)(2,1)}, bf16[32,1024]{1,0:T(8,128)(2,1)S(1)}, u32[]{:S(2)}, u32[]{:S(2)}) collective-permute-start(bf16[32,1024]{1,0:T(8,128)(2,1)} %bitcast.42), channel_id=1, source_target_pairs={{128,0},{192,64},{0,128},{64,192},{129,1},{193,65},{1,129},{65,193... | collective-permute-start | bytes 196616 | tf_op jit(solution)/shard_map/ppermute | solution.py:34
  10.8 25.9 %collective-permute-start.2 = (bf16[32,1024]{1,0:T(8,128)(2,1)}, bf16[32,1024]{1,0:T(8,128)(2,1)S(1)}, u32[]{:S(2)}, u32[]{:S(2)}) collective-permute-start(bf16[32,1024]{1,0:T(8,128)(2,1)} %bitcast.43), channel_id=1, source_target_pairs={{192,0},{0,64},{64,128},{128,192},{193,1},{1,65},{65,129},{129,193... | collective-permute-start | bytes 196616 | tf_op jit(solution)/shard_map/ppermute | solution.py:34
  10.8 87.1 %all-gather.6.cloned.1.call-start = ((), (), s32[]{:S(2)}) async-start(), calls=%async_computation.1 | async-start | bytes 4456448 | tf_op jit(solution)/shard_map/all_gather | solution.py:406
  36.7 19.8 %copy-start.4 = (bf16[256,2048]{1,0:T(8,128)(2,1)}, bf16[256,2048]{1,0:T(8,128)(2,1)S(1)}, u32[]{:S(2)}) copy-start(bf16[256,2048]{1,0:T(8,128)(2,1)S(1)} %collective-permute-done.3.peer_ref) | copy-start | bytes 3145732
  37.1 6.7 %collective-permute-start.7 = (bf16[264,256]{1,0:T(8,128)(2,1)S(1)}, bf16[264,256]{1,0:T(8,128)(2,1)S(1)}, u32[]{:S(2)}, u32[]{:S(2)}) collective-permute-start(bf16[264,256]{1,0:T(8,128)(2,1)S(1)} %concatenate.61), channel_id=1, source_target_pairs={{64,0},{128,64},{192,128},{0,192},{65,1},{129,65},{193,129},{1,193... | collective-permute-start | bytes 405512 | tf_op jit(solution)/shard_map/ppermute | solution.py:34
  39.1 12.6 %collective-permute-start.4 = (bf16[392,256]{1,0:T(8,128)(2,1)S(1)}, bf16[392,256]{1,0:T(8,128)(2,1)S(1)}, u32[]{:S(2)}, u32[]{:S(2)}) collective-permute-start(bf16[392,256]{1,0:T(8,128)(2,1)S(1)} %constant_dynamic-update-slice_fusion), channel_id=1, source_target_pairs={{16,0},{17,1},{18,2},{19,3},{20,4},{21,5},{22,6},{23,7},{24,8},{25... | collective-permute-start | bytes 602120 | tf_op jit(solution)/shard_map/ppermute | solution.py:30
  39.7 12.0 %collective-permute-start.5 = (bf16[392,256]{1,0:T(8,128)(2,1)S(1)}, bf16[392,256]{1,0:T(8,128)(2,1)S(1)}, u32[]{:S(2)}, u32[]{:S(2)}) collective-permute-start(bf16[392,256]{1,0:T(8,128)(2,1)S(1)} %constant_dynamic-update-slice_fusion), channel_id=1, source_target_pairs={{32,0},{33,1},{34,2},{35,3},{36,4},{37,5},{38,6},{39,7},{40,8},{41... | collective-permute-start | bytes 602120 | tf_op jit(solution)/shard_map/ppermute | solution.py:30
  40.5 11.1 %collective-permute-start.6 = (bf16[392,256]{1,0:T(8,128)(2,1)S(1)}, bf16[392,256]{1,0:T(8,128)(2,1)S(1)}, u32[]{:S(2)}, u32[]{:S(2)}) collective-permute-start(bf16[392,256]{1,0:T(8,128)(2,1)S(1)} %constant_dynamic-update-slice_fusion), channel_id=1, source_target_pairs={{48,0},{49,1},{50,2},{51,3},{52,4},{53,5},{54,6},{55,7},{56,8},{57... | collective-permute-start | bytes 602120 | tf_op jit(solution)/shard_map/ppermute | solution.py:30
  42.4 5.7 %collective-permute-start.8 = (bf16[264,256]{1,0:T(8,128)(2,1)S(1)}, bf16[264,256]{1,0:T(8,128)(2,1)S(1)}, u32[]{:S(2)}, u32[]{:S(2)}) collective-permute-start(bf16[264,256]{1,0:T(8,128)(2,1)S(1)} %concatenate.61), channel_id=1, source_target_pairs={{128,0},{192,64},{0,128},{64,192},{129,1},{193,65},{1,129},{65,193... | collective-permute-start | bytes 405512 | tf_op jit(solution)/shard_map/ppermute | solution.py:34
  43.7 7.9 %collective-permute-start.9 = (bf16[264,256]{1,0:T(8,128)(2,1)S(1)}, bf16[264,256]{1,0:T(8,128)(2,1)S(1)}, u32[]{:S(2)}, u32[]{:S(2)}) collective-permute-start(bf16[264,256]{1,0:T(8,128)(2,1)S(1)} %concatenate.61), channel_id=1, source_target_pairs={{192,0},{0,64},{64,128},{128,192},{193,1},{1,65},{65,129},{129,193... | collective-permute-start | bytes 405512 | tf_op jit(solution)/shard_map/ppermute | solution.py:34
  53.4 23.4 %copy-start.8 = (bf16[1024,256]{1,0:T(8,128)(2,1)}, bf16[1024,256]{1,0:T(8,128)(2,1)S(1)}, u32[]{:S(2)}) copy-start(bf16[1024,256]{1,0:T(8,128)(2,1)S(1)} %pad_maximum_fusion.1.p0) | copy-start | bytes 1572868
  53.4 18.9 %copy-start.12 = (bf16[2048]{0:T(1024)(128)(2,1)S(1)}, bf16[2048]{0:T(1024)(128)(2,1)}, u32[]{:S(2)}) copy-start(bf16[2048]{0:T(1024)(128)(2,1)} %param.13) | copy-start | bytes 12292
  53.4 12.6 %collective-permute-start.10 = (bf16[1024,256]{1,0:T(8,128)(2,1)S(1)}, bf16[1024,256]{1,0:T(8,128)(2,1)S(1)}, u32[]{:S(2)}, u32[]{:S(2)}) collective-permute-start(bf16[1024,256]{1,0:T(8,128)(2,1)S(1)} %pad_maximum_fusion.1.p0), channel_id=1, source_target_pairs={{64,0},{128,64},{192,128},{0,192},{65,1},{129,65},{193,129},{1,193... | collective-permute-start | bytes 1572872 | tf_op jit(solution)/shard_map/ppermute | solution.py:34
  53.5 24.4 %collective-permute-start.11 = (bf16[1024,256]{1,0:T(8,128)(2,1)S(1)}, bf16[1024,256]{1,0:T(8,128)(2,1)}, u32[]{:S(2)}, u32[]{:S(2)}) collective-permute-start(bf16[1024,256]{1,0:T(8,128)(2,1)S(1)} %pad_maximum_fusion.1.p0), channel_id=1, source_target_pairs={{128,0},{192,64},{0,128},{64,192},{129,1},{193,65},{1,129},{65,193... | collective-permute-start | bytes 1572872 | tf_op jit(solution)/shard_map/ppermute | solution.py:34
  54.5 24.9 %collective-permute-start.12 = (bf16[1024,256]{1,0:T(8,128)(2,1)S(1)}, bf16[1024,256]{1,0:T(8,128)(2,1)}, u32[]{:S(2)}, u32[]{:S(2)}) collective-permute-start(bf16[1024,256]{1,0:T(8,128)(2,1)S(1)} %pad_maximum_fusion.1.p0), channel_id=1, source_target_pairs={{192,0},{0,64},{64,128},{128,192},{193,1},{1,65},{65,129},{129,193... | collective-permute-start | bytes 1572872 | tf_op jit(solution)/shard_map/ppermute | solution.py:34
  56.6 21.3 %copy-start.9 = (bf16[1024,256]{1,0:T(8,128)(2,1)}, bf16[1024,256]{1,0:T(8,128)(2,1)S(1)}, u32[]{:S(2)}) copy-start(bf16[1024,256]{1,0:T(8,128)(2,1)S(1)} %pad_maximum_fusion.2.q0) | copy-start | bytes 1572868
  56.6 22.8 %collective-permute-start.13 = (bf16[1024,256]{1,0:T(8,128)(2,1)S(1)}, bf16[1024,256]{1,0:T(8,128)(2,1)S(1)}, u32[]{:S(2)}, u32[]{:S(2)}) collective-permute-start(bf16[1024,256]{1,0:T(8,128)(2,1)S(1)} %pad_maximum_fusion.2.q0), channel_id=1, source_target_pairs={{16,0},{17,1},{18,2},{19,3},{20,4},{21,5},{22,6},{23,7},{24,8},{25... | collective-permute-start | bytes 1572872 | tf_op jit(solution)/shard_map/ppermute | solution.py:30
  58.2 24.9 %collective-permute-start.14 = (bf16[1024,256]{1,0:T(8,128)(2,1)S(1)}, bf16[1024,256]{1,0:T(8,128)(2,1)S(1)}, u32[]{:S(2)}, u32[]{:S(2)}) collective-permute-start(bf16[1024,256]{1,0:T(8,128)(2,1)S(1)} %pad_maximum_fusion.2.q0), channel_id=1, source_target_pairs={{32,0},{33,1},{34,2},{35,3},{36,4},{37,5},{38,6},{39,7},{40,8},{41... | collective-permute-start | bytes 1572872 | tf_op jit(solution)/shard_map/ppermute | solution.py:30
  66.0 5.2 %copy-start.13 = (bf16[1024,256]{1,0:T(8,128)(2,1)}, bf16[1024,256]{1,0:T(8,128)(2,1)S(1)}, u32[]{:S(2)}) copy-start(bf16[1024,256]{1,0:T(8,128)(2,1)S(1)} %collective-permute-done.10.p1) | copy-start | bytes 1572868
  66.0 17.1 %collective-permute-start.15 = (bf16[1024,256]{1,0:T(8,128)(2,1)S(1)}, bf16[1024,256]{1,0:T(8,128)(2,1)}, u32[]{:S(2)}, u32[]{:S(2)}) collective-permute-start(bf16[1024,256]{1,0:T(8,128)(2,1)S(1)} %pad_maximum_fusion.2.q0), channel_id=1, source_target_pairs={{48,0},{49,1},{50,2},{51,3},{52,4},{53,5},{54,6},{55,7},{56,8},{57... | collective-permute-start | bytes 1572872 | tf_op jit(solution)/shard_map/ppermute | solution.py:30
  77.9 43.6 %copy-start.2 = (bf16[256,1024]{1,0:T(8,128)(2,1)}, bf16[256,1024]{1,0:T(8,128)(2,1)S(1)}, u32[]{:S(2)}) copy-start(bf16[256,1024]{1,0:T(8,128)(2,1)S(1)} %constant_dynamic-slice_fusion.10.refs_0_) | copy-start | bytes 1572868
  79.4 7.6 %copy-start.14 = (bf16[1024,256]{1,0:T(8,128)(2,1)}, bf16[1024,256]{1,0:T(8,128)(2,1)S(1)}, u32[]{:S(2)}) copy-start(bf16[1024,256]{1,0:T(8,128)(2,1)S(1)} %collective-permute-done.13.q1) | copy-start | bytes 1572868
  83.1 3.9 %copy-start.15 = (bf16[1024,256]{1,0:T(8,128)(2,1)}, bf16[1024,256]{1,0:T(8,128)(2,1)S(1)}, u32[]{:S(2)}) copy-start(bf16[1024,256]{1,0:T(8,128)(2,1)S(1)} %collective-permute-done.14.q2) | copy-start | bytes 1572868
  83.1 23.7 %collective-permute-start.18 = (bf16[256,1024]{1,0:T(8,128)(2,1)S(1)}, bf16[256,1024]{1,0:T(8,128)(2,1)S(1)}, u32[]{:S(2)}, u32[]{:S(2)}) collective-permute-start(bf16[256,1024]{1,0:T(8,128)(2,1)S(1)} %constant_dynamic-slice_fusion.10.refs_0_), channel_id=1, source_target_pairs={{16,0},{17,1},{18,2},{19,3},{20,4},{21,5},{22,6},{23,7},{24,8},{25... | collective-permute-start | bytes 1572872 | tf_op jit(solution)/shard_map/ppermute | solution.py:30
  84.4 24.0 %collective-permute-start.19 = (bf16[256,1024]{1,0:T(8,128)(2,1)S(1)}, bf16[256,1024]{1,0:T(8,128)(2,1)S(1)}, u32[]{:S(2)}, u32[]{:S(2)}) collective-permute-start(bf16[256,1024]{1,0:T(8,128)(2,1)S(1)} %constant_dynamic-slice_fusion.10.refs_0_), channel_id=1, source_target_pairs={{32,0},{33,1},{34,2},{35,3},{36,4},{37,5},{38,6},{39,7},{40,8},{41... | collective-permute-start | bytes 1572872 | tf_op jit(solution)/shard_map/ppermute | solution.py:30
  94.8 16.3 %collective-permute-start.17 = (bf16[2,512,256]{2,1,0:T(8,128)(2,1)}, bf16[2,512,256]{2,1,0:T(8,128)(2,1)S(1)}, u32[]{:S(2)}, u32[]{:S(2)}) collective-permute-start(bf16[2,512,256]{2,1,0:T(8,128)(2,1)} %get-tuple-element.108.ko_ref.vo_ref), channel_id=1, source_target_pairs={{0,2},{1,3},{2,4},{3,5},{4,6},{5,7},{6,8},{7,9},{8,10},{9,11},{10,... | collective-permute-start | bytes 1572872 | tf_op jit(solution)/shard_map/ppermute | solution.py:40
  97.4 24.1 %collective-permute-start.16 = (bf16[256,1024]{1,0:T(8,128)(2,1)S(1)}, bf16[256,1024]{1,0:T(8,128)(2,1)}, u32[]{:S(2)}, u32[]{:S(2)}) collective-permute-start(bf16[256,1024]{1,0:T(8,128)(2,1)S(1)} %constant_dynamic-slice_fusion.10.refs_0_), channel_id=1, source_target_pairs={{48,0},{49,1},{50,2},{51,3},{52,4},{53,5},{54,6},{55,7},{56,8},{57... | collective-permute-start | bytes 1572872 | tf_op jit(solution)/shard_map/ppermute | solution.py:30
  97.9 10.5 %copy-start = (bf16[2,512,256]{2,1,0:T(8,128)(2,1)S(1)}, bf16[2,512,256]{2,1,0:T(8,128)(2,1)}, u32[]{:S(2)}) copy-start(bf16[2,512,256]{2,1,0:T(8,128)(2,1)} %get-tuple-element.108.ko_ref.vo_ref) | copy-start | bytes 1572868
  106.7 17.7 %copy-start.1 = (bf16[2,512,256]{2,1,0:T(8,128)(2,1)S(1)}, bf16[2,512,256]{2,1,0:T(8,128)(2,1)}, u32[]{:S(2)}) copy-start(bf16[2,512,256]{2,1,0:T(8,128)(2,1)} %get-tuple-element.108.ko_ref.vo_ref) | copy-start | bytes 1572868
  106.8 21.1 %copy-start.5 = (bf16[256,1024]{1,0:T(8,128)(2,1)}, bf16[256,1024]{1,0:T(8,128)(2,1)S(1)}, u32[]{:S(2)}) copy-start(bf16[256,1024]{1,0:T(8,128)(2,1)S(1)} %collective-permute-done.18.refs_1_) | copy-start | bytes 1572868
  108.4 19.4 %copy-start.6 = (bf16[256,1024]{1,0:T(8,128)(2,1)}, bf16[256,1024]{1,0:T(8,128)(2,1)S(1)}, u32[]{:S(2)}) copy-start(bf16[256,1024]{1,0:T(8,128)(2,1)S(1)} %collective-permute-done.19.refs_2_) | copy-start | bytes 1572868
  108.4 15.5 %collective-permute-start.25 = (bf16[2,512,256]{2,1,0:T(8,128)(2,1)S(1)}, bf16[2,512,256]{2,1,0:T(8,128)(2,1)}, u32[]{:S(2)}, u32[]{:S(2)}) collective-permute-start(bf16[2,512,256]{2,1,0:T(8,128)(2,1)S(1)} %copy-done), channel_id=1, source_target_pairs={{1,0},{0,1},{3,2},{2,3},{5,4},{4,5},{7,6},{6,7},{9,8},{8,9},{11,10... | collective-permute-start | bytes 1572872 | tf_op jit(solution)/shard_map/ppermute | solution.py:30
  111.1 0.8 copy-start.3
  121.5 5.4 %collective-permute-start.21 = (bf16[256,1024]{1,0:T(8,128)(2,1)S(1)}, bf16[256,1024]{1,0:T(8,128)(2,1)S(1)}, u32[]{:S(2)}, u32[]{:S(2)}) collective-permute-start(bf16[256,1024]{1,0:T(8,128)(2,1)S(1)} %constant_dynamic-slice_fusion.10.refs_0_), channel_id=1, source_target_pairs={{1,0},{0,1},{3,2},{2,3},{5,4},{4,5},{7,6},{6,7},{9,8},{8,9},{11,10... | collective-permute-start | bytes 1572872 | tf_op jit(solution)/shard_map/ppermute | solution.py:30
  123.4 3.6 %collective-permute-start.22 = (bf16[256,1024]{1,0:T(8,128)(2,1)S(1)}, bf16[256,1024]{1,0:T(8,128)(2,1)}, u32[]{:S(2)}, u32[]{:S(2)}) collective-permute-start(bf16[256,1024]{1,0:T(8,128)(2,1)S(1)} %collective-permute-done.18.refs_1_), channel_id=1, source_target_pairs={{1,0},{0,1},{3,2},{2,3},{5,4},{4,5},{7,6},{6,7},{9,8},{8,9},{11,10... | collective-permute-start | bytes 1572872 | tf_op jit(solution)/shard_map/ppermute | solution.py:30
  123.4 4.3 %collective-permute-start.23 = (bf16[256,1024]{1,0:T(8,128)(2,1)S(1)}, bf16[256,1024]{1,0:T(8,128)(2,1)}, u32[]{:S(2)}, u32[]{:S(2)}) collective-permute-start(bf16[256,1024]{1,0:T(8,128)(2,1)S(1)} %collective-permute-done.19.refs_2_), channel_id=1, source_target_pairs={{1,0},{0,1},{3,2},{2,3},{5,4},{4,5},{7,6},{6,7},{9,8},{8,9},{11,10... | collective-permute-start | bytes 1572872 | tf_op jit(solution)/shard_map/ppermute | solution.py:30
  123.9 4.0 %collective-permute-start.24 = (bf16[256,1024]{1,0:T(8,128)(2,1)}, bf16[256,1024]{1,0:T(8,128)(2,1)}, u32[]{:S(2)}, u32[]{:S(2)}) collective-permute-start(bf16[256,1024]{1,0:T(8,128)(2,1)} %collective-permute-done.16.refs_3_), channel_id=1, source_target_pairs={{1,0},{0,1},{3,2},{2,3},{5,4},{4,5},{7,6},{6,7},{9,8},{8,9},{11,10... | collective-permute-start | bytes 1572872 | tf_op jit(solution)/shard_map/ppermute | solution.py:30
  123.9 3.1 %collective-permute-start.20 = (bf16[256,512]{1,0:T(8,128)(2,1)}, bf16[256,512]{1,0:T(8,128)(2,1)S(1)}, u32[]{:S(2)}, u32[]{:S(2)}) collective-permute-start(bf16[256,512]{1,0:T(8,128)(2,1)} %get-tuple-element.103), channel_id=1, source_target_pairs={{1,0},{0,1},{3,2},{2,3},{5,4},{4,5},{7,6},{6,7},{9,8},{8,9},{11,10... | collective-permute-start | bytes 786440 | tf_op jit(solution)/shard_map/ppermute | solution.py:30
  127.0 0.9 copy-start.10
  127.0 0.9 copy-start.7
Sparse Core Ops, SparseCore 0:
  10.9 42.0 all-gather.3
  54.9 40.5 all-gather.5

commit v4 on v3

--- a/solution.py
+++ b/solution.py
@@ -340,6 +340,29 @@
     )(place_xc, *args)
 
 
+def choose_kernel(y_ref, owner_ref, *refs):
+    *owners, out_ref = refs
+    steps = (owner_ref[y_ref[0]] - y_ref[0] + NY) % NY
+    for k, owner in enumerate(owners):
+
+        @pl.when(steps == k)
+        def _(owner=owner):
+            for i in range(4):
+                out_ref[32 * i : 32 * (i + 1), :] = owner[:, i * 256 : (i + 1) * 256]
+
+
+def choose(y, prefix_owner, owners):
+    vmem = pl.BlockSpec(memory_space=pltpu.VMEM)
+    smem = pl.BlockSpec(memory_space=pltpu.SMEM)
+    return pl.pallas_call(
+        choose_kernel,
+        out_shape=jax.ShapeDtypeStruct((128, 256), jnp.bfloat16),
+        in_specs=[smem, smem] + [vmem] * NY,
+        out_specs=vmem,
+        name="choose",
+    )(y, prefix_owner, *owners)
+
+
 GROUP_ZC = [[place(x, z, c) for z in range(NZ) for c in range(NC)] for x in range(NX)]
 
 
@@ -357,7 +380,6 @@
     own = hidden_in[0]
     out_strip = lax.all_gather(w_out, "tok", axis_index_groups=GROUP_ZC, tiled=True)
     owners = [prefix_kv[0]] + [from_grp(prefix_kv[0], d) for d in range(1, NY)]
-    owner = (prefix_owner[y] - y) % NY
 
     def columns(c):
         start = jnp.where(y < 2, 512 * c + 256 * y, 512 * y + 256 * c)
@@ -379,10 +401,10 @@
 
     marks_x = both[:, 32, :256]
     strip = lax.dynamic_slice_in_dim(both[:, :32], core * 256, 256, 2).reshape(512, 256)
-    prefix_rows = lax.dynamic_index_in_dim(jnp.stack(owners), owner, 0, keepdims=False)
+    prefix_rows = choose(y[None], prefix_owner, owners)
     p_own = jnp.concatenate(
         [strip[:256]]
-        + [prefix_rows[:, i * 256 : (i + 1) * 256] for i in range(4)]
+        + [prefix_rows]
         + [jnp.pad(marks_x[14:], ((0, 6), (0, 0)))]
     )
     q_own = jnp.concatenate([strip[256:], jnp.zeros((8, 256), jnp.bfloat16)])

time: 140 us -> 140 us (level)
  Pallas kernels: 32.5 us -> 34.1 us
    pallas_call x0 -> x1, Pallas kernels: none -> 1.6 us  [choose(): pl.pallas_call(choose_kernel, out_shape=jax.ShapeDtypeStruct((128, 256),...]
  transfers between devices with their start and end apart: 28 -> 28, of which waited for: 10 -> 10; matrix products, arithmetic and copies ran while one was open for 9% -> 9% of each run, Pallas kernels for 20% -> 21%
where the time goes in v4:
time: 140 us
  starting transfers between devices  34.4 us (25%)
  Pallas kernels  34.1 us (24%)
  blocking collectives  22.5 us (16%)
  waiting for transfers between devices  21 us (15%)
  between operations  14.5 us (10%)
  other arithmetic  9.36 us (7%)
  local copies, waits for them, and re-layouts  3.76 us (3%)
    all_gather x1, blocking collectives, per_device(): both = lax.all_gather(first, 'tok', axis_index_groups=GROUP_ZC)  22.5 us
    ppermute x16, starting transfers between devices, from_tok(): return lax.ppermute(block, 'tok', route)  22 us
    ppermute x9, waiting for transfers between devices, from_grp(): return lax.ppermute(block, 'grp', [((y + dy) % NY, y) for y in range(NY)])  11.9 us
    ppermute x9, starting transfers between devices, from_grp(): return lax.ppermute(block, 'grp', [((y + dy) % NY, y) for y in range(NY)])  9.73 us
    ppermute x16, waiting for transfers between devices, from_tok(): return lax.ppermute(block, 'tok', route)  9.09 us
    pallas_call x1, Pallas kernels, prefix_attention(): pl.pallas_call(functools.partial(prefix_kernel, scale), out_shape=(out, o...  8.82 us
    pallas_call x1, Pallas kernels, joint_projection(): pl.pallas_call(qkv_kernel, out_shape=(out, out), grid_spec=pltpu.Prefetch...  7.8 us
    pallas_call x1, Pallas kernels, suffix_attention(): pl.pallas_call(functools.partial(suffix_kernel, scale), out_shape=(out, o...  7.37 us
  transfers between devices with their start and end apart: 28, of which 10 were waited for; matrix products, arithmetic and copies ran while one was open for 9% of the time, Pallas kernels for 21%

profile of v4, /device:TPU:23, one launch (start us, length us, event | category | flops | bytes accessed | tf_op | source)
XLA Modules:
  0.0 139.6 jit_solution(6873213550667310186)
XLA Ops:
  7.2 0.8 collective-permute-start.3
  8.2 2.6 %collective-permute-start.1 = (bf16[32,1024]{1,0:T(8,128)(2,1)}, bf16[32,1024]{1,0:T(8,128)(2,1)S(1)}, u32[]{:S(2)}, u32[]{:S(2)}) collective-permute-start(bf16[32,1024]{1,0:T(8,128)(2,1)} %bitcast.35), channel_id=1, source_target_pairs={{128,0},{192,64},{0,128},{64,192},{129,1},{193,65},{1,129},{65,193... | collective-permute-start | bytes 196616 | tf_op jit(solution)/shard_map/ppermute | solution.py:34
  10.9 0.7 constant_dynamic-slice_fusion.9
  11.6 0.7 add_convert_fusion
  12.3 22.5 %all-gather = bf16[640,512]{1,0:T(8,128)(2,1)S(1)} all-gather(bf16[40,512]{1,0:T(8,128)(2,1)S(1)} %fusion.17), channel_id=2, replica_groups={{0,1,2,3,4,5,6,7,8,9,10,11,12,13,14,15},{16,17,18,19,20,21,22,23,24,25,..., dimensions={0}, use_global_device_ids=true | all-gather | bytes 696320 | tf_op jit(solution)/shard_map/all_gather | solution.py:396
  35.1 1.9 %collective-permute-start.7 = (bf16[264,256]{1,0:T(8,128)(2,1)S(1)}, bf16[264,256]{1,0:T(8,128)(2,1)S(1)}, u32[]{:S(2)}, u32[]{:S(2)}) collective-permute-start(bf16[264,256]{1,0:T(8,128)(2,1)S(1)} %concatenate.61), channel_id=1, source_target_pairs={{64,0},{128,64},{192,128},{0,192},{65,1},{129,65},{193,129},{1,193... | collective-permute-start | bytes 405512 | tf_op jit(solution)/shard_map/ppermute | solution.py:34
  37.0 1.6 %choose.1 = bf16[128,256]{1,0:T(8,128)(2,1)} custom-call(s32[1]{0:T(128)} %bitcast.4.y_ref, s32[4]{0:T(128)} %owner_ref.1, bf16[32,1024]{1,0:T(8,128)(2,1)} %bitcast.37, bf16[32,1024]{1,0:T(8,128)(2,1)} %copy-done.11, bf16[32,1024]{1,0:T(8,128)(2,1)} %copy-done.12, bf16[32,1024]{1,0:T(8,128)(2,1)} %copy-done.13), custom_call_target="tpu_custom_call" | custom-call | tf_op jit(solution)/shard_map/choose/pallas_call | solution.py:357
  38.6 0.9 fusion.14
  39.5 0.6 collective-permute-start.4
  40.1 0.8 collective-permute-start.5
  40.9 1.8 %collective-permute-start.6 = (bf16[392,256]{1,0:T(8,128)(2,1)S(1)}, bf16[392,256]{1,0:T(8,128)(2,1)S(1)}, u32[]{:S(2)}, u32[]{:S(2)}) collective-permute-start(bf16[392,256]{1,0:T(8,128)(2,1)S(1)} %fusion.14), channel_id=1, source_target_pairs={{48,0},{49,1},{50,2},{51,3},{52,4},{53,5},{54,6},{55,7},{56,8},{57... | collective-permute-start | bytes 602120 | tf_op jit(solution)/shard_map/ppermute | solution.py:30
  42.8 1.4 collective-permute-start.8
  44.1 0.6 collective-permute-start.9
  44.8 3.7 %collective-permute-done.8 = bf16[264,256]{1,0:T(8,128)(2,1)S(1)} collective-permute-done((bf16[264,256]{1,0:T(8,128)(2,1)S(1)}, bf16[264,256]{1,0:T(8,128)(2,1)S(1)}, u32[]{:S(2)}, u32[]{:S(2)}) %collective-permute-start.8) | collective-permute-done | bytes 135200 | tf_op jit(solution)/shard_map/ppermute | solution.py:34
  48.5 3.6 %collective-permute-done.9 = bf16[264,256]{1,0:T(8,128)(2,1)S(1)} collective-permute-done((bf16[264,256]{1,0:T(8,128)(2,1)S(1)}, bf16[264,256]{1,0:T(8,128)(2,1)S(1)}, u32[]{:S(2)}, u32[]{:S(2)}) %collective-permute-start.9) | collective-permute-done | bytes 135200 | tf_op jit(solution)/shard_map/ppermute | solution.py:34
  52.1 0.7 maximum_maximum_fusion
  53.0 0.6 pad_add_fusion.place_ref
  53.9 1.3 collective-permute-start.11
  55.1 1.7 %collective-permute-start.12 = (bf16[1024,256]{1,0:T(8,128)(2,1)S(1)}, bf16[1024,256]{1,0:T(8,128)(2,1)}, u32[]{:S(2)}, u32[]{:S(2)}) collective-permute-start(bf16[1024,256]{1,0:T(8,128)(2,1)S(1)} %pad_maximum_fusion.1.p0), channel_id=1, source_target_pairs={{192,0},{0,64},{64,128},{128,192},{193,1},{1,65},{65,129},{129,193... | collective-permute-start | bytes 1572872 | tf_op jit(solution)/shard_map/ppermute | solution.py:34
  57.0 1.5 %collective-permute-start.13 = (bf16[1024,256]{1,0:T(8,128)(2,1)S(1)}, bf16[1024,256]{1,0:T(8,128)(2,1)S(1)}, u32[]{:S(2)}, u32[]{:S(2)}) collective-permute-start(bf16[1024,256]{1,0:T(8,128)(2,1)S(1)} %pad_maximum_fusion.2.q0), channel_id=1, source_target_pairs={{16,0},{17,1},{18,2},{19,3},{20,4},{21,5},{22,6},{23,7},{24,8},{25... | collective-permute-start | bytes 1572872 | tf_op jit(solution)/shard_map/ppermute | solution.py:30
  58.5 3.1 %collective-permute-start.14 = (bf16[1024,256]{1,0:T(8,128)(2,1)S(1)}, bf16[1024,256]{1,0:T(8,128)(2,1)}, u32[]{:S(2)}, u32[]{:S(2)}) collective-permute-start(bf16[1024,256]{1,0:T(8,128)(2,1)S(1)} %pad_maximum_fusion.2.q0), channel_id=1, source_target_pairs={{32,0},{33,1},{34,2},{35,3},{36,4},{37,5},{38,6},{39,7},{40,8},{41... | collective-permute-start | bytes 1572872 | tf_op jit(solution)/shard_map/ppermute | solution.py:30
  62.1 1.0 fusion.15
  63.4 3.0 %collective-permute-done.10.p1 = bf16[1024,256]{1,0:T(8,128)(2,1)S(1)} collective-permute-done((bf16[1024,256]{1,0:T(8,128)(2,1)S(1)}, bf16[1024,256]{1,0:T(8,128)(2,1)S(1)}, u32[]{:S(2)}, u32[]{:S(2)}) %collective-permute-start.10) | collective-permute-done | bytes 524320 | tf_op jit(solution)/shard_map/ppermute | solution.py:34
  66.4 3.5 %collective-permute-start.15 = (bf16[1024,256]{1,0:T(8,128)(2,1)S(1)}, bf16[1024,256]{1,0:T(8,128)(2,1)S(1)}, u32[]{:S(2)}, u32[]{:S(2)}) collective-permute-start(bf16[1024,256]{1,0:T(8,128)(2,1)S(1)} %pad_maximum_fusion.2.q0), channel_id=1, source_target_pairs={{48,0},{49,1},{50,2},{51,3},{52,4},{53,5},{54,6},{55,7},{56,8},{57... | collective-permute-start | bytes 1572872 | tf_op jit(solution)/shard_map/ppermute | solution.py:30
  69.8 0.8 pad_maximum_fusion.4.cos_ref
  70.7 0.8 pad_maximum_fusion.5.sin_ref
  71.6 1.0 pad_maximum_fusion.bias_ref
  73.2 4.0 %input_norm.1 = (bf16[512,1024]{1,0:T(8,128)(2,1)}, bf16[512,1024]{1,0:T(8,128)(2,1)}) custom-call(s32[1]{0:T(128)} %bitcast.7.x_ref, bf16[256,2048]{1,0:T(8,128)(2,1)} %bitcast.30, bf16[256,2048]{1,0:T(8,128)(2,1)} %copy-done.4, bf16[1,2048]{1,0:T(2,128)(2,1)} %broadcast_in_dim.52.gain_ref), custom_call_target="tpu_custom_call" | custom-call | tf_op jit(solution)/shard_map/input_norm/pallas_call | solution.py:68
  77.2 1.1 constant_dynamic-slice_fusion.10.refs_0_
  78.3 1.6 %collective-permute-done.12.p3 = bf16[1024,256]{1,0:T(8,128)(2,1)} collective-permute-done((bf16[1024,256]{1,0:T(8,128)(2,1)S(1)}, bf16[1024,256]{1,0:T(8,128)(2,1)}, u32[]{:S(2)}, u32[]{:S(2)}) %collective-permute-start.12) | collective-permute-done | bytes 524320 | tf_op jit(solution)/shard_map/ppermute | solution.py:34
  79.9 3.6 %collective-permute-done.14.q2 = bf16[1024,256]{1,0:T(8,128)(2,1)} collective-permute-done((bf16[1024,256]{1,0:T(8,128)(2,1)S(1)}, bf16[1024,256]{1,0:T(8,128)(2,1)}, u32[]{:S(2)}, u32[]{:S(2)}) %collective-permute-start.14) | collective-permute-done | bytes 524320 | tf_op jit(solution)/shard_map/ppermute | solution.py:30
  83.6 1.2 collective-permute-start.18
  84.8 2.6 %collective-permute-start.19 = (bf16[256,1024]{1,0:T(8,128)(2,1)S(1)}, bf16[256,1024]{1,0:T(8,128)(2,1)S(1)}, u32[]{:S(2)}, u32[]{:S(2)}) collective-permute-start(bf16[256,1024]{1,0:T(8,128)(2,1)S(1)} %constant_dynamic-slice_fusion.10.refs_0_), channel_id=1, source_target_pairs={{32,0},{33,1},{34,2},{35,3},{36,4},{37,5},{38,6},{39,7},{40,8},{41... | collective-permute-start | bytes 1572872 | tf_op jit(solution)/shard_map/ppermute | solution.py:30
  87.3 7.8 %joint_projection.1 = (bf16[2,512,256]{2,1,0:T(8,128)(2,1)}, bf16[2,512,256]{2,1,0:T(8,128)(2,1)}) custom-call(s32[1]{0:T(128)} %bitcast.4.y_ref, bf16[512,1024]{1,0:T(8,128)(2,1)} %get-tuple-element.80.np_ref, bf16[512,1024]{1,0:T(8,128)(2,1)} %get-tuple-element.81.nq_ref, bf16[1024,256]{1,0:T(8,128)(2,1)} %copy-done.8, bf16[1024,256]{1,0:T(8,128)(2,1)} %copy-done.15, ...), custom_call_target="tpu_custom_call" | custom-call | flops 2147483648 | bytes 8388608 | tf_op jit(solution)/shard_map/joint_projection/pallas_call | solution.py:146
  95.1 2.5 %collective-permute-start.17 = (bf16[2,512,256]{2,1,0:T(8,128)(2,1)}, bf16[2,512,256]{2,1,0:T(8,128)(2,1)S(1)}, u32[]{:S(2)}, u32[]{:S(2)}) collective-permute-start(bf16[2,512,256]{2,1,0:T(8,128)(2,1)} %get-tuple-element.108.ko_ref.vo_ref), channel_id=1, source_target_pairs={{0,2},{1,3},{2,4},{3,5},{4,6},{5,7},{6,8},{7,9},{8,10},{9,11},{10,... | collective-permute-start | bytes 1572872 | tf_op jit(solution)/shard_map/ppermute | solution.py:40
  97.7 0.6 collective-permute-start.16
  98.3 8.8 %prefix_attention.1 = (f32[4,512,128]{2,1,0:T(8,128)}, f32[4,512,128]{2,1,0:T(8,128)}) custom-call(s32[1]{0:T(128)} %bitcast.18.core_ref, bf16[2,512,256]{2,1,0:T(8,128)(2,1)} %get-tuple-element.94.q_ref, bf16[2048,1024]{1,0:T(8,128)(2,1)} %all-gather.6.cloned.1.call-done.k_ref.v_ref, bf16[2048,1024]{1,0:T(8,128)(2,1)} %all-gather.6.cloned.1.call-done.k_ref.v_ref), custom_call_target="tpu_custom_call" | custom-call | flops 2147483648 | bytes 4194304 | tf_op jit(solution)/shard_map/prefix_attention/pallas_call | solution.py:220
  107.1 1.8 %collective-permute-done.19.refs_2_ = bf16[256,1024]{1,0:T(8,128)(2,1)S(1)} collective-permute-done((bf16[256,1024]{1,0:T(8,128)(2,1)S(1)}, bf16[256,1024]{1,0:T(8,128)(2,1)S(1)}, u32[]{:S(2)}, u32[]{:S(2)}) %collective-permute-start.19) | collective-permute-done | bytes 524320 | tf_op jit(solution)/shard_map/ppermute | solution.py:30
  108.9 2.5 %collective-permute-start.25 = (bf16[2,512,256]{2,1,0:T(8,128)(2,1)S(1)}, bf16[2,512,256]{2,1,0:T(8,128)(2,1)}, u32[]{:S(2)}, u32[]{:S(2)}) collective-permute-start(bf16[2,512,256]{2,1,0:T(8,128)(2,1)S(1)} %copy-done), channel_id=1, source_target_pairs={{1,0},{0,1},{3,2},{2,3},{5,4},{4,5},{7,6},{6,7},{9,8},{8,9},{11,10... | collective-permute-start | bytes 1572872 | tf_op jit(solution)/shard_map/ppermute | solution.py:30
  111.4 0.8 copy-done.3
  112.2 7.4 %suffix_attention.1 = (bf16[256,512]{1,0:T(8,128)(2,1)}, bf16[256,512]{1,0:T(8,128)(2,1)}) custom-call(s32[1]{0:T(128)} %bitcast.18.core_ref, bf16[2,512,256]{2,1,0:T(8,128)(2,1)} %get-tuple-element.94.q_ref, bf16[2,512,256]{2,1,0:T(8,128)(2,1)} %get-tuple-element.108.ko_ref.vo_ref, bf16[2,512,256]{2,1,0:T(8,128)(2,1)} %get-tuple-element.108.ko_ref.vo_ref, ...), custom_call_target="tpu_custom_call" | custom-call | flops 805306368 | bytes 4194304 | tf_op jit(solution)/shard_map/suffix_attention/pallas_call | solution.py:282
  119.6 2.1 %collective-permute-done.16.refs_3_ = bf16[256,1024]{1,0:T(8,128)(2,1)} collective-permute-done((bf16[256,1024]{1,0:T(8,128)(2,1)S(1)}, bf16[256,1024]{1,0:T(8,128)(2,1)}, u32[]{:S(2)}, u32[]{:S(2)}) %collective-permute-start.16) | collective-permute-done | bytes 524320 | tf_op jit(solution)/shard_map/ppermute | solution.py:30
  121.7 1.9 %collective-permute-start.21 = (bf16[256,1024]{1,0:T(8,128)(2,1)S(1)}, bf16[256,1024]{1,0:T(8,128)(2,1)S(1)}, u32[]{:S(2)}, u32[]{:S(2)}) collective-permute-start(bf16[256,1024]{1,0:T(8,128)(2,1)S(1)} %constant_dynamic-slice_fusion.10.refs_0_), channel_id=1, source_target_pairs={{1,0},{0,1},{3,2},{2,3},{5,4},{4,5},{7,6},{6,7},{9,8},{8,9},{11,10... | collective-permute-start | bytes 1572872 | tf_op jit(solution)/shard_map/ppermute | solution.py:30
  124.7 1.0 broadcast_select_fusion
  125.7 0.8 pad_maximum_fusion.3
  126.5 0.7 collective-permute-done.20.other_ref
  127.3 0.7 collective-permute-done.23.refs_6_
  128.2 4.6 %output_projection.1 = bf16[256,2048]{1,0:T(8,128)(2,1)} custom-call(s32[2]{0:T(128)} %pad_add_fusion.place_ref, bf16[256,512]{1,0:T(8,128)(2,1)} %get-tuple-element.102.mine_ref, bf16[256,512]{1,0:T(8,128)(2,1)} %copy-done.10, bf16[256,1024]{1,0:T(8,128)(2,1)} %copy-done.2, bf16[256,1024]{1,0:T(8,128)(2,1)} %copy-done.5, bf16[256,1024]{1,0:T(8,128)(2,1)} %copy-done.6, ...), custom_call_target="tpu_custom_call" | custom-call | flops 1073741824 | bytes 6291456 | tf_op jit(solution)/shard_map/output_projection/pallas_call | solution.py:329
  (95 shorter events, 3.7 us)
Async XLA Ops:
  7.2 70.0 %all-gather.4.cloned.1.call-start = ((), (), s32[]{:S(2)}) async-start(), calls=%async_computation | async-start | bytes 1114112 | tf_op jit(solution)/shard_map/all_gather | solution.py:381
  7.2 27.6 %collective-permute-start.3 = (bf16[256,2048]{1,0:T(8,128)(2,1)}, bf16[256,2048]{1,0:T(8,128)(2,1)S(1)}, u32[]{:S(2)}, u32[]{:S(2)}) collective-permute-start(bf16[256,2048]{1,0:T(8,128)(2,1)} %bitcast.29), channel_id=1, source_target_pairs={{1,0},{0,1},{3,2},{2,3},{5,4},{4,5},{7,6},{6,7},{9,8},{8,9},{11,10... | collective-permute-start | bytes 3145736 | tf_op jit(solution)/shard_map/ppermute | solution.py:30
  8.0 26.8 %collective-permute-start = (bf16[32,1024]{1,0:T(8,128)(2,1)}, bf16[32,1024]{1,0:T(8,128)(2,1)S(1)}, u32[]{:S(2)}, u32[]{:S(2)}) collective-permute-start(bf16[32,1024]{1,0:T(8,128)(2,1)} %bitcast.34), channel_id=1, source_target_pairs={{64,0},{128,64},{192,128},{0,192},{65,1},{129,65},{193,129},{1,193... | collective-permute-start | bytes 196616 | tf_op jit(solution)/shard_map/ppermute | solution.py:34
  8.2 26.6 %collective-permute-start.1 = (bf16[32,1024]{1,0:T(8,128)(2,1)}, bf16[32,1024]{1,0:T(8,128)(2,1)S(1)}, u32[]{:S(2)}, u32[]{:S(2)}) collective-permute-start(bf16[32,1024]{1,0:T(8,128)(2,1)} %bitcast.35), channel_id=1, source_target_pairs={{128,0},{192,64},{0,128},{64,192},{129,1},{193,65},{1,129},{65,193... | collective-permute-start | bytes 196616 | tf_op jit(solution)/shard_map/ppermute | solution.py:34
  10.8 24.0 %collective-permute-start.2 = (bf16[32,1024]{1,0:T(8,128)(2,1)}, bf16[32,1024]{1,0:T(8,128)(2,1)S(1)}, u32[]{:S(2)}, u32[]{:S(2)}) collective-permute-start(bf16[32,1024]{1,0:T(8,128)(2,1)} %bitcast.36), channel_id=1, source_target_pairs={{192,0},{0,64},{64,128},{128,192},{193,1},{1,65},{65,129},{129,193... | collective-permute-start | bytes 196616 | tf_op jit(solution)/shard_map/ppermute | solution.py:34
  10.8 87.5 %all-gather.6.cloned.1.call-start = ((), (), s32[]{:S(2)}) async-start(), calls=%async_computation.1 | async-start | bytes 4456448 | tf_op jit(solution)/shard_map/all_gather | solution.py:428
  34.8 2.2 %copy-start.11 = (bf16[32,1024]{1,0:T(8,128)(2,1)}, bf16[32,1024]{1,0:T(8,128)(2,1)S(1)}, u32[]{:S(2)}) copy-start(bf16[32,1024]{1,0:T(8,128)(2,1)S(1)} %collective-permute-done.refs_1_) | copy-start | bytes 196612
  34.8 2.2 %copy-start.12 = (bf16[32,1024]{1,0:T(8,128)(2,1)}, bf16[32,1024]{1,0:T(8,128)(2,1)S(1)}, u32[]{:S(2)}) copy-start(bf16[32,1024]{1,0:T(8,128)(2,1)S(1)} %collective-permute-done.1.refs_2_) | copy-start | bytes 196612
  34.8 2.2 %copy-start.13 = (bf16[32,1024]{1,0:T(8,128)(2,1)}, bf16[32,1024]{1,0:T(8,128)(2,1)S(1)}, u32[]{:S(2)}) copy-start(bf16[32,1024]{1,0:T(8,128)(2,1)S(1)} %collective-permute-done.2.refs_3_) | copy-start | bytes 196612
  34.8 22.1 %copy-start.4 = (bf16[256,2048]{1,0:T(8,128)(2,1)}, bf16[256,2048]{1,0:T(8,128)(2,1)S(1)}, u32[]{:S(2)}) copy-start(bf16[256,2048]{1,0:T(8,128)(2,1)S(1)} %collective-permute-done.3.peer_ref) | copy-start | bytes 3145732
  35.1 9.0 %collective-permute-start.7 = (bf16[264,256]{1,0:T(8,128)(2,1)S(1)}, bf16[264,256]{1,0:T(8,128)(2,1)S(1)}, u32[]{:S(2)}, u32[]{:S(2)}) collective-permute-start(bf16[264,256]{1,0:T(8,128)(2,1)S(1)} %concatenate.61), channel_id=1, source_target_pairs={{64,0},{128,64},{192,128},{0,192},{65,1},{129,65},{193,129},{1,193... | collective-permute-start | bytes 405512 | tf_op jit(solution)/shard_map/ppermute | solution.py:34
  39.5 12.6 %collective-permute-start.4 = (bf16[392,256]{1,0:T(8,128)(2,1)S(1)}, bf16[392,256]{1,0:T(8,128)(2,1)S(1)}, u32[]{:S(2)}, u32[]{:S(2)}) collective-permute-start(bf16[392,256]{1,0:T(8,128)(2,1)S(1)} %fusion.14), channel_id=1, source_target_pairs={{16,0},{17,1},{18,2},{19,3},{20,4},{21,5},{22,6},{23,7},{24,8},{25... | collective-permute-start | bytes 602120 | tf_op jit(solution)/shard_map/ppermute | solution.py:30
  40.1 12.0 %collective-permute-start.5 = (bf16[392,256]{1,0:T(8,128)(2,1)S(1)}, bf16[392,256]{1,0:T(8,128)(2,1)S(1)}, u32[]{:S(2)}, u32[]{:S(2)}) collective-permute-start(bf16[392,256]{1,0:T(8,128)(2,1)S(1)} %fusion.14), channel_id=1, source_target_pairs={{32,0},{33,1},{34,2},{35,3},{36,4},{37,5},{38,6},{39,7},{40,8},{41... | collective-permute-start | bytes 602120 | tf_op jit(solution)/shard_map/ppermute | solution.py:30
  40.9 11.1 %collective-permute-start.6 = (bf16[392,256]{1,0:T(8,128)(2,1)S(1)}, bf16[392,256]{1,0:T(8,128)(2,1)S(1)}, u32[]{:S(2)}, u32[]{:S(2)}) collective-permute-start(bf16[392,256]{1,0:T(8,128)(2,1)S(1)} %fusion.14), channel_id=1, source_target_pairs={{48,0},{49,1},{50,2},{51,3},{52,4},{53,5},{54,6},{55,7},{56,8},{57... | collective-permute-start | bytes 602120 | tf_op jit(solution)/shard_map/ppermute | solution.py:30
  42.8 5.7 %collective-permute-start.8 = (bf16[264,256]{1,0:T(8,128)(2,1)S(1)}, bf16[264,256]{1,0:T(8,128)(2,1)S(1)}, u32[]{:S(2)}, u32[]{:S(2)}) collective-permute-start(bf16[264,256]{1,0:T(8,128)(2,1)S(1)} %concatenate.61), channel_id=1, source_target_pairs={{128,0},{192,64},{0,128},{64,192},{129,1},{193,65},{1,129},{65,193... | collective-permute-start | bytes 405512 | tf_op jit(solution)/shard_map/ppermute | solution.py:34
  44.1 7.9 %collective-permute-start.9 = (bf16[264,256]{1,0:T(8,128)(2,1)S(1)}, bf16[264,256]{1,0:T(8,128)(2,1)S(1)}, u32[]{:S(2)}, u32[]{:S(2)}) collective-permute-start(bf16[264,256]{1,0:T(8,128)(2,1)S(1)} %concatenate.61), channel_id=1, source_target_pairs={{192,0},{0,64},{64,128},{128,192},{193,1},{1,65},{65,129},{129,193... | collective-permute-start | bytes 405512 | tf_op jit(solution)/shard_map/ppermute | solution.py:34
  53.8 23.4 %copy-start.8 = (bf16[1024,256]{1,0:T(8,128)(2,1)}, bf16[1024,256]{1,0:T(8,128)(2,1)S(1)}, u32[]{:S(2)}) copy-start(bf16[1024,256]{1,0:T(8,128)(2,1)S(1)} %pad_maximum_fusion.1.p0) | copy-start | bytes 1572868
  53.8 18.8 %copy-start.14 = (bf16[2048]{0:T(1024)(128)(2,1)S(1)}, bf16[2048]{0:T(1024)(128)(2,1)}, u32[]{:S(2)}) copy-start(bf16[2048]{0:T(1024)(128)(2,1)} %param.13) | copy-start | bytes 12292
  53.8 12.6 %collective-permute-start.10 = (bf16[1024,256]{1,0:T(8,128)(2,1)S(1)}, bf16[1024,256]{1,0:T(8,128)(2,1)S(1)}, u32[]{:S(2)}, u32[]{:S(2)}) collective-permute-start(bf16[1024,256]{1,0:T(8,128)(2,1)S(1)} %pad_maximum_fusion.1.p0), channel_id=1, source_target_pairs={{64,0},{128,64},{192,128},{0,192},{65,1},{129,65},{193,129},{1,193... | collective-permute-start | bytes 1572872 | tf_op jit(solution)/shard_map/ppermute | solution.py:34
  53.9 24.4 %collective-permute-start.11 = (bf16[1024,256]{1,0:T(8,128)(2,1)S(1)}, bf16[1024,256]{1,0:T(8,128)(2,1)}, u32[]{:S(2)}, u32[]{:S(2)}) collective-permute-start(bf16[1024,256]{1,0:T(8,128)(2,1)S(1)} %pad_maximum_fusion.1.p0), channel_id=1, source_target_pairs={{128,0},{192,64},{0,128},{64,192},{129,1},{193,65},{1,129},{65,193... | collective-permute-start | bytes 1572872 | tf_op jit(solution)/shard_map/ppermute | solution.py:34
  55.1 24.8 %collective-permute-start.12 = (bf16[1024,256]{1,0:T(8,128)(2,1)S(1)}, bf16[1024,256]{1,0:T(8,128)(2,1)}, u32[]{:S(2)}, u32[]{:S(2)}) collective-permute-start(bf16[1024,256]{1,0:T(8,128)(2,1)S(1)} %pad_maximum_fusion.1.p0), channel_id=1, source_target_pairs={{192,0},{0,64},{64,128},{128,192},{193,1},{1,65},{65,129},{129,193... | collective-permute-start | bytes 1572872 | tf_op jit(solution)/shard_map/ppermute | solution.py:34
  57.0 21.3 %copy-start.9 = (bf16[1024,256]{1,0:T(8,128)(2,1)}, bf16[1024,256]{1,0:T(8,128)(2,1)S(1)}, u32[]{:S(2)}) copy-start(bf16[1024,256]{1,0:T(8,128)(2,1)S(1)} %pad_maximum_fusion.2.q0) | copy-start | bytes 1572868
  57.0 23.0 %collective-permute-start.13 = (bf16[1024,256]{1,0:T(8,128)(2,1)S(1)}, bf16[1024,256]{1,0:T(8,128)(2,1)S(1)}, u32[]{:S(2)}, u32[]{:S(2)}) collective-permute-start(bf16[1024,256]{1,0:T(8,128)(2,1)S(1)} %pad_maximum_fusion.2.q0), channel_id=1, source_target_pairs={{16,0},{17,1},{18,2},{19,3},{20,4},{21,5},{22,6},{23,7},{24,8},{25... | collective-permute-start | bytes 1572872 | tf_op jit(solution)/shard_map/ppermute | solution.py:30
  58.5 25.0 %collective-permute-start.14 = (bf16[1024,256]{1,0:T(8,128)(2,1)S(1)}, bf16[1024,256]{1,0:T(8,128)(2,1)}, u32[]{:S(2)}, u32[]{:S(2)}) collective-permute-start(bf16[1024,256]{1,0:T(8,128)(2,1)S(1)} %pad_maximum_fusion.2.q0), channel_id=1, source_target_pairs={{32,0},{33,1},{34,2},{35,3},{36,4},{37,5},{38,6},{39,7},{40,8},{41... | collective-permute-start | bytes 1572872 | tf_op jit(solution)/shard_map/ppermute | solution.py:30
  66.4 5.2 %copy-start.15 = (bf16[1024,256]{1,0:T(8,128)(2,1)}, bf16[1024,256]{1,0:T(8,128)(2,1)S(1)}, u32[]{:S(2)}) copy-start(bf16[1024,256]{1,0:T(8,128)(2,1)S(1)} %collective-permute-done.10.p1) | copy-start | bytes 1572868
  66.4 17.2 %collective-permute-start.15 = (bf16[1024,256]{1,0:T(8,128)(2,1)S(1)}, bf16[1024,256]{1,0:T(8,128)(2,1)S(1)}, u32[]{:S(2)}, u32[]{:S(2)}) collective-permute-start(bf16[1024,256]{1,0:T(8,128)(2,1)S(1)} %pad_maximum_fusion.2.q0), channel_id=1, source_target_pairs={{48,0},{49,1},{50,2},{51,3},{52,4},{53,5},{54,6},{55,7},{56,8},{57... | collective-permute-start | bytes 1572872 | tf_op jit(solution)/shard_map/ppermute | solution.py:30
  78.3 43.4 %copy-start.2 = (bf16[256,1024]{1,0:T(8,128)(2,1)}, bf16[256,1024]{1,0:T(8,128)(2,1)S(1)}, u32[]{:S(2)}) copy-start(bf16[256,1024]{1,0:T(8,128)(2,1)S(1)} %constant_dynamic-slice_fusion.10.refs_0_) | copy-start | bytes 1572868
  79.9 7.4 %copy-start.16 = (bf16[1024,256]{1,0:T(8,128)(2,1)}, bf16[1024,256]{1,0:T(8,128)(2,1)S(1)}, u32[]{:S(2)}) copy-start(bf16[1024,256]{1,0:T(8,128)(2,1)S(1)} %collective-permute-done.13.q1) | copy-start | bytes 1572868
  83.6 3.8 %copy-start.17 = (bf16[1024,256]{1,0:T(8,128)(2,1)}, bf16[1024,256]{1,0:T(8,128)(2,1)S(1)}, u32[]{:S(2)}) copy-start(bf16[1024,256]{1,0:T(8,128)(2,1)S(1)} %collective-permute-done.15.q3) | copy-start | bytes 1572868
  83.6 23.6 %collective-permute-start.18 = (bf16[256,1024]{1,0:T(8,128)(2,1)S(1)}, bf16[256,1024]{1,0:T(8,128)(2,1)S(1)}, u32[]{:S(2)}, u32[]{:S(2)}) collective-permute-start(bf16[256,1024]{1,0:T(8,128)(2,1)S(1)} %constant_dynamic-slice_fusion.10.refs_0_), channel_id=1, source_target_pairs={{16,0},{17,1},{18,2},{19,3},{20,4},{21,5},{22,6},{23,7},{24,8},{25... | collective-permute-start | bytes 1572872 | tf_op jit(solution)/shard_map/ppermute | solution.py:30
  84.8 24.1 %collective-permute-start.19 = (bf16[256,1024]{1,0:T(8,128)(2,1)S(1)}, bf16[256,1024]{1,0:T(8,128)(2,1)S(1)}, u32[]{:S(2)}, u32[]{:S(2)}) collective-permute-start(bf16[256,1024]{1,0:T(8,128)(2,1)S(1)} %constant_dynamic-slice_fusion.10.refs_0_), channel_id=1, source_target_pairs={{32,0},{33,1},{34,2},{35,3},{36,4},{37,5},{38,6},{39,7},{40,8},{41... | collective-permute-start | bytes 1572872 | tf_op jit(solution)/shard_map/ppermute | solution.py:30
  95.1 16.3 %collective-permute-start.17 = (bf16[2,512,256]{2,1,0:T(8,128)(2,1)}, bf16[2,512,256]{2,1,0:T(8,128)(2,1)S(1)}, u32[]{:S(2)}, u32[]{:S(2)}) collective-permute-start(bf16[2,512,256]{2,1,0:T(8,128)(2,1)} %get-tuple-element.108.ko_ref.vo_ref), channel_id=1, source_target_pairs={{0,2},{1,3},{2,4},{3,5},{4,6},{5,7},{6,8},{7,9},{8,10},{9,11},{10,... | collective-permute-start | bytes 1572872 | tf_op jit(solution)/shard_map/ppermute | solution.py:40
  97.7 24.0 %collective-permute-start.16 = (bf16[256,1024]{1,0:T(8,128)(2,1)S(1)}, bf16[256,1024]{1,0:T(8,128)(2,1)}, u32[]{:S(2)}, u32[]{:S(2)}) collective-permute-start(bf16[256,1024]{1,0:T(8,128)(2,1)S(1)} %constant_dynamic-slice_fusion.10.refs_0_), channel_id=1, source_target_pairs={{48,0},{49,1},{50,2},{51,3},{52,4},{53,5},{54,6},{55,7},{56,8},{57... | collective-permute-start | bytes 1572872 | tf_op jit(solution)/shard_map/ppermute | solution.py:30
  98.3 10.6 %copy-start = (bf16[2,512,256]{2,1,0:T(8,128)(2,1)S(1)}, bf16[2,512,256]{2,1,0:T(8,128)(2,1)}, u32[]{:S(2)}) copy-start(bf16[2,512,256]{2,1,0:T(8,128)(2,1)} %get-tuple-element.108.ko_ref.vo_ref) | copy-start | bytes 1572868
  107.1 17.6 %copy-start.1 = (bf16[2,512,256]{2,1,0:T(8,128)(2,1)S(1)}, bf16[2,512,256]{2,1,0:T(8,128)(2,1)}, u32[]{:S(2)}) copy-start(bf16[2,512,256]{2,1,0:T(8,128)(2,1)} %get-tuple-element.108.ko_ref.vo_ref) | copy-start | bytes 1572868
  107.1 21.0 %copy-start.5 = (bf16[256,1024]{1,0:T(8,128)(2,1)}, bf16[256,1024]{1,0:T(8,128)(2,1)S(1)}, u32[]{:S(2)}) copy-start(bf16[256,1024]{1,0:T(8,128)(2,1)S(1)} %collective-permute-done.18.refs_1_) | copy-start | bytes 1572868
  108.9 19.2 %copy-start.6 = (bf16[256,1024]{1,0:T(8,128)(2,1)}, bf16[256,1024]{1,0:T(8,128)(2,1)S(1)}, u32[]{:S(2)}) copy-start(bf16[256,1024]{1,0:T(8,128)(2,1)S(1)} %collective-permute-done.19.refs_2_) | copy-start | bytes 1572868
  108.9 15.3 %collective-permute-start.25 = (bf16[2,512,256]{2,1,0:T(8,128)(2,1)S(1)}, bf16[2,512,256]{2,1,0:T(8,128)(2,1)}, u32[]{:S(2)}, u32[]{:S(2)}) collective-permute-start(bf16[2,512,256]{2,1,0:T(8,128)(2,1)S(1)} %copy-done), channel_id=1, source_target_pairs={{1,0},{0,1},{3,2},{2,3},{5,4},{4,5},{7,6},{6,7},{9,8},{8,9},{11,10... | collective-permute-start | bytes 1572872 | tf_op jit(solution)/shard_map/ppermute | solution.py:30
  111.4 0.8 copy-start.3
  121.7 5.5 %collective-permute-start.21 = (bf16[256,1024]{1,0:T(8,128)(2,1)S(1)}, bf16[256,1024]{1,0:T(8,128)(2,1)S(1)}, u32[]{:S(2)}, u32[]{:S(2)}) collective-permute-start(bf16[256,1024]{1,0:T(8,128)(2,1)S(1)} %constant_dynamic-slice_fusion.10.refs_0_), channel_id=1, source_target_pairs={{1,0},{0,1},{3,2},{2,3},{5,4},{4,5},{7,6},{6,7},{9,8},{8,9},{11,10... | collective-permute-start | bytes 1572872 | tf_op jit(solution)/shard_map/ppermute | solution.py:30
  123.7 3.6 %collective-permute-start.22 = (bf16[256,1024]{1,0:T(8,128)(2,1)S(1)}, bf16[256,1024]{1,0:T(8,128)(2,1)}, u32[]{:S(2)}, u32[]{:S(2)}) collective-permute-start(bf16[256,1024]{1,0:T(8,128)(2,1)S(1)} %collective-permute-done.18.refs_1_), channel_id=1, source_target_pairs={{1,0},{0,1},{3,2},{2,3},{5,4},{4,5},{7,6},{6,7},{9,8},{8,9},{11,10... | collective-permute-start | bytes 1572872 | tf_op jit(solution)/shard_map/ppermute | solution.py:30
  123.7 4.3 %collective-permute-start.23 = (bf16[256,1024]{1,0:T(8,128)(2,1)S(1)}, bf16[256,1024]{1,0:T(8,128)(2,1)}, u32[]{:S(2)}, u32[]{:S(2)}) collective-permute-start(bf16[256,1024]{1,0:T(8,128)(2,1)S(1)} %collective-permute-done.19.refs_2_), channel_id=1, source_target_pairs={{1,0},{0,1},{3,2},{2,3},{5,4},{4,5},{7,6},{6,7},{9,8},{8,9},{11,10... | collective-permute-start | bytes 1572872 | tf_op jit(solution)/shard_map/ppermute | solution.py:30
  124.2 4.0 %collective-permute-start.24 = (bf16[256,1024]{1,0:T(8,128)(2,1)}, bf16[256,1024]{1,0:T(8,128)(2,1)}, u32[]{:S(2)}, u32[]{:S(2)}) collective-permute-start(bf16[256,1024]{1,0:T(8,128)(2,1)} %collective-permute-done.16.refs_3_), channel_id=1, source_target_pairs={{1,0},{0,1},{3,2},{2,3},{5,4},{4,5},{7,6},{6,7},{9,8},{8,9},{11,10... | collective-permute-start | bytes 1572872 | tf_op jit(solution)/shard_map/ppermute | solution.py:30
  124.2 3.1 %collective-permute-start.20 = (bf16[256,512]{1,0:T(8,128)(2,1)}, bf16[256,512]{1,0:T(8,128)(2,1)S(1)}, u32[]{:S(2)}, u32[]{:S(2)}) collective-permute-start(bf16[256,512]{1,0:T(8,128)(2,1)} %get-tuple-element.103), channel_id=1, source_target_pairs={{1,0},{0,1},{3,2},{2,3},{5,4},{4,5},{7,6},{6,7},{9,8},{8,9},{11,10... | collective-permute-start | bytes 786440 | tf_op jit(solution)/shard_map/ppermute | solution.py:30
  127.2 0.9 copy-start.10
  127.2 0.9 copy-start.7
Sparse Core Ops, SparseCore 0:
  10.9 42.0 all-gather.3
  54.9 40.7 all-gather.5
